TPU v7x, 32 devices: a whole 2x2x4 slice. The times are simulated.
32 devices in a mesh: fsdp: 16 (over z, x, core), dp: 2 (over y).
Axes of the slice: x: 2, y: 2, z: 4, core: 2. Of those that a mesh axis runs over, the one named last changes fastest.
Arguments:
- tokens: bfloat16 [32768, 768], P(('fsdp', 'dp')), may hold values from -6 to 6
- segment_ids: int32 [32, 1024], P(('fsdp', 'dp')), may hold values from -1 to 15, as said below
- projection: float32 [12, 32, 64], replicated, may hold values from -0.75 to 0.75
- norm1_gain: bfloat16 [768], P('fsdp'), may hold values from 0.5 to 1.5
- norm1_bias: bfloat16 [768], P('fsdp'), may hold values from -1.1953125 to 1.1953125
- qkv_weight: bfloat16 [768, 2304], P('fsdp'), may hold values from -0.21875 to 0.21875
- qkv_bias: bfloat16 [2304], P('fsdp'), may hold values from -1.1953125 to 1.1953125
- out_weight: bfloat16 [768, 768], P('fsdp'), may hold values from -1.5 to 1.5
- out_bias: bfloat16 [768], P('fsdp'), may hold values from -1.1953125 to 1.1953125
- norm2_gain: bfloat16 [768], P('fsdp'), may hold values from 0.5 to 1.5
- norm2_bias: bfloat16 [768], P('fsdp'), may hold values from -1.1953125 to 1.1953125
- in_weight: bfloat16 [768, 3072], P('fsdp'), may hold values from -0.21875 to 0.21875
- in_bias: bfloat16 [3072], P('fsdp'), may hold values from -1.1953125 to 1.1953125
- ffn_out_weight: bfloat16 [3072, 768], P('fsdp'), may hold values from -0.109375 to 0.109375
- ffn_out_bias: bfloat16 [768], P('fsdp'), may hold values from -1.1953125 to 1.1953125
- cotangent: bfloat16 [32768, 768], P(('fsdp', 'dp')), may hold values from -6 to 6
Outputs:
- output: bfloat16 [32768, 768], P(('fsdp', 'dp'))
- tokens_grad: bfloat16 [32768, 768], P(('fsdp', 'dp'))
- norm1_gain_grad: float32 [768], P('fsdp')
- norm1_bias_grad: float32 [768], P('fsdp')
- qkv_weight_grad: float32 [768, 2304], P('fsdp')
- query_key_bias_grad: float32 [1536], P('fsdp')
- value_bias_grad: float32 [768], P('fsdp')
- out_weight_grad: float32 [768, 768], P('fsdp')
- out_bias_grad: float32 [768], P('fsdp')
- norm2_gain_grad: float32 [768], P('fsdp')
- norm2_bias_grad: float32 [768], P('fsdp')
- in_weight_grad: float32 [768, 3072], P('fsdp')
- in_bias_grad: float32 [3072], P('fsdp')
- ffn_out_weight_grad: float32 [3072, 768], P('fsdp')
- ffn_out_bias_grad: float32 [768], P('fsdp')
Inputs may be any that keep to these rules, and one draw needn't show every extreme that they name: `segment_ids`: in each sequence the ids never fall until the padding; the last 1 to 256 rows of every sequence are -1 and no others; every sequence reaches id 16 - 1; some segments may have no rows.
All inputs are finite; a program needn't handle non-finite values.
Results may differ from a plain program's by a relative error of at most 0.01.
Values may be sent and summed in bfloat16 or wider, within the bound.
A program may use at most 192 MiB of HBM per device.

v0:
```python
import jax
import jax.numpy as jnp
from jax import lax
from jax.sharding import PartitionSpec as P

HEADS = 12
HEAD_DIM = 64
SEGS = 16


highest = lax.Precision.HIGHEST
epsilon = 1e-05


def norm_forward(rows, gain, shift):
    row_mean = jnp.mean(rows, axis=-1, keepdims=True)
    centred = rows - row_mean
    inv_std = lax.rsqrt(jnp.mean(centred * centred, axis=-1, keepdims=True) + epsilon)
    normed = centred * inv_std
    return (normed * gain + shift, normed, inv_std)


def norm_backward(incoming, normed, inv_std, gain):
    scaled = incoming * gain
    mean_one = jnp.mean(scaled, axis=-1, keepdims=True)
    mean_two = jnp.mean(scaled * normed, axis=-1, keepdims=True)
    input_grad = inv_std * (scaled - mean_one - normed * mean_two)
    return (input_grad, jnp.sum(incoming * normed, axis=0), jnp.sum(incoming, axis=0))


def rotary_tables(length, half_width):
    positions = jnp.arange(length, dtype=jnp.float32)
    frequency = 10000.0 ** (-jnp.arange(half_width, dtype=jnp.float32) / half_width)
    angles = positions[:, None] * frequency[None, :]
    return (jnp.cos(angles)[:, None, :], jnp.sin(angles)[:, None, :])


def rotate(values, cosine, sine):
    half_width = values.shape[-1] // 2
    lower_half = values[..., :half_width]
    upper_half = values[..., half_width:]
    return jnp.concatenate(
        [lower_half * cosine - upper_half * sine, lower_half * sine + upper_half * cosine], axis=-1
    )


def segment_core(query_rows, key_rows, value_rows, segment, projection):
    length = query_rows.shape[0]
    cosine, sine = rotary_tables(length, query_rows.shape[-1] // 2)
    feat_query = jax.nn.softplus(
        jnp.einsum("nhd,hfd->nhf", rotate(query_rows, cosine, sine), projection, precision=highest)
    )
    feat_key = jax.nn.softplus(
        jnp.einsum("nhd,hfd->nhf", rotate(key_rows, cosine, sine), projection, precision=highest)
    )
    member = (segment[:, None] == jnp.arange(SEGS, dtype=jnp.int32)[None, :]).astype(jnp.float32)
    present = jnp.sum(member, axis=-1)
    masked_keys = member[:, :, None, None] * feat_key[:, None]
    kv_state = jnp.einsum("nshf,nhd->shfd", masked_keys, value_rows, precision=highest)
    totals = jnp.sum(masked_keys, axis=0)
    masked_queries = member[:, :, None, None] * feat_query[:, None]
    numerator = jnp.einsum("nshf,shfd->nhd", masked_queries, kv_state, precision=highest)
    denominator = (
        jnp.einsum("nshf,shf->nh", masked_queries, totals, precision=highest)
        + (1.0 - present)[:, None]
    )
    return numerator / denominator[:, :, None]


def attend(projected, segment_ids, projection):
    seq_count, length = segment_ids.shape
    shaped = projected.reshape(seq_count, length, 3, HEADS, HEAD_DIM)

    def one_sequence(pieces):
        rows, segment = pieces
        return segment_core(rows[:, 0], rows[:, 1], rows[:, 2], segment, projection)

    return lax.map(one_sequence, (shaped, segment_ids)).reshape(
        seq_count * length, HEADS * HEAD_DIM
    )


def attend_back(projected, segment_ids, projection, grad_attended):
    seq_count, length = segment_ids.shape
    shaped = projected.reshape(seq_count, length, 3, HEADS, HEAD_DIM)
    upstream_rows = grad_attended.reshape(seq_count, length, HEADS, HEAD_DIM)

    def one_sequence(pieces):
        rows, segment, upstream = pieces

        def local_core(query_rows, key_rows, value_rows):
            return segment_core(query_rows, key_rows, value_rows, segment, projection)

        unused, pull = jax.vjp(local_core, rows[:, 0], rows[:, 1], rows[:, 2])
        grads = pull(upstream)
        return jnp.stack(grads, axis=1)

    result = lax.map(one_sequence, (shaped, segment_ids, upstream_rows))
    return result.reshape(seq_count * length, 3 * HEADS * HEAD_DIM)


def contract_rows(left, right):
    return lax.dot_general(
        left, right, (((0,), (0,)), ((), ())), preferred_element_type=jnp.float32
    )


def contract_cols(left, right):
    return lax.dot_general(
        left, right, (((1,), (1,)), ((), ())), preferred_element_type=jnp.float32
    )


def fetch_block(params):
    return (
        lax.all_gather(params[0], "fsdp", axis=0, tiled=True),
        lax.all_gather(params[1], "fsdp", axis=0, tiled=True),
        lax.all_gather(params[2], "fsdp", axis=0, tiled=True),
        lax.all_gather(params[3], "fsdp", axis=0, tiled=True),
        lax.all_gather(params[4], "fsdp", axis=0, tiled=True),
        lax.all_gather(params[5], "fsdp", axis=0, tiled=True),
    )


def backward_weights(params):
    return (
        lax.all_gather(params[0], "fsdp", axis=0, tiled=True),
        lax.all_gather(params[1], "fsdp", axis=0, tiled=True),
        lax.all_gather(params[2], "fsdp", axis=0, tiled=True),
        lax.all_gather(params[3], "fsdp", axis=0, tiled=True),
        lax.all_gather(params[4], "fsdp", axis=0, tiled=True),
        lax.all_gather(params[5], "fsdp", axis=0, tiled=True),
    )


def reduce_grads(grads):
    pieces = (
        lax.psum_scatter(grads[0], "fsdp", scatter_dimension=0, tiled=True),
        lax.psum_scatter(grads[1], "fsdp", scatter_dimension=0, tiled=True),
        lax.psum_scatter(grads[2], "fsdp", scatter_dimension=0, tiled=True),
        lax.psum_scatter(grads[3], "fsdp", scatter_dimension=0, tiled=True),
        lax.psum_scatter(grads[4], "fsdp", scatter_dimension=0, tiled=True),
        lax.psum_scatter(grads[5], "fsdp", scatter_dimension=0, tiled=True),
    )
    return (
        lax.psum(pieces[0].astype(jnp.bfloat16), "dp").astype(jnp.float32),
        lax.psum(pieces[1].astype(jnp.bfloat16), "dp").astype(jnp.float32),
        lax.psum(pieces[2].astype(jnp.bfloat16), "dp").astype(jnp.float32),
        lax.psum(pieces[3].astype(jnp.bfloat16), "dp").astype(jnp.float32),
        lax.psum(pieces[4].astype(jnp.bfloat16), "dp").astype(jnp.float32),
        lax.psum(pieces[5].astype(jnp.bfloat16), "dp").astype(jnp.float32),
    )


def body(
    tokens,
    segment_ids,
    projection,
    norm1_gain,
    norm1_bias,
    qkv_weight,
    qkv_bias,
    out_weight,
    out_bias,
    norm2_gain,
    norm2_bias,
    in_weight,
    in_bias,
    ffn_out_weight,
    ffn_out_bias,
    cotangent,
):
    attn_local = (norm1_gain, norm1_bias, qkv_weight, qkv_bias, out_weight, out_bias)
    ffn_local = (norm2_gain, norm2_bias, in_weight, in_bias, ffn_out_weight, ffn_out_bias)
    model_width = tokens.shape[1]
    groups = lax.axis_size("fsdp")
    attn_full = fetch_block(attn_local)
    gain_one, shift_one, weight_qkv, bias_qkv, weight_out, bias_out = attn_full
    residual = tokens.astype(jnp.float32)
    normed_out_one, normed_one, inv_one = norm_forward(
        residual, gain_one.astype(jnp.float32), shift_one.astype(jnp.float32)
    )
    hidden_one = normed_out_one.astype(jnp.bfloat16)
    projected = jnp.dot(
        hidden_one, weight_qkv, preferred_element_type=jnp.float32
    ) + bias_qkv.astype(jnp.float32)
    attended = attend(projected, segment_ids, projection).astype(jnp.bfloat16)
    branch_one = jnp.dot(
        attended, weight_out, preferred_element_type=jnp.float32
    ) + bias_out.astype(jnp.float32)
    middle = residual + branch_one
    ffn_full = fetch_block(ffn_local)
    gain_two, shift_two, weight_in, bias_in, weight_ffo, bias_ffo = ffn_full
    normed_out_two, normed_two, inv_two = norm_forward(
        middle, gain_two.astype(jnp.float32), shift_two.astype(jnp.float32)
    )
    hidden_two = normed_out_two.astype(jnp.bfloat16)
    pre_act = jnp.dot(hidden_two, weight_in, preferred_element_type=jnp.float32) + bias_in.astype(
        jnp.float32
    )
    activated = jax.nn.gelu(pre_act, approximate=False).astype(jnp.bfloat16)
    branch_two = jnp.dot(
        activated, weight_ffo, preferred_element_type=jnp.float32
    ) + bias_ffo.astype(jnp.float32)
    output = (middle + branch_two).astype(jnp.bfloat16)
    upstream = cotangent.astype(jnp.float32)
    ffn_back = backward_weights(ffn_local)
    back_gain_two, unused_shift_two, back_in, unused_bias_in, back_ffo, unused_bias_ffo = ffn_back
    grad_ffo_weight = contract_rows(activated, cotangent)
    grad_ffo_bias = jnp.sum(upstream, axis=0)
    grad_activated = contract_cols(cotangent, back_ffo)
    slope = (
        0.5 * (1.0 + lax.erf(pre_act * 0.7071067811865476))
        + pre_act * jnp.exp(-0.5 * pre_act * pre_act) * 0.3989422804014327
    )
    grad_pre = (grad_activated * slope).astype(jnp.bfloat16)
    grad_in_weight = contract_rows(hidden_two, grad_pre)
    grad_in_bias = jnp.sum(grad_pre.astype(jnp.float32), axis=0)
    grad_hidden_two = contract_cols(grad_pre, back_in)
    back_two, grad_gain_two, grad_shift_two = norm_backward(
        grad_hidden_two, normed_two, inv_two, back_gain_two.astype(jnp.float32)
    )
    grad_middle = upstream + back_two
    ffn_grads = reduce_grads(
        (
            grad_gain_two,
            grad_shift_two,
            grad_in_weight,
            grad_in_bias,
            grad_ffo_weight,
            grad_ffo_bias,
        )
    )
    attn_back = backward_weights(attn_local)
    back_gain_one, unused_shift_one, back_qkv, unused_bias_qkv, back_out, unused_bias_out = (
        attn_back
    )
    grad_branch = grad_middle.astype(jnp.bfloat16)
    grad_out_weight = contract_rows(attended, grad_branch)
    grad_out_bias = jnp.sum(grad_branch.astype(jnp.float32), axis=0)
    grad_attended = contract_cols(grad_branch, back_out)
    grad_projected = attend_back(projected, segment_ids, projection, grad_attended).astype(
        jnp.bfloat16
    )
    grad_qkv_weight = contract_rows(hidden_one, grad_projected)
    grad_qkv_bias = jnp.sum(grad_projected.astype(jnp.float32), axis=0)
    bias_packed = jnp.concatenate(
        [
            grad_qkv_bias[: 2 * model_width].reshape(groups, -1),
            grad_qkv_bias[2 * model_width :].reshape(groups, -1),
        ],
        axis=1,
    ).reshape(-1)
    grad_hidden_one = contract_cols(grad_projected, back_qkv)
    back_one, grad_gain_one, grad_shift_one = norm_backward(
        grad_hidden_one, normed_one, inv_one, back_gain_one.astype(jnp.float32)
    )
    tokens_grad = (grad_middle + back_one).astype(jnp.bfloat16)
    attn_grads = reduce_grads(
        (
            grad_gain_one,
            grad_shift_one,
            grad_qkv_weight,
            bias_packed,
            grad_out_weight,
            grad_out_bias,
        )
    )
    owned_bias = attn_grads[3]
    split_point = 2 * model_width // groups
    return (
        output,
        tokens_grad,
        attn_grads[0],
        attn_grads[1],
        attn_grads[2],
        owned_bias[:split_point],
        owned_bias[split_point:],
        attn_grads[4],
        attn_grads[5],
        ffn_grads[0],
        ffn_grads[1],
        ffn_grads[2],
        ffn_grads[3],
        ffn_grads[4],
        ffn_grads[5],
    )


def solution(mesh):
    in_specs = (
        P(("fsdp", "dp"), None),
        P(("fsdp", "dp"), None),
        P(),
        P("fsdp"),
        P("fsdp"),
        P("fsdp", None),
        P("fsdp"),
        P("fsdp", None),
        P("fsdp"),
        P("fsdp"),
        P("fsdp"),
        P("fsdp", None),
        P("fsdp"),
        P("fsdp", None),
        P("fsdp"),
        P(("fsdp", "dp"), None),
    )
    out_specs = (
        P(("fsdp", "dp"), None),
        P(("fsdp", "dp"), None),
        P("fsdp"),
        P("fsdp"),
        P("fsdp", None),
        P("fsdp"),
        P("fsdp"),
        P("fsdp", None),
        P("fsdp"),
        P("fsdp"),
        P("fsdp"),
        P("fsdp", None),
        P("fsdp"),
        P("fsdp", None),
        P("fsdp"),
    )
    return jax.shard_map(body, mesh=mesh, in_specs=in_specs, out_specs=out_specs, check_vma=False)
```

profile of v0, /device:TPU:0, one launch (start us, length us, event | category | flops | bytes accessed | tf_op | source)
XLA Modules:
  0.0 792.6 jit_solution(11601006534894251956)
XLA Ops:
  22.0 63.5 %all-reduce.21 = (bf16[2304]{0:T(1024)(128)(2,1)S(1)}, bf16[768]{0:T(1024)(128)(2,1)S(1)}, bf16[768]{0:T(1024)(128)(2,1)S(1)}, bf16[768]{0:T(1024)(128)(2,1)}, b...) all-reduce(bf16[2304]{0:T(1024)(128)(2,1)S(1)} %dynamic-update-slic, ...), channel_id=1, replica_groups=mesh['fsdp'=16,'dp'=2] {'fsdp'}, use_global_device_ids=true, to_apply=%add.6 | all-reduce | flops 9984 | bytes 39936
  94.6 8.6 %convolution_add_fusion = f32[1024,2304]{1,0:T(8,128)} fusion(bf16[768,2304]{1,0:T(8,128)(2,1)} %all-gather.5.cloned.1.call-done, f32[2304]{0:T(1024)} %convert_element_type.162, bf16[1024,768]{0,1:T(8,128)(2,1)S(1)} %copy.55, f32[768]{0:T(1024)} %convert_element_type.160, f32[768]{0:T(1024)S(1)} %convert_element_type.159, f32[1024]{0:T(1024)S(1)} %add_rsqrt_fusion.1, ...), kind=kOutput, calls=%fused_computation.58 | convolution fusion | flops 3630956544 | bytes 14572544 | tf_op jit(solution)/shard_map/dot_general | solution.py:184
  103.3 9.7 %copy.56 = f32[1024,2304]{0,1:T(8,128)} copy(f32[1024,2304]{1,0:T(8,128)} %convolution_add_fusion) | data formatting | bytes 18874368 | tf_op jit(solution)/shard_map/add | solution.py:184
  113.0 3.8 slice_bitcast_fusion.1
  118.4 3.7 compare_select_fusion.5
  122.1 21.6 %fusion.10 = f32[12,64,16,32]{1,3,2,0:T(8,128)S(1)} fusion(f32[1024,12,32]{0,2,1:T(8,128)S(1)} %get-tuple-element.162, f32[1024,16]{0,1:T(8,128)S(1)} %fusion.102, f32[1024,3,12,64]{0,3,2,1:T(8,128)S(1)} %bitcast.184), kind=kOutput, calls=%fused_computation.11 | convolution fusion | flops 4838129664 | bytes 6356992 | tf_op jit(solution)/shard_map/while/body/eval_jaxpr/nshf,nhd->shfd/dot_general | solution.py:59
  145.6 3.7 compare_select_fusion.4
  149.3 16.0 %fusion.4 = f32[12,1,1024,1]{2,1,3,0:T(1,128)S(1)} fusion(f32[16,12,32,1]{2,3,0,1:T(1,128)S(1)} %bitcast.190, f32[1024,12,32]{0,2,1:T(8,128)S(1)} %get-tuple-element.160, f32[1024,16]{0,1:T(8,128)S(1)} %fusion.102), kind=kOutput, calls=%fused_computation.4 | convolution fusion | flops 81788928 | bytes 1712128 | tf_op jit(solution)/shard_map/while/body/eval_jaxpr/nshf,shf->nh/dot_general | solution.py:64
  166.0 18.3 %fusion.65 = (bf16[1024,12,64]{0,2,1:T(8,128)(2,1)}, f32[12,64,1024,1]{2,1,3,0:T(8,128)}) fusion(f32[1024,12]{0,1:T(8,128)S(1)} %fusion.101, f32[1024,12,32]{0,2,1:T(8,128)S(1)} %get-tuple-element.160, f32[1024,16]{0,1:T(8,128)S(1)} %fusion.102, f32[12,64,16,32]{1,3,2,0:T(8,128)S(1)} %fusion.10), kind=kOutput, calls=%fused_computation.98 | convolution fusion | flops 4839702528 | bytes 7979008 | tf_op jit(solution)/shard_map/while/body/eval_jaxpr/nshf,shfd->nhd/dot_general | solution.py:62
  189.9 38.9 %fusion.16 = (bf16[1024,3072]{1,0:T(8,128)(2,1)}, f32[1024,3072]{1,0:T(8,128)}) fusion(f32[3072]{0:T(1024)S(1)} %copy-done.34, bf16[768,3072]{1,0:T(8,128)(2,1)} %all-gather.9.cloned.1.call-done, f32[1024,768]{0,1:T(8,128)} %copy-done.3, f32[768]{0:T(1024)S(1)} %copy-done.37, f32[768]{0:T(1024)S(1)} %convert_element_type.167, f32[1024]{0:T(1024)S(1)} %add_rsqrt_fusion, ...), kind=kOutput, calls=%fused_computation.21 | convolution fusion | flops 5043388416 | bytes 26765312 | tf_op jit(solution)/shard_map/dot_general | solution.py:198
  228.8 11.9 %convert_reduce_fusion = (f32[3072]{0:T(1024)S(1)}, bf16[1024,3072]{1,0:T(8,128)(2,1)S(1)}) fusion(f32[1024,3072]{1,0:T(8,128)} %get-tuple-element.169, f32[3072]{0:T(1024)S(1)} %copy-done.34, bf16[1024,768]{1,0:T(8,128)(2,1)S(1)} %copy-done.12, bf16[3072,768]{1,0:T(8,128)(2,1)} %all-gather.11.cloned.1.call-done), kind=kOutput, calls=%fused_computation.28 | convolution fusion | flops 4872729600 | bytes 25190400 | tf_op jit(solution)/shard_map/dot_general | solution.py:109
  240.8 6.8 fusion.123
  247.5 3.7 copy.59
  264.5 21.4 %fusion.2 = f32[12,64,16,32]{1,3,2,0:T(8,128)S(1)} fusion(f32[1024,12,32]{0,2,1:T(8,128)S(1)} %copy-done.18, f32[1024,16]{0,1:T(8,128)S(1)} %fusion.102, f32[1024,12,64]{0,2,1:T(8,128)S(1)} %bitcast.187, f32[1024,12]{0,1:T(8,128)S(1)} %copy-done.28), kind=kOutput, calls=%fused_computation.2 | convolution fusion | flops 4838916096 | bytes 6406144 | tf_op jit(solution)/shard_map/while/body/eval_jaxpr/transpose(jvp(nshf,shfd->nhd))/dot_general | solution.py:62
  286.8 49.4 %fusion = f32[12,1,16,32]{3,1,2,0:T(1,128)S(1)} fusion(f32[1024,12,32]{0,2,1:T(8,128)S(1)} %copy-done.18, f32[1024,16]{0,1:T(8,128)S(1)} %fusion.102, f32[12,1024,1,1]{1,0,2,3:T(8,128)S(1)} %get-tuple-element.155), kind=kOutput, calls=%fused_computation | convolution fusion | flops 81788928 | bytes 1712128 | tf_op jit(solution)/shard_map/while/body/eval_jaxpr/transpose(jvp(nshf,shf->nh))/dot_general | solution.py:64
  336.2 22.6 %multiply_reduce_fusion.1 = f32[12,1024,32]{1,2,0:T(8,128)S(1)} fusion(f32[12,16,32]{2,1,0:T(8,128)S(1)} %bitcast.191, f32[12,1024]{1,0:T(8,128)S(1)} %get-tuple-element.154, f32[1024,16]{0,1:T(8,128)S(1)} %fusion.102, f32[12,64,16,32]{1,3,2,0:T(8,128)S(1)} %copy-done.49, f32[1024,12,64]{0,2,1:T(8,128)S(1)} %bitcast.189, f32[1024,12]{0,1:T(8,128)S(1)} %copy-done.28), kind=kOutput, calls=%fused_computation.16 | convolution fusion | flops 4857397248 | bytes 6479872 | tf_op jit(solution)/shard_map/while/body/eval_jaxpr/transpose(jvp(nshf,shfd->nhd))/dot_general | solution.py:62
  358.8 22.8 %fusion.13 = f32[1024,12,32]{0,2,1:T(8,128)S(1)} fusion(f32[16,12,32]{2,0,1:T(8,128)S(1)} %bitcast.196, f32[1024,16]{0,1:T(8,128)S(1)} %fusion.102, f32[12,64,16,32]{1,3,2,0:T(8,128)S(1)} %fusion.2, f32[1024,3,12,64]{0,3,2,1:T(8,128)} %bitcast.181), kind=kOutput, calls=%fused_computation.15 | convolution fusion | flops 4850319360 | bytes 6381568 | tf_op jit(solution)/shard_map/while/body/eval_jaxpr/transpose(jvp(nshf,nhd->shfd))/dot_general | solution.py:59
  381.6 4.0 convolution_bitcast_fusion
  385.6 4.0 convolution_bitcast_fusion.1
  392.8 17.0 %fusion.71 = bf16[1024,1,12,64]{0,3,2,1:T(8,128)(2,1)S(1)} fusion(f32[12,64,16,32]{1,3,2,0:T(8,128)S(1)} %fusion.2, f32[1024,12,32]{0,2,1:T(8,128)S(1)} %copy-done.8, f32[1024,16]{0,1:T(8,128)S(1)} %fusion.102), kind=kOutput, calls=%fused_computation.115 | convolution fusion | flops 4838129664 | bytes 4784128 | tf_op jit(solution)/shard_map/while/body/eval_jaxpr/transpose(jvp(nshf,nhd->shfd))/dot_general | solution.py:59
  412.9 6.3 fusion.115
  419.3 10.7 %fusion.118 = f32[768,3072]{1,0:T(8,128)} fusion(bf16[1024,3072]{1,0:T(8,128)(2,1)} %copy-done.47, f32[1024,768]{0,1:T(8,128)} %copy-done.3, f32[768]{0:T(1024)S(1)} %copy-done.37, f32[768]{0:T(1024)S(1)} %convert_element_type.167, f32[1024]{0:T(1024)S(1)} %add_rsqrt_fusion, f32[1024]{0:T(1024)S(1)} %broadcast_multiply_fusion.4), kind=kOutput, calls=%fused_computation.196 | convolution fusion | flops 4835770368 | bytes 18888704 | tf_op jit(solution)/shard_map/dot_general | solution.py:103
  431.5 10.9 %fusion.124 = f32[3072,768]{1,0:T(8,128)} fusion(bf16[1024,3072]{1,0:T(8,128)(2,1)} %get-tuple-element.168, bf16[1024,768]{1,0:T(8,128)(2,1)S(1)} %copy-done.13), kind=kOutput, calls=%fused_computation.202 | convolution fusion | flops 4831838208 | bytes 17301504 | tf_op jit(solution)/shard_map/dot_general | solution.py:103
  444.8 9.8 %fusion.122 = (f32[768]{0:T(1024)S(1)}, f32[1024,768]{1,0:T(8,128)}) fusion(bf16[1024,2304]{0,1:T(8,128)(2,1)} %bitcast.186, bf16[768,2304]{1,0:T(8,128)(2,1)} %all-gather.5.cloned.1.call-done), kind=kOutput, calls=%fused_computation.200 | convolution fusion | flops 3624664320 | bytes 11406336 | tf_op jit(solution)/shard_map/dot_general | solution.py:109
  454.6 3.5 copy.60
  461.0 59.4 %all-reduce.20 = (bf16[2304]{0:T(1024)(128)(2,1)S(1)}, bf16[768]{0:T(1024)(128)(2,1)S(1)}, bf16[768]{0:T(1024)(128)(2,1)S(1)}, bf16[768]{0:T(1024)(128)(2,1)S(1)...) all-reduce(f32[2304]{0:T(1024)S(1)} %reshape.194, ...), channel_id=5, replica_groups=mesh['fsdp'=16,'dp'=2] {'fsdp'}, use_global_device_ids=true, to_apply=%region_23.25.clone | all-reduce | flops 9984 | bytes 59904
  521.0 4.9 all-reduce.22
  530.6 10.9 %add_convert_fusion = bf16[1024,768]{0,1:T(8,128)(2,1)} fusion(f32[1024,768]{0,1:T(8,128)} %copy-done.3, bf16[1024,3072]{1,0:T(8,128)(2,1)} %get-tuple-element.168, bf16[3072,768]{1,0:T(8,128)(2,1)} %all-gather.11.cloned.1.call-done, f32[768]{0:T(1024)S(1)} %convert_element_type.172), kind=kOutput, calls=%fused_computation.109 | convolution fusion | flops 4834197504 | bytes 15731712 | tf_op jit(solution)/shard_map/dot_general | solution.py:202
  544.9 77.4 %reduce-scatter.9.cloned.1.call-done = f32[48,3072]{1,0:T(8,128)} async-done(((f32[768,3072]{1,0:T(8,128)}), f32[48,3072]{1,0:T(8,128)}) %reduce-scatter.9.cloned.1.call-update) | async-done | bytes 589840 | tf_op jit(solution)/shard_map/reduce_scatter | solution.py:140
  624.2 114.0 %reduce-scatter.11.cloned.1.call-done = f32[192,768]{1,0:T(8,128)} async-done(((f32[3072,768]{1,0:T(8,128)}), f32[192,768]{1,0:T(8,128)}) %reduce-scatter.11.cloned.1.call-update) | async-done | bytes 589840 | tf_op jit(solution)/shard_map/reduce_scatter | solution.py:142
  740.0 3.9 fusion.54
  747.0 31.6 %all-reduce.26.cloned.1.call-done = (bf16[48,2304]{1,0:T(8,128)(2,1)}, bf16[48,768]{1,0:T(8,128)(2,1)}, bf16[48,3072]{1,0:T(8,128)(2,1)}, bf16[192,768]{1,0:T(8,128)(2,1)}) async-done(((bf16[48,2304]{1,0:T(8,128)(2,1)}, bf16[48,768]{1,0:T(8,128)(2,1)}, bf16[48,3072]{1,0:T(8,128)(2,1)}, bf16[192,768]{1,0:T(8,128)(2,1)}), (bf16[48,2304]{1,0:T(8,128)(2,1)}, bf16[48,768]{1,0:T(8,128)(2,1)}, ...) | async-done | bytes 884752 | tf_op jit(solution)/shard_map/psum | solution.py:148
  (222 shorter events, 79.0 us)
Async XLA Ops:
  7.2 111.2 %copy-start = (f32[12,32,64]{2,1,0:T(8,128)S(1)}, f32[12,32,64]{2,1,0:T(8,128)}, u32[]{:S(2)}) copy-start(f32[12,32,64]{2,1,0:T(8,128)} %param.19) | copy-start | bytes 294916
  7.2 87.5 %all-gather.5.cloned.1.call-start = ((), (), s32[]{:S(2)}) async-start(), calls=%async_computation.4 | async-start | bytes 3760128 | tf_op jit(solution)/shard_map/all_gather | solution.py:118
  7.9 176.4 %all-gather.7.cloned.1.call-start = ((), (), s32[]{:S(2)}) async-start(), calls=%async_computation.5 | async-start | bytes 1253376 | tf_op jit(solution)/shard_map/all_gather | solution.py:120
  8.7 181.2 %all-gather.9.cloned.1.call-start = ((), (), s32[]{:S(2)}) async-start(), calls=%async_computation.6 | async-start | bytes 5013504 | tf_op jit(solution)/shard_map/all_gather | solution.py:118
  9.4 219.4 %all-gather.11.cloned.1.call-start = ((), (), s32[]{:S(2)}) async-start(), calls=%async_computation.7 | async-start | bytes 5013504 | tf_op jit(solution)/shard_map/all_gather | solution.py:120
  10.0 531.5 %reduce-scatter.7.cloned.1.call-start = ((), (), s32[]{:S(2)}) async-start(), calls=%async_computation.9 | async-start | bytes 2506752 | tf_op jit(solution)/shard_map/reduce_scatter | solution.py:142
  85.5 9.2 %copy-start.29 = (f32[768]{0:T(1024)}, f32[768]{0:T(1024)S(1)}, u32[]{:S(2)}) copy-start(f32[768]{0:T(1024)S(1)} %convert_element_type.159) | copy-start | bytes 9220
  86.7 6.3 copy-start.12
  88.5 95.8 %copy-start.1 = (bf16[1024,768]{0,1:T(8,128)(2,1)}, bf16[1024,768]{0,1:T(8,128)(2,1)S(1)}, u32[]{:S(2)}) copy-start(bf16[1024,768]{0,1:T(8,128)(2,1)S(1)} %copy.55) | copy-start | bytes 4718596
  88.9 14.4 %copy-start.25 = (f32[1024]{0:T(1024)}, f32[1024]{0:T(1024)S(1)}, u32[]{:S(2)}) copy-start(f32[1024]{0:T(1024)S(1)} %broadcast_multiply_fusion.5) | copy-start | bytes 12292
  89.3 13.9 %copy-start.31 = (f32[1024]{0:T(1024)}, f32[1024]{0:T(1024)S(1)}, u32[]{:S(2)}) copy-start(f32[1024]{0:T(1024)S(1)} %add_rsqrt_fusion.1) | copy-start | bytes 12292
  90.6 26.3 %copy-start.19 = (f32[1024,32]{0,1:T(8,128)}, f32[1024,32]{0,1:T(8,128)S(1)}, u32[]{:S(2)}) copy-start(f32[1024,32]{0,1:T(8,128)S(1)} %get-tuple-element.158) | copy-start | bytes 393220
  113.0 9.1 %slice-start = ((s8[9437184]{0:T(1024)(128)(4,1)}), s8[4194304]{0:T(1024)(128)(4,1)S(1)}, s32[]{:S(2)}) async-start(s8[9437184]{0:T(1024)(128)(4,1)} %bitcast.182), calls=%async_computation.13 | async-start | bytes 8388608
  113.0 9.1 %slice-start.1 = ((s8[9437184]{0:T(1024)(128)(4,1)}), s8[4194304]{0:T(1024)(128)(4,1)S(1)}, s32[]{:S(2)}) async-start(s8[9437184]{0:T(1024)(128)(4,1)} %bitcast.182), calls=%async_computation.14 | async-start | bytes 8388608
  116.8 5.2 slice-start.2
  122.0 21.6 %copy-start.7 = (f32[1024,12,32]{0,2,1:T(8,128)}, f32[1024,12,32]{0,2,1:T(8,128)S(1)}, u32[]{:S(2)}) copy-start(f32[1024,12,32]{0,2,1:T(8,128)S(1)} %get-tuple-element.162) | copy-start | bytes 4718596
  143.7 21.7 %copy-start.48 = (f32[12,64,16,32]{1,3,2,0:T(8,128)}, f32[12,64,16,32]{1,3,2,0:T(8,128)S(1)}, u32[]{:S(2)}) copy-start(f32[12,64,16,32]{1,3,2,0:T(8,128)S(1)} %fusion.10) | copy-start | bytes 4718596
  149.3 16.1 %copy-start.17 = (f32[1024,12,32]{0,2,1:T(8,128)}, f32[1024,12,32]{0,2,1:T(8,128)S(1)}, u32[]{:S(2)}) copy-start(f32[1024,12,32]{0,2,1:T(8,128)S(1)} %get-tuple-element.160) | copy-start | bytes 4718596
  149.3 16.0 %copy-start.33 = (f32[1024]{0:T(1024)S(1)}, f32[1024]{0:T(1024)}, u32[]{:S(2)}) copy-start(f32[1024]{0:T(1024)} %broadcast_subtract_fusion) | copy-start | bytes 12292
  166.0 18.3 %copy-start.38 = (f32[768]{0:T(1024)S(1)}, f32[768]{0:T(1024)}, u32[]{:S(2)}) copy-start(f32[768]{0:T(1024)} %convert_element_type.166) | copy-start | bytes 9220
  228.8 11.9 %copy-start.44 = (bf16[768,3072]{1,0:T(8,128)(2,1)S(1)}, bf16[768,3072]{1,0:T(8,128)(2,1)}, u32[]{:S(2)}) copy-start(bf16[768,3072]{1,0:T(8,128)(2,1)} %all-gather.9.cloned.1.call-done) | copy-start | bytes 14155780
  240.7 6.8 copy-start.47
  261.0 282.1 %reduce-scatter.5.cloned.1.call-start = ((), (), s32[]{:S(2)}) async-start(), calls=%async_computation.8 | async-start | bytes 7520256 | tf_op jit(solution)/shard_map/reduce_scatter | solution.py:140
  264.4 21.4 %copy-start.11 = (f32[12,64,1024,1]{2,1,3,0:T(8,128)S(1)}, f32[12,64,1024,1]{2,1,3,0:T(8,128)}, u32[]{:S(2)}) copy-start(f32[12,64,1024,1]{2,1,3,0:T(8,128)} %get-tuple-element.165) | copy-start | bytes 9437188
  286.8 49.4 %copy-start.24 = (f32[16,12,32]{2,0,1:T(8,128)S(1)}, f32[16,12,32]{2,0,1:T(8,128)}, u32[]{:S(2)}) copy-start(f32[16,12,32]{2,0,1:T(8,128)} %copy-done.23) | copy-start | bytes 73732
  286.8 49.4 %copy-start.49 = (f32[12,64,16,32]{1,3,2,0:T(8,128)S(1)}, f32[12,64,16,32]{1,3,2,0:T(8,128)}, u32[]{:S(2)}) copy-start(f32[12,64,16,32]{1,3,2,0:T(8,128)} %copy-done.48) | copy-start | bytes 4718596
  358.8 22.8 %copy-start.15 = (f32[12,1024,32]{1,2,0:T(8,128)S(1)}, f32[12,1024,32]{1,2,0:T(8,128)}, u32[]{:S(2)}) copy-start(f32[12,1024,32]{1,2,0:T(8,128)} %get-tuple-element.163) | copy-start | bytes 4718596
  385.6 4.0 copy-start.20
  385.6 4.0 copy-start.22
  419.2 203.1 %reduce-scatter.9.cloned.1.call-start = ((), (), s32[]{:S(2)}) async-start(), calls=%async_computation.10 | async-start | bytes 10027008 | tf_op jit(solution)/shard_map/reduce_scatter | solution.py:140
  430.0 308.2 %reduce-scatter.11.cloned.1.call-start = ((), (), s32[]{:S(2)}) async-start(), calls=%async_computation.11 | async-start | bytes 10027008 | tf_op jit(solution)/shard_map/reduce_scatter | solution.py:142
  442.4 336.2 %all-reduce.26.cloned.1.call-start = ((), (), s32[]{:S(2)}) async-start(), calls=%async_computation.12 | async-start | bytes 1769472 | tf_op jit(solution)/shard_map/psum | solution.py:148
  (30 other events, 80.8 us)
Sparse Core Ops, SparseCore 0:
  10.3 50.8 all-gather.4
  63.5 36.6 all-gather.6
  102.5 52.2 all-gather.8
  156.9 51.7 all-gather.10
  261.1 60.1 reduce-scatter.6
  419.3 87.8 reduce-scatter.4
  511.3 110.9 reduce-scatter.8
  627.0 111.0 reduce-scatter.10
  741.8 36.7 all-reduce.25
where the time goes:
time: 801 us; the launch traced here: 793 us
  matrix products  329 us (41%)
  waiting for transfers between devices  226 us (28%)
  blocking collectives  128 us (16%)
  local copies, waits for them, and re-layouts  46.5 us (6%)
  other arithmetic  44.3 us (6%)
  between operations  19.1 us (2%)
    unnamed x2, blocking collectives  123 us
    reduce_scatter x2, waiting for transfers between devices, reduce_grads(): lax.psum_scatter(grads[4], 'fsdp', scatter_dimension=0, tiled=True)  114 us
    reduce_scatter x2, waiting for transfers between devices, reduce_grads(): lax.psum_scatter(grads[2], 'fsdp', scatter_dimension=0, tiled=True)  77.4 us
    dot_general x2, matrix products, segment_core(): jnp.einsum('nshf,shf->nh', masked_queries, totals, precision=highest)  65.4 us
    dot_general x3, matrix products, segment_core(): jnp.einsum('nshf,shfd->nhd', masked_queries, kv_state, precision=highest)  62.4 us
    dot_general x3, matrix products, segment_core(): jnp.einsum('nshf,nhd->shfd', masked_keys, value_rows, precision=highest)  61.4 us
    dot_general x1, matrix products, body(): jnp.dot(hidden_two, weight_in, preferred_element_type=jnp.float32)  38.9 us
    dot_general x4, matrix products, contract_cols(): lax.dot_general(left, right, (((1,), (1,)), ((), ())), preferred_element_...  31.8 us
  transfers between devices with their start and end apart: 9, of which 3 were waited for; matrix products, arithmetic and copies ran while one was open for 47% of the time, Pallas kernels for 0%

commit v1 on v0

v1 whole, which is shorter than its diff:
```python
import functools

import jax
import jax.numpy as jnp
import numpy as np
from jax import lax
from jax.experimental import pallas as pl
from jax.experimental.pallas import tpu as pltpu
from jax.sharding import PartitionSpec as P

HEADS = 12
HEAD_DIM = 64
FEATS = 32
SEGS = 16
PACK = 4
GROUPS = HEADS // PACK
WIDE = PACK * HEAD_DIM
SLIM = PACK * FEATS
STATE = SEGS * SLIM
EPSILON = 1e-05
F32 = jnp.float32
BF16 = jnp.bfloat16
VMEM_LIMIT = 67_000_000

GAIN1, SHIFT1, BIAS_OUT, GAIN2, SHIFT2, BIAS_FFO, BIAS_QKV, BIAS_IN = range(8)


def contract(left, right, left_dim, right_dim):
    return lax.dot_general(
        left, right, (((left_dim,), (right_dim,)), ((), ())), preferred_element_type=F32
    )


def nn(left, right):
    return contract(left, right, 1, 0)


def nt(left, right):
    return contract(left, right, 1, 1)


def tn(left, right):
    return contract(left, right, 0, 0)


def tile(index, size):
    return pl.ds(pl.multiple_of(index * size, size), size)


def iota(shape, dim):
    return lax.broadcasted_iota(jnp.int32, shape, dim)


def split_two(values):
    high = values.astype(BF16)
    return high, (values - high.astype(F32)).astype(BF16)


def normalize(rows):
    centred = rows - jnp.mean(rows, axis=-1, keepdims=True)
    inv_std = lax.rsqrt(jnp.mean(centred * centred, axis=-1, keepdims=True) + EPSILON)
    return centred * inv_std, inv_std


def normalize_back(incoming, normed, inv_std, gain):
    scaled = incoming * gain
    mean_one = jnp.mean(scaled, axis=-1, keepdims=True)
    mean_two = jnp.mean(scaled * normed, axis=-1, keepdims=True)
    return inv_std * (scaled - mean_one - normed * mean_two)


def column_sum(values):
    return jnp.sum(values, axis=0, keepdims=True)


def head_blocks(rows, columns, row_width, column_width):
    return (iota((rows, columns), 0) // row_width) == (iota((rows, columns), 1) // column_width)


def ones_where(mask):
    return jnp.where(mask, 1.0, 0.0).astype(BF16)


def projection_blocks(proj_ref, group):
    small = proj_ref[tile(group, SLIM), :].astype(BF16)
    source, lane = iota((HEAD_DIM, WIDE), 0), iota((HEAD_DIM, WIDE), 1) % HEAD_DIM
    half = HEAD_DIM // 2
    plain = jnp.where(source == lane, 1.0, 0.0)
    turned = jnp.where(source == (lane + half) % HEAD_DIM, jnp.where(lane < half, 1.0, -1.0), 0.0)
    keep = head_blocks(SLIM, WIDE, FEATS, HEAD_DIM)
    return (
        jnp.where(keep, nn(small, plain.astype(BF16)), 0.0).astype(BF16),
        jnp.where(keep, nn(small, turned.astype(BF16)), 0.0).astype(BF16),
    )


def segment_masks(seg_ref, one_ref, mexp_ref):
    length = seg_ref.shape[1]
    one_ref[...] = ones_where(iota((SEGS, length), 0) == seg_ref[...])
    expand = ones_where(head_blocks(SEGS, STATE, 1, SLIM))

    @pl.loop(0, length // 256)
    def _(r):
        mexp_ref[tile(r, 256), :] = tn(one_ref[:, tile(r, 256)], expand).astype(BF16)


def denominators(fq, one_rows, total):
    high, low = split_two(total)
    total_rows = tn(one_rows, high) + tn(one_rows, low)
    absent = 1.0 - tn(one_rows, jnp.ones((SEGS, WIDE), BF16))
    products = (fq.astype(F32) * total_rows).astype(BF16)
    wide = nn(products, ones_where(head_blocks(SLIM, WIDE, FEATS, HEAD_DIM))) + absent
    slim = nn(products, ones_where(head_blocks(SLIM, SLIM, FEATS, FEATS))) + absent[:, :SLIM]
    return total_rows, wide, slim, absent


def spread(features, masks):
    return jnp.concatenate([features] * SEGS, axis=1) * masks


def segment_states(feature_ref, one_ref, value, group, out_ref, base):
    turned = feature_ref[:, tile(group, SLIM)].astype(F32).T.astype(BF16)
    keep = head_blocks(SLIM, WIDE, FEATS, HEAD_DIM)
    chunk = 8
    for part in range(SEGS // chunk):
        left = jnp.concatenate(
            [turned * one_ref[s : s + 1, :] for s in range(part * chunk, (part + 1) * chunk)], axis=0
        )
        sums = nn(left, value)
        for s in range(chunk):
            piece = jnp.where(keep, sums[s * SLIM : (s + 1) * SLIM], 0.0).astype(BF16)
            row = base + (part * chunk + s) * SLIM
            out_ref[pl.ds(pl.multiple_of(row, SLIM), SLIM), :] = piece


def masked_sum(products, masks):
    out = products[:, :SLIM] * masks[:, :SLIM].astype(F32)
    for s in range(1, SEGS):
        span = slice(s * SLIM, (s + 1) * SLIM)
        out = out + products[:, span] * masks[:, span].astype(F32)
    return out


def twice(table):
    return jnp.concatenate([table, table], axis=1)


def phase_norm_one(tok_ref, vec_ref, h1_ref, hbar_ref):
    length, width = tok_ref.shape
    hbar_ref[...] = jnp.zeros_like(hbar_ref)

    @pl.loop(0, tok_ref.shape[0] // 256)
    def _(r):
        normed, _inv = normalize(tok_ref[tile(r, 256), :].astype(F32))
        rows = normed * vec_ref[GAIN1 : GAIN1 + 1, :width] + vec_ref[SHIFT1 : SHIFT1 + 1, :width]
        h1_ref[tile(r, 256), :] = rows.astype(BF16)
        hbar_ref[0:1, :] += column_sum(rows) * (1.0 / length)


def phase_attention(
    h1_ref, hbar_ref, w_qkv_ref, vec_ref, proj_ref, cos_ref, sin_ref, one_ref, mexp_ref,
    fq_ref, fk_ref, sq_ref, sk_ref, v_ref, state_ref, total_ref, att_ref, attc_ref,
):
    length, width = h1_ref.shape

    @pl.loop(0, GROUPS)
    def _(g):
        cols, feats = tile(g, WIDE), tile(g, SLIM)
        plain, turned = projection_blocks(proj_ref, g)
        for kind, (feat_ref, slope_ref) in enumerate(((fq_ref, sq_ref), (fk_ref, sk_ref))):
            span = pl.ds(pl.multiple_of(kind * width + g * WIDE, WIDE), WIDE)

            @pl.loop(0, length // 512)
            def _(r):
                rows = tile(r, 512)
                x = nn(h1_ref[rows, :], w_qkv_ref[:, span]) + vec_ref[BIAS_QKV : BIAS_QKV + 1, span]
                u = nt((x * twice(cos_ref[rows, :])).astype(BF16), plain) + nt(
                    (x * twice(sin_ref[rows, :])).astype(BF16), turned
                )
                small = jnp.exp(-jnp.abs(u))
                feat_ref[rows, feats] = (jnp.maximum(u, 0.0) + jnp.log1p(small)).astype(BF16)
                slope_ref[rows, feats] = jnp.where(u >= 0.0, 1.0, small) / (1.0 + small)

        span = pl.ds(pl.multiple_of(2 * width + g * WIDE, WIDE), WIDE)
        shared = nn(hbar_ref[...].astype(BF16), w_qkv_ref[:, span])[0:1]

        @pl.loop(0, length // 512)
        def _(r):
            rows = tile(r, 512)
            v_ref[rows, cols] = (nn(h1_ref[rows, :], w_qkv_ref[:, span]) - shared).astype(BF16)

        shared = shared + vec_ref[BIAS_QKV : BIAS_QKV + 1, span]

        segment_states(fk_ref, one_ref, v_ref[:, cols], g, state_ref, g * STATE)
        total = nn(one_ref[...], fk_ref[:, feats])
        total_ref[:, feats] = total

        @pl.loop(0, length // 256)
        def _(r):
            rows = tile(r, 256)
            fq = fq_ref[rows, feats]
            numerator = nn(spread(fq, mexp_ref[rows, :]), state_ref[tile(g, STATE), :])
            _rows, wide, _slim, absent = denominators(fq, one_ref[:, rows], total_ref[:, feats])
            centred = numerator / wide
            attc_ref[rows, cols] = centred.astype(BF16)
            att_ref[rows, cols] = (centred + (1.0 - absent) * shared).astype(BF16)


def phase_middle(tok_ref, att_ref, w_out_ref, vec_ref, mid_ref, h2_ref):
    length, width = tok_ref.shape

    @pl.loop(0, length // 512)
    def _(r):
        rows = tile(r, 512)
        middle = (
            tok_ref[rows, :].astype(F32)
            + nn(att_ref[rows, :], w_out_ref[...])
            + vec_ref[BIAS_OUT : BIAS_OUT + 1, :width]
        )
        mid_ref[rows, :] = middle
        normed, _inv = normalize(middle)
        hidden = normed * vec_ref[GAIN2 : GAIN2 + 1, :width] + vec_ref[SHIFT2 : SHIFT2 + 1, :width]
        h2_ref[rows, :] = hidden.astype(BF16)


def phase_gelu(h2_ref, w_in_ref, vec_ref, act_ref, slope_ref):
    length, hidden = h2_ref.shape[0], w_in_ref.shape[1]

    @pl.loop(0, hidden // 256)
    def _(j):
        cols = tile(j, 256)
        pre = nn(h2_ref[...], w_in_ref[:, cols]) + vec_ref[BIAS_IN : BIAS_IN + 1, cols]
        gate = 0.5 * (1.0 + lax.erf(pre * 0.7071067811865476))
        act_ref[:, cols] = (pre * gate).astype(BF16)
        slope = gate + pre * jnp.exp(-0.5 * pre * pre) * 0.3989422804014327
        slope_ref[:, cols] = slope.astype(BF16)


def phase_ffo_grad(act_ref, cot_ref, g_ffo_ref):
    @pl.loop(0, act_ref.shape[1] // 512)
    def _(j):
        g_ffo_ref[tile(j, 512), :] = tn(act_ref[:, tile(j, 512)], cot_ref[...]).astype(BF16)


def phase_output(mid_ref, act_ref, w_ffo_ref, vec_ref, out_ref):
    length, width = mid_ref.shape

    @pl.loop(0, length // 512)
    def _(r):
        rows = tile(r, 512)
        total = mid_ref[rows, :] + nn(act_ref[rows, :], w_ffo_ref[...])
        out_ref[rows, :] = (total + vec_ref[BIAS_FFO : BIAS_FFO + 1, :width]).astype(BF16)


def phase_grad_pre(cot_ref, w_ffo_ref, slope_ref, gpre_ref, small_ref):
    @pl.loop(0, w_ffo_ref.shape[0] // 256)
    def _(j):
        cols = tile(j, 256)
        grad = nt(cot_ref[...], w_ffo_ref[cols, :]) * slope_ref[:, cols].astype(F32)
        grad = grad.astype(BF16)
        gpre_ref[:, cols] = grad
        small_ref[BIAS_IN : BIAS_IN + 1, cols] = column_sum(grad.astype(F32))


def phase_weight_grad(left_ref, right_ref, out_ref):
    @pl.loop(0, left_ref.shape[1] // 256)
    def _(i):
        out_ref[tile(i, 256), :] = tn(left_ref[:, tile(i, 256)], right_ref[...]).astype(BF16)


def phase_norm_two_back(gpre_ref, w_in_ref, mid_ref, cot_ref, vec_ref, gmid_ref, gbr_ref, small_ref):
    length, width = mid_ref.shape
    small_ref[GAIN2 : SHIFT2 + 1, :width] = jnp.zeros((2, width), F32)
    small_ref[BIAS_FFO : BIAS_FFO + 1, :width] = jnp.zeros((1, width), F32)
    small_ref[BIAS_OUT : BIAS_OUT + 1, :width] = jnp.zeros((1, width), F32)

    @pl.loop(0, length // 512)
    def _(r):
        rows = tile(r, 512)
        incoming = nt(gpre_ref[rows, :], w_in_ref[...])
        normed, inv_std = normalize(mid_ref[rows, :])
        upstream = cot_ref[rows, :].astype(F32)
        grad = upstream + normalize_back(incoming, normed, inv_std, vec_ref[GAIN2 : GAIN2 + 1, :width])
        gmid_ref[rows, :] = grad
        branch = grad.astype(BF16)
        gbr_ref[rows, :] = branch
        small_ref[GAIN2 : GAIN2 + 1, :width] += column_sum(incoming * normed)
        small_ref[SHIFT2 : SHIFT2 + 1, :width] += column_sum(incoming)
        small_ref[BIAS_FFO : BIAS_FFO + 1, :width] += column_sum(upstream)
        small_ref[BIAS_OUT : BIAS_OUT + 1, :width] += column_sum(branch.astype(F32))


def phase_attention_back(
    gbr_ref, w_out_ref, attc_ref, proj_ref, cos_ref, sin_ref, one_ref, mexp_ref,
    fq_ref, fk_ref, sq_ref, sk_ref, v_ref, state_ref, total_ref,
    dnum_ref, dstate_ref, dtotal_ref, gproj_ref, small_ref,
):
    length, width = gbr_ref.shape

    @pl.loop(0, GROUPS)
    def _(g):
        cols, feats = tile(g, WIDE), tile(g, SLIM)
        q_span = cols
        k_span = pl.ds(pl.multiple_of(width + g * WIDE, WIDE), WIDE)
        v_span = pl.ds(pl.multiple_of(2 * width + g * WIDE, WIDE), WIDE)
        plain, turned = projection_blocks(proj_ref, g)
        dtotal_ref[...] = jnp.zeros_like(dtotal_ref)
        for span in (q_span, k_span, v_span):
            small_ref[BIAS_QKV : BIAS_QKV + 1, span] = jnp.zeros((1, WIDE), F32)

        def unrotate(grad, rows, span):
            high, low = split_two(grad)
            back = (nn(high, plain) + nn(low, plain)) * twice(cos_ref[rows, :])
            back = back + (nn(high, turned) + nn(low, turned)) * twice(sin_ref[rows, :])
            back = back.astype(BF16)
            gproj_ref[rows, span] = back
            small_ref[BIAS_QKV : BIAS_QKV + 1, span] += column_sum(back.astype(F32))

        @pl.loop(0, length // 256)
        def _(r):
            rows = tile(r, 256)
            grad_att = nt(gbr_ref[rows, :], w_out_ref[cols, :])
            fq = fq_ref[rows, feats]
            total_rows, wide, slim, _absent = denominators(fq, one_ref[:, rows], total_ref[:, feats])
            dnum = (grad_att / wide).astype(BF16)
            dnum_ref[rows, :] = dnum
            dots = nn(
                (dnum.astype(F32) * attc_ref[rows, cols].astype(F32)).astype(BF16),
                ones_where(head_blocks(WIDE, SLIM, HEAD_DIM, FEATS)),
            )
            dden = -dots
            dfq = masked_sum(nt(dnum, state_ref[tile(g, STATE), :]), mexp_ref[rows, :])
            dfq = dfq + dden * total_rows
            dtotal_ref[...] += nn(one_ref[:, rows], (dden * fq.astype(F32)).astype(BF16))
            unrotate(dfq * sq_ref[rows, feats], rows, q_span)

        segment_states(fq_ref, one_ref, dnum_ref[...], g, dstate_ref, 0)

        @pl.loop(0, length // 256)
        def _(r):
            rows = tile(r, 256)
            dv = nn(spread(fk_ref[rows, feats], mexp_ref[rows, :]), dstate_ref[...]).astype(BF16)
            gproj_ref[rows, v_span] = dv
            small_ref[BIAS_QKV : BIAS_QKV + 1, v_span] += column_sum(dv.astype(F32))
            high, low = split_two(dtotal_ref[...])
            one_rows = one_ref[:, rows]
            dfk = masked_sum(nt(v_ref[rows, cols], dstate_ref[...]), mexp_ref[rows, :])
            dfk = dfk + tn(one_rows, high) + tn(one_rows, low)
            unrotate(dfk * sk_ref[rows, feats], rows, k_span)


def phase_norm_one_back(gproj_ref, w_qkv_ref, tok_ref, gmid_ref, vec_ref, tgrad_ref, small_ref):
    length, width = tok_ref.shape
    small_ref[GAIN1 : SHIFT1 + 1, :width] = jnp.zeros((2, width), F32)

    @pl.loop(0, length // 512)
    def _(r):
        rows = tile(r, 512)
        incoming = nt(gproj_ref[rows, :], w_qkv_ref[...])
        normed, inv_std = normalize(tok_ref[rows, :].astype(F32))
        back = normalize_back(incoming, normed, inv_std, vec_ref[GAIN1 : GAIN1 + 1, :width])
        tgrad_ref[rows, :] = (gmid_ref[rows, :] + back).astype(BF16)
        small_ref[GAIN1 : GAIN1 + 1, :width] += column_sum(incoming * normed)
        small_ref[SHIFT1 : SHIFT1 + 1, :width] += column_sum(incoming)


def forward_kernel(
    tok, seg, proj, cos, sin, vec, w_qkv, w_out, w_in,
    h1, fq, fk, sq, sk, v, state, total, att, attc, mid, h2, act, slope, one, mexp, hbar,
):
    segment_masks(seg, one, mexp)
    phase_norm_one(tok, vec, h1, hbar)
    phase_attention(
        h1, hbar, w_qkv, vec, proj, cos, sin, one, mexp,
        fq, fk, sq, sk, v, state, total, att, attc,
    )
    phase_middle(tok, att, w_out, vec, mid, h2)
    phase_gelu(h2, w_in, vec, act, slope)


def feed_kernel(cot, vec, w_in, w_ffo, mid, h2, act, slope, out, g_ffo, g_in, gmid, gbr, small, gpre):
    phase_ffo_grad(act, cot, g_ffo)
    phase_output(mid, act, w_ffo, vec, out)
    phase_grad_pre(cot, w_ffo, slope, gpre, small)
    phase_weight_grad(h2, gpre, g_in)
    phase_norm_two_back(gpre, w_in, mid, cot, vec, gmid, gbr, small)


def back_kernel(
    tok, seg, proj, cos, sin, vec, w_qkv, w_out, h1, fq, fk, sq, sk, v, state, total, att, attc, gmid, gbr,
    tgrad, g_out, g_qkv, small, one, mexp, dnum, dstate, dtotal, gproj,
):
    segment_masks(seg, one, mexp)
    phase_weight_grad(att, gbr, g_out)
    phase_attention_back(
        gbr, w_out, attc, proj, cos, sin, one, mexp, fq, fk, sq, sk, v, state, total,
        dnum, dstate, dtotal, gproj, small,
    )
    phase_weight_grad(h1, gproj, g_qkv)
    phase_norm_one_back(gproj, w_qkv, tok, gmid, vec, tgrad, small)


def shape(dims, dtype=BF16):
    return jax.ShapeDtypeStruct(dims, dtype)


def in_vmem(count):
    return [pl.BlockSpec(memory_space=pltpu.VMEM)] * count


def call_plain(kernel, name, outs, scratch, *operands):
    return pl.pallas_call(
        kernel,
        out_shape=outs,
        in_specs=in_vmem(len(operands)),
        out_specs=in_vmem(len(outs)),
        scratch_shapes=scratch,
        compiler_params=pltpu.CompilerParams(vmem_limit_bytes=VMEM_LIMIT),
        name=name,
    )(*operands)


def position_tables(length):
    half = HEAD_DIM // 2
    frequency = 10000.0 ** (-np.arange(half, dtype=np.float64) / half)
    angles = np.arange(length, dtype=np.float64)[:, None] * frequency[None, :]
    repeat = SLIM // half
    return (
        np.tile(np.cos(angles), (1, repeat)).astype(np.float32),
        np.tile(np.sin(angles), (1, repeat)).astype(np.float32),
    )


def gather(value):
    return lax.all_gather(value, "fsdp", axis=0, tiled=True)


def reduce_full(grad):
    piece = lax.psum_scatter(grad.astype(F32), "fsdp", scatter_dimension=0, tiled=True)
    return lax.psum(piece.astype(BF16), "dp").astype(F32)


def body(
    tokens, segment_ids, projection, norm1_gain, norm1_bias, qkv_weight, qkv_bias, out_weight, out_bias,
    norm2_gain, norm2_bias, in_weight, in_bias, ffn_out_weight, ffn_out_bias, cotangent,
):
    length, width = tokens.shape
    hidden = in_weight.shape[1]
    groups = lax.axis_size("fsdp")
    cos, sin = position_tables(length)
    proj = projection.reshape(HEADS * FEATS, HEAD_DIM)
    w_qkv, w_out, w_in, w_ffo = (
        gather(w) for w in (qkv_weight, out_weight, in_weight, ffn_out_weight)
    )
    vec = jnp.stack(
        [
            jnp.pad(gather(v).astype(F32), (0, hidden - v.shape[0] * groups))
            for v in (
                norm1_gain, norm1_bias, out_bias, norm2_gain, norm2_bias, ffn_out_bias, qkv_bias, in_bias,
            )
        ]
    )
    feats = HEADS * FEATS
    masks = [pltpu.VMEM((SEGS, length), BF16), pltpu.VMEM((length, STATE), BF16)]
    h1, fq, fk, sq, sk, v, state, total, att, attc, mid, h2, act, slope = call_plain(
        forward_kernel,
        "forward",
        [
            shape((length, width)), shape((length, feats)), shape((length, feats)),
            shape((length, feats), F32), shape((length, feats), F32), shape((length, width)),
            shape((GROUPS * STATE, WIDE)), shape((SEGS, feats), F32), shape((length, width)),
            shape((length, width)),
            shape((length, width), F32), shape((length, width)), shape((length, hidden)),
            shape((length, hidden)),
        ],
        masks + [pltpu.VMEM((8, width), F32)],
        tokens, segment_ids, proj, cos, sin, vec, w_qkv, w_out, w_in,
    )
    output, g_ffo, g_in, gmid, gbr, small_two = call_plain(
        feed_kernel,
        "feed",
        [
            shape((length, width)), shape((hidden, width)), shape((width, hidden)),
            shape((length, width), F32), shape((length, width)), shape((8, hidden), F32),
        ],
        [pltpu.VMEM((length, hidden), BF16)],
        cotangent, vec, w_in, w_ffo, mid, h2, act, slope,
    )
    tgrad, g_out, g_qkv, small_one = call_plain(
        back_kernel,
        "back",
        [
            shape((length, width)), shape((width, width)), shape((width, 3 * width)), shape((8, hidden), F32),
        ],
        masks
        + [
            pltpu.VMEM((length, WIDE), BF16), pltpu.VMEM((STATE, WIDE), BF16),
            pltpu.VMEM((SEGS, SLIM), F32), pltpu.VMEM((length, 3 * width), BF16),
        ],
        tokens, segment_ids, proj, cos, sin, vec, w_qkv, w_out,
        h1, fq, fk, sq, sk, v, state, total, att, attc, gmid, gbr,
    )
    smalls = {
        GAIN1: small_one[GAIN1, :width], SHIFT1: small_one[SHIFT1, :width],
        BIAS_OUT: small_two[BIAS_OUT, :width], GAIN2: small_two[GAIN2, :width],
        SHIFT2: small_two[SHIFT2, :width], BIAS_FFO: small_two[BIAS_FFO, :width],
        BIAS_QKV: small_one[BIAS_QKV, : 3 * width], BIAS_IN: small_two[BIAS_IN, :],
    }
    qkv_bias_grad = smalls[BIAS_QKV]
    return (
        output,
        tgrad,
        reduce_full(smalls[GAIN1]),
        reduce_full(smalls[SHIFT1]),
        reduce_full(g_qkv),
        reduce_full(qkv_bias_grad[: 2 * width]),
        reduce_full(qkv_bias_grad[2 * width :]),
        reduce_full(g_out),
        reduce_full(smalls[BIAS_OUT]),
        reduce_full(smalls[GAIN2]),
        reduce_full(smalls[SHIFT2]),
        reduce_full(g_in),
        reduce_full(smalls[BIAS_IN]),
        reduce_full(g_ffo),
        reduce_full(smalls[BIAS_FFO]),
    )


def solution(mesh):
    rows = P(("fsdp", "dp"), None)
    vector, matrix = P("fsdp"), P("fsdp", None)
    in_specs = (
        rows, rows, P(), vector, vector, matrix, vector, matrix, vector,
        vector, vector, matrix, vector, matrix, vector, rows,
    )
    out_specs = (
        rows, rows, vector, vector, matrix, vector, vector, matrix, vector,
        vector, vector, matrix, vector, matrix, vector,
    )
    return jax.shard_map(body, mesh=mesh, in_specs=in_specs, out_specs=out_specs, check_vma=False)
```

time: 801 us -> 676 us (0.84)
  matrix products: 329 us -> 0 us
  Pallas kernels: 0 us -> 150 us
  waiting for transfers between devices: 226 us -> 357 us
  local copies, waits for them, and re-layouts: 46.5 us -> 12.5 us
  other arithmetic: 44.3 us -> 10.5 us
    dot_general x24 -> x0, matrix products: 329 us -> none  [the longest x2 65.4 us: segment_core(): jnp.einsum('nshf,shf->nh', masked_queries, totals, precision=highest)]
    pallas_call x0 -> x3, Pallas kernels: none -> 150 us  [call_plain(): pl.pallas_call(kernel, out_shape=outs, in_specs=in_vmem(len(operands)), o...]
    reduce_scatter x4, waiting for transfers between devices: 191 us -> 283 us  [reduce_full(): lax.psum_scatter(grad.astype(F32), 'fsdp', scatter_dimension=0, tiled=True)]
    all_gather x4, waiting for transfers between devices: 0.04 us -> 70 us  [gather(): return lax.all_gather(value, 'fsdp', axis=0, tiled=True)]
    psum x1, waiting for transfers between devices: 31.6 us -> 0.01 us  [reduce_full(): return lax.psum(piece.astype(BF16), 'dp').astype(F32)]
    unnamed x135 -> x30, local copies, waits for them, and re-layouts: 24.5 us -> 8.73 us
    convert_element_type x25 -> x13, other arithmetic: 25.1 us -> 9.8 us  [reduce_full(): return lax.psum(piece.astype(BF16), 'dp').astype(F32)]
    reduce_sum x10 -> x0, other arithmetic: 13.1 us -> none  [the longest x2 5.94 us: norm_backward(): jnp.sum(incoming * normed, axis=0)]
  transfers between devices with their start and end apart: 9 -> 9, of which waited for: 3 -> 7; matrix products, arithmetic and copies ran while one was open for 47% -> 3% of each run, Pallas kernels for 0% -> 8%
where the time goes in v1:
time: 676 us; the launch traced here: 675 us
  waiting for transfers between devices  357 us (53%)
  Pallas kernels  150 us (22%)
  blocking collectives  127 us (19%)
  between operations  17.9 us (3%)
  local copies, waits for them, and re-layouts  12.5 us (2%)
  other arithmetic  10.5 us (2%)
    reduce_scatter x4, waiting for transfers between devices, reduce_full(): lax.psum_scatter(grad.astype(F32), 'fsdp', scatter_dimension=0, tiled=True)  283 us
    pallas_call x3, Pallas kernels, call_plain(): pl.pallas_call(kernel, out_shape=outs, in_specs=in_vmem(len(operands)), o...  150 us
    unnamed x2, blocking collectives  122 us
    all_gather x4, waiting for transfers between devices, gather(): return lax.all_gather(value, 'fsdp', axis=0, tiled=True)  70 us
  transfers between devices with their start and end apart: 9, of which 7 were waited for; matrix products, arithmetic and copies ran while one was open for 3% of the time, Pallas kernels for 8%

profile of v1, /device:TPU:0, one launch (start us, length us, event | category | flops | bytes accessed | tf_op | source)
XLA Modules:
  0.0 675.4 jit_solution(2986344822364916067)
XLA Ops:
  8.0 0.7 all-gather.9.cloned.1.call-update
  8.7 0.7 all-gather.5.cloned.1.call-update
  10.0 1.3 fusion
  13.3 0.8 dynamic-update-slice
  14.2 0.8 dynamic-update-slice.1
  15.0 0.8 dynamic-update-slice.2
  15.8 0.8 dynamic-update-slice.3
  16.7 0.8 dynamic-update-slice.4
  17.5 0.8 dynamic-update-slice.5
  18.3 0.8 dynamic-update-slice.6
  19.2 0.8 dynamic-update-slice.7
  20.0 63.5 %all-reduce.25 = (bf16[768]{0:T(1024)(128)(2,1)S(1)}, bf16[768]{0:T(1024)(128)(2,1)S(1)}, bf16[768]{0:T(1024)(128)(2,1)S(1)}, bf16[768]{0:T(1024)(128)(2,1)S(1)}...) all-reduce(bf16[768]{0:T(1024)(128)(2,1)S(1)} %dynamic-update-slice, ...), channel_id=1, replica_groups=mesh['fsdp'=16,'dp'=2] {'fsdp'}, use_global_device_ids=true, to_apply=%add.7 | all-reduce | flops 9984 | bytes 39936
  84.6 15.3 %all-gather.9.cloned.1.call-done.w_qkv = bf16[768,2304]{1,0:T(8,128)(2,1)} async-done(((bf16[48,2304]{1,0:T(8,128)(2,1)}), bf16[768,2304]{1,0:T(8,128)(2,1)}) %all-gather.9.cloned.1.call-update) | async-done | bytes 3538960 | tf_op jit(solution)/shard_map/all_gather | solution.py:435
  99.9 54.6 %all-gather.5.cloned.1.call-done.w_in = bf16[768,3072]{1,0:T(8,128)(2,1)} async-done(((bf16[48,3072]{1,0:T(8,128)(2,1)}), bf16[768,3072]{1,0:T(8,128)(2,1)}) %all-gather.5.cloned.1.call-update) | async-done | bytes 4718608 | tf_op jit(solution)/shard_map/all_gather | solution.py:435
  154.4 53.8 %forward.1 = (bf16[1024,768]{1,0:T(8,128)(2,1)}, bf16[1024,384]{1,0:T(8,128)(2,1)}, bf16[1024,384]{1,0:T(8,128)(2,1)}, f32[1024,384]{1,0:T(8,128)}, f32[1024,384...) custom-call(bf16[1024,768]{1,0:T(8,128)(2,1)} %tok.3, ...), custom_call_target="tpu_custom_call" | custom-call | tf_op jit(solution)/shard_map/forward/pallas_call | solution.py:412
  208.4 43.3 %feed.1 = (bf16[1024,768]{1,0:T(8,128)(2,1)}, bf16[3072,768]{1,0:T(8,128)(2,1)}, bf16[768,3072]{1,0:T(8,128)(2,1)}, f32[1024,768]{1,0:T(8,128)}, bf16[1024,768]{1,0:T(8,128)(2,1)}, /*index=5*/f32[8,3072]{1,0:T(8,128)}) custom-call(bf16[1024,768]{1,0:T(8,128)(2,1)} %cot.1, f32[8,3072]{1,0:T(8,128)} %stack.46.vec, ...), custom_call_target="tpu_custom_call" | custom-call | tf_op jit(solution)/shard_map/feed/pallas_call | solution.py:412
  251.7 52.9 %back.1 = (bf16[1024,768]{1,0:T(8,128)(2,1)}, bf16[768,768]{1,0:T(8,128)(2,1)}, bf16[768,2304]{1,0:T(8,128)(2,1)}, f32[8,3072]{1,0:T(8,128)}) custom-call(bf16[1024,768]{1,0:T(8,128)(2,1)} %tok.3, s32[1,1024]{1,0:T(1,128)} %seg.3, f32[384,64]{1,0:T(8,128)} %bitcast.7, f32[1024,128]{1,0:T(8,128)} %constant.8.clone.cos, f32[1024,128]{1,0:T(8,128)} %constant.9.clone.sin, ...), custom_call_target="tpu_custom_call" | custom-call | tf_op jit(solution)/shard_map/back/pallas_call | solution.py:412
  305.3 0.7 reduce-scatter.11.cloned.1.call-update
  306.0 0.7 reduce-scatter.9.cloned.1.call-update
  306.8 54.7 %reduce-scatter.7.cloned.1.call-done = bf16[48,768]{1,0:T(8,128)(2,1)} async-done(((bf16[768,768]{1,0:T(8,128)(2,1)}), bf16[48,768]{1,0:T(8,128)(2,1)}) %reduce-scatter.7.cloned.1.call-update) | async-done | bytes 73744 | tf_op jit(solution)/shard_map/reduce_scatter | solution.py:439
  361.5 70.8 %reduce-scatter.5.cloned.1.call-done = bf16[48,2304]{1,0:T(8,128)(2,1)} async-done(((bf16[768,2304]{1,0:T(8,128)(2,1)}), bf16[48,2304]{1,0:T(8,128)(2,1)}) %reduce-scatter.5.cloned.1.call-update) | async-done | bytes 221200 | tf_op jit(solution)/shard_map/reduce_scatter | solution.py:439
  432.2 78.4 %reduce-scatter.11.cloned.1.call-done = bf16[192,768]{1,0:T(8,128)(2,1)} async-done(((bf16[3072,768]{1,0:T(8,128)(2,1)}), bf16[192,768]{1,0:T(8,128)(2,1)}) %reduce-scatter.11.cloned.1.call-update) | async-done | bytes 294928 | tf_op jit(solution)/shard_map/reduce_scatter | solution.py:439
  510.6 79.0 %reduce-scatter.9.cloned.1.call-done = bf16[48,3072]{1,0:T(8,128)(2,1)} async-done(((bf16[768,3072]{1,0:T(8,128)(2,1)}), bf16[48,3072]{1,0:T(8,128)(2,1)}) %reduce-scatter.9.cloned.1.call-update) | async-done | bytes 294928 | tf_op jit(solution)/shard_map/reduce_scatter | solution.py:439
  591.6 0.9 slice.45
  592.5 0.8 slice_reduce_fusion.5
  593.3 0.8 slice_reduce_fusion
  594.2 0.9 slice_reduce_fusion.1
  595.1 58.3 %all-reduce.24 = (bf16[768]{0:T(1024)(128)(2,1)S(1)}, bf16[768]{0:T(1024)(128)(2,1)S(1)}, bf16[1536]{0:T(1024)(128)(2,1)S(1)}, bf16[768]{0:T(1024)(128)(2,1)S(1)...) all-reduce(f32[768]{0:T(1024)S(1)} %get-tuple-element.69, ...), channel_id=2, replica_groups=mesh['fsdp'=16,'dp'=2] {'fsdp'}, use_global_device_ids=true, to_apply=%region_0.1.clone | all-reduce | flops 9984 | bytes 59904
  654.0 5.0 all-reduce.26
  663.7 1.9 convert_element_type.129
  665.6 1.8 convert_element_type.134
  667.4 0.8 convert_element_type.113
  (65 shorter events, 9.2 us)
Async XLA Ops:
  7.2 77.4 %all-gather.11.cloned.1.call-start = ((), (), s32[]{:S(2)}) async-start(), calls=%async_computation.7 | async-start | bytes 1253376 | tf_op jit(solution)/shard_map/all_gather | solution.py:435
  7.9 92.0 %all-gather.9.cloned.1.call-start = ((), (), s32[]{:S(2)}) async-start(), calls=%async_computation.6 | async-start | bytes 3760128 | tf_op jit(solution)/shard_map/all_gather | solution.py:435
  8.7 145.8 %all-gather.5.cloned.1.call-start = ((), (), s32[]{:S(2)}) async-start(), calls=%async_computation.4 | async-start | bytes 5013504 | tf_op jit(solution)/shard_map/all_gather | solution.py:435
  9.4 199.0 %all-gather.7.cloned.1.call-start = ((), (), s32[]{:S(2)}) async-start(), calls=%async_computation.5 | async-start | bytes 5013504 | tf_op jit(solution)/shard_map/all_gather | solution.py:435
  10.0 351.5 %reduce-scatter.7.cloned.1.call-start = ((), (), s32[]{:S(2)}) async-start(), calls=%async_computation.9 | async-start | bytes 1253376 | tf_op jit(solution)/shard_map/reduce_scatter | solution.py:439
  304.6 127.6 %reduce-scatter.5.cloned.1.call-start = ((), (), s32[]{:S(2)}) async-start(), calls=%async_computation.8 | async-start | bytes 3760128 | tf_op jit(solution)/shard_map/reduce_scatter | solution.py:439
  305.2 205.4 %reduce-scatter.11.cloned.1.call-start = ((), (), s32[]{:S(2)}) async-start(), calls=%async_computation.11 | async-start | bytes 5013504 | tf_op jit(solution)/shard_map/reduce_scatter | solution.py:439
  306.0 283.7 %reduce-scatter.9.cloned.1.call-start = ((), (), s32[]{:S(2)}) async-start(), calls=%async_computation.10 | async-start | bytes 5013504 | tf_op jit(solution)/shard_map/reduce_scatter | solution.py:439
  306.7 357.0 %all-reduce.30.cloned.1.call-start = ((), (), s32[]{:S(2)}) async-start(), calls=%async_computation.12 | async-start | bytes 1769472 | tf_op jit(solution)/shard_map/psum | solution.py:440
  663.7 3.7 copy-start
  663.7 4.5 copy-start.1
Sparse Core Ops, SparseCore 0:
  10.3 41.1 all-gather.10
  53.8 46.0 all-gather.8
  102.2 52.2 all-gather.4
  156.6 51.7 all-gather.6
  304.8 56.6 reduce-scatter.6
  365.2 66.9 reduce-scatter.4
  436.1 74.4 reduce-scatter.10
  514.9 74.6 reduce-scatter.8
  592.1 36.0 all-reduce.29

commit v2 on v1

v2 whole, which is shorter than its diff:
```python
import functools

import jax
import jax.numpy as jnp
import numpy as np
from jax import lax
from jax.experimental import pallas as pl
from jax.experimental.pallas import tpu as pltpu
from jax.sharding import PartitionSpec as P

HEADS = 12
HEAD_DIM = 64
FEATS = 32
SEGS = 16
PACK = 4
GROUPS = HEADS // PACK
WIDE = PACK * HEAD_DIM
SLIM = PACK * FEATS
STATE = SEGS * SLIM
EPSILON = 1e-05
F32 = jnp.float32
BF16 = jnp.bfloat16
VMEM_LIMIT = 67_000_000

GAIN1, SHIFT1, BIAS_OUT, GAIN2, SHIFT2, BIAS_FFO, BIAS_QKV, BIAS_IN = range(8)
QUERY_KEY, VALUE = 8, 9


def contract(left, right, left_dim, right_dim):
    return lax.dot_general(
        left, right, (((left_dim,), (right_dim,)), ((), ())), preferred_element_type=F32
    )


def nn(left, right):
    return contract(left, right, 1, 0)


def nt(left, right):
    return contract(left, right, 1, 1)


def tn(left, right):
    return contract(left, right, 0, 0)


def tile(index, size):
    return pl.ds(pl.multiple_of(index * size, size), size)


def iota(shape, dim):
    return lax.broadcasted_iota(jnp.int32, shape, dim)


def split_two(values):
    high = values.astype(BF16)
    return high, (values - high.astype(F32)).astype(BF16)


def normalize(rows):
    centred = rows - jnp.mean(rows, axis=-1, keepdims=True)
    inv_std = lax.rsqrt(jnp.mean(centred * centred, axis=-1, keepdims=True) + EPSILON)
    return centred * inv_std, inv_std


def normalize_back(incoming, normed, inv_std, gain):
    scaled = incoming * gain
    mean_one = jnp.mean(scaled, axis=-1, keepdims=True)
    mean_two = jnp.mean(scaled * normed, axis=-1, keepdims=True)
    return inv_std * (scaled - mean_one - normed * mean_two)


def column_sum(values):
    return jnp.sum(values, axis=0, keepdims=True)


def head_blocks(rows, columns, row_width, column_width):
    return (iota((rows, columns), 0) // row_width) == (iota((rows, columns), 1) // column_width)


def ones_where(mask):
    return jnp.where(mask, 1.0, 0.0).astype(BF16)


def projection_blocks(proj_ref, group):
    small = proj_ref[tile(group, SLIM), :].astype(BF16)
    source, lane = iota((HEAD_DIM, WIDE), 0), iota((HEAD_DIM, WIDE), 1) % HEAD_DIM
    half = HEAD_DIM // 2
    plain = jnp.where(source == lane, 1.0, 0.0)
    turned = jnp.where(source == (lane + half) % HEAD_DIM, jnp.where(lane < half, 1.0, -1.0), 0.0)
    keep = head_blocks(SLIM, WIDE, FEATS, HEAD_DIM)
    return (
        jnp.where(keep, nn(small, plain.astype(BF16)), 0.0).astype(BF16),
        jnp.where(keep, nn(small, turned.astype(BF16)), 0.0).astype(BF16),
    )


def segment_masks(seg_ref, one_ref, mexp_ref):
    length = seg_ref.shape[1]
    one_ref[...] = ones_where(iota((SEGS, length), 0) == seg_ref[...])
    expand = ones_where(head_blocks(SEGS, STATE, 1, SLIM))

    @pl.loop(0, length // 256)
    def _(r):
        mexp_ref[tile(r, 256), :] = tn(one_ref[:, tile(r, 256)], expand).astype(BF16)


def denominators(fq, one_rows, total):
    high, low = split_two(total)
    total_rows = tn(one_rows, high) + tn(one_rows, low)
    absent = 1.0 - tn(one_rows, jnp.ones((SEGS, WIDE), BF16))
    products = (fq.astype(F32) * total_rows).astype(BF16)
    wide = nn(products, ones_where(head_blocks(SLIM, WIDE, FEATS, HEAD_DIM))) + absent
    slim = nn(products, ones_where(head_blocks(SLIM, SLIM, FEATS, FEATS))) + absent[:, :SLIM]
    return total_rows, wide, slim, absent


def spread(features, masks):
    return jnp.concatenate([features] * SEGS, axis=1) * masks


def segment_states(feature_ref, one_ref, value, group, out_ref, base):
    turned = feature_ref[:, tile(group, SLIM)].astype(F32).T.astype(BF16)
    keep = head_blocks(SLIM, WIDE, FEATS, HEAD_DIM)
    chunk = 8
    for part in range(SEGS // chunk):
        left = jnp.concatenate(
            [turned * one_ref[s : s + 1, :] for s in range(part * chunk, (part + 1) * chunk)], axis=0
        )
        sums = nn(left, value)
        for s in range(chunk):
            piece = jnp.where(keep, sums[s * SLIM : (s + 1) * SLIM], 0.0).astype(BF16)
            row = base + (part * chunk + s) * SLIM
            out_ref[pl.ds(pl.multiple_of(row, SLIM), SLIM), :] = piece


def masked_sum(products, masks):
    out = products[:, :SLIM] * masks[:, :SLIM].astype(F32)
    for s in range(1, SEGS):
        span = slice(s * SLIM, (s + 1) * SLIM)
        out = out + products[:, span] * masks[:, span].astype(F32)
    return out


def twice(table):
    return jnp.concatenate([table, table], axis=1)


class Poll:
    def __init__(self, *plan):
        self.plan = plan


def checkpoint(poll, index=0, stride=1, base=0, inner=0, count=1):
    if poll is None:
        return
    now = index * stride + base + inner
    for number, steps in enumerate(poll.plan):
        if not steps or not base <= number % stride < base + count:
            continue

        @pl.when(now == number)
        def _(steps=steps):
            for step in steps:
                step()


def phase_normalize(tok_ref, normed_ref):
    @pl.loop(0, tok_ref.shape[0] // 256)
    def _(r):
        normed_ref[tile(r, 256), :] = normalize(tok_ref[tile(r, 256), :].astype(F32))[0]


def phase_norm_one(normed_ref, vec_ref, h1_ref, hbar_ref):
    length, width = normed_ref.shape
    hbar_ref[...] = jnp.zeros_like(hbar_ref)

    @pl.loop(0, length // 256)
    def _(r):
        normed = normed_ref[tile(r, 256), :]
        rows = normed * vec_ref[GAIN1 : GAIN1 + 1, :width] + vec_ref[SHIFT1 : SHIFT1 + 1, :width]
        h1_ref[tile(r, 256), :] = rows.astype(BF16)
        hbar_ref[0:1, :] += column_sum(rows) * (1.0 / length)


def phase_attention(
    h1_ref, hbar_ref, w_qkv_ref, vec_ref, proj_ref, cos_ref, sin_ref, one_ref, mexp_ref,
    fq_ref, fk_ref, sq_ref, sk_ref, v_ref, state_ref, total_ref, att_ref, attc_ref, poll=None,
):
    length, width = h1_ref.shape

    @pl.loop(0, GROUPS)
    def _(g):
        cols, feats = tile(g, WIDE), tile(g, SLIM)
        plain, turned = projection_blocks(proj_ref, g)
        for kind, (feat_ref, slope_ref) in enumerate(((fq_ref, sq_ref), (fk_ref, sk_ref))):
            span = pl.ds(pl.multiple_of(kind * width + g * WIDE, WIDE), WIDE)
            weight = w_qkv_ref.at[g, :, pl.ds(kind * WIDE, WIDE)]

            @pl.loop(0, length // 512)
            def _(r):
                rows = tile(r, 512)
                x = nn(h1_ref[rows, :], weight[...]) + vec_ref[BIAS_QKV : BIAS_QKV + 1, span]
                u = nt((x * twice(cos_ref[rows, :])).astype(BF16), plain) + nt(
                    (x * twice(sin_ref[rows, :])).astype(BF16), turned
                )
                small = jnp.exp(-jnp.abs(u))
                feat_ref[rows, feats] = (jnp.maximum(u, 0.0) + jnp.log1p(small)).astype(BF16)
                slope_ref[rows, feats] = jnp.where(u >= 0.0, 1.0, small) / (1.0 + small)

            checkpoint(poll, g, 5, kind)

        span = pl.ds(pl.multiple_of(2 * width + g * WIDE, WIDE), WIDE)
        weight = w_qkv_ref.at[g, :, pl.ds(2 * WIDE, WIDE)]
        shared = nn(hbar_ref[...].astype(BF16), weight[...])[0:1]

        @pl.loop(0, length // 512)
        def _(r):
            rows = tile(r, 512)
            v_ref[rows, cols] = (nn(h1_ref[rows, :], weight[...]) - shared).astype(BF16)

        checkpoint(poll, g, 5, 2)
        shared = shared + vec_ref[BIAS_QKV : BIAS_QKV + 1, span]

        segment_states(fk_ref, one_ref, v_ref[:, cols], g, state_ref, g * STATE)
        total_ref[:, feats] = nn(one_ref[...], fk_ref[:, feats])
        checkpoint(poll, g, 5, 3)

        @pl.loop(0, length // 256)
        def _(r):
            rows = tile(r, 256)
            fq = fq_ref[rows, feats]
            numerator = nn(spread(fq, mexp_ref[rows, :]), state_ref[tile(g, STATE), :])
            _rows, wide, _slim, absent = denominators(fq, one_ref[:, rows], total_ref[:, feats])
            centred = numerator / wide
            attc_ref[rows, cols] = centred.astype(BF16)
            att_ref[rows, cols] = (centred + (1.0 - absent) * shared).astype(BF16)

        checkpoint(poll, g, 5, 4)


def phase_middle(tok_ref, att_ref, w_out_ref, vec_ref, mid_ref, h2_ref):
    length, width = tok_ref.shape

    @pl.loop(0, length // 512)
    def _(r):
        rows = tile(r, 512)
        middle = (
            tok_ref[rows, :].astype(F32)
            + nn(att_ref[rows, :], w_out_ref[...])
            + vec_ref[BIAS_OUT : BIAS_OUT + 1, :width]
        )
        mid_ref[rows, :] = middle
        normed, _inv = normalize(middle)
        hidden = normed * vec_ref[GAIN2 : GAIN2 + 1, :width] + vec_ref[SHIFT2 : SHIFT2 + 1, :width]
        h2_ref[rows, :] = hidden.astype(BF16)


def phase_gelu(h2_ref, w_in_ref, vec_ref, act_ref, slope_ref, first=0, last=None, poll=None):
    last = w_in_ref.shape[1] // 256 if last is None else last

    @pl.loop(first, last)
    def _(j):
        cols = tile(j, 256)
        pre = nn(h2_ref[...], w_in_ref[:, cols]) + vec_ref[BIAS_IN : BIAS_IN + 1, cols]
        gate = 0.5 * (1.0 + lax.erf(pre * 0.7071067811865476))
        act_ref[:, cols] = (pre * gate).astype(BF16)
        slope = gate + pre * jnp.exp(-0.5 * pre * pre) * 0.3989422804014327
        slope_ref[:, cols] = slope.astype(BF16)
        checkpoint(poll, j, 1)


def phase_output(mid_ref, act_ref, w_ffo_ref, vec_ref, out_ref, poll=None):
    length, width = mid_ref.shape

    @pl.loop(0, length // 256)
    def _(r):
        rows = tile(r, 256)
        total = mid_ref[rows, :] + nn(act_ref[rows, :], w_ffo_ref[...])
        out_ref[rows, :] = (total + vec_ref[BIAS_FFO : BIAS_FFO + 1, :width]).astype(BF16)
        checkpoint(poll, r, 1)


def phase_grad_pre(cot_ref, w_ffo_ref, slope_ref, gpre_ref, small_ref, poll=None):
    @pl.loop(0, w_ffo_ref.shape[0] // 256)
    def _(j):
        cols = tile(j, 256)
        grad = nt(cot_ref[...], w_ffo_ref[cols, :]) * slope_ref[:, cols].astype(F32)
        grad = grad.astype(BF16)
        gpre_ref[:, cols] = grad
        small_ref[BIAS_IN : BIAS_IN + 1, cols] = column_sum(grad.astype(F32))
        checkpoint(poll, j, 1)


def phase_weight_grad(left_ref, right_ref, out_ref, poll=None):
    chunk, tall = min(768, right_ref.shape[1]), 384

    @pl.loop(0, right_ref.shape[1] // chunk)
    def _(j):
        cols = tile(j, chunk)

        @pl.loop(0, left_ref.shape[1] // tall)
        def _(i):
            rows = tile(i, tall)
            out_ref[rows, cols] = tn(left_ref[:, rows], right_ref[:, cols]).astype(BF16)
            checkpoint(poll, j * (left_ref.shape[1] // tall) + i)


def phase_norm_two_back(
    gpre_ref, w_in_ref, mid_ref, cot_ref, vec_ref, gmid_ref, gbr_ref, small_ref, poll=None
):
    length, width = mid_ref.shape
    small_ref[GAIN2 : SHIFT2 + 1, :width] = jnp.zeros((2, width), F32)
    small_ref[BIAS_FFO : BIAS_FFO + 1, :width] = jnp.zeros((1, width), F32)
    small_ref[BIAS_OUT : BIAS_OUT + 1, :width] = jnp.zeros((1, width), F32)

    @pl.loop(0, length // 512)
    def _(r):
        rows = tile(r, 512)
        incoming = nt(gpre_ref[rows, :], w_in_ref[...])
        normed, inv_std = normalize(mid_ref[rows, :])
        upstream = cot_ref[rows, :].astype(F32)
        grad = upstream + normalize_back(incoming, normed, inv_std, vec_ref[GAIN2 : GAIN2 + 1, :width])
        gmid_ref[rows, :] = grad
        branch = grad.astype(BF16)
        gbr_ref[rows, :] = branch
        small_ref[GAIN2 : GAIN2 + 1, :width] += column_sum(incoming * normed)
        small_ref[SHIFT2 : SHIFT2 + 1, :width] += column_sum(incoming)
        small_ref[BIAS_FFO : BIAS_FFO + 1, :width] += column_sum(upstream)
        small_ref[BIAS_OUT : BIAS_OUT + 1, :width] += column_sum(branch.astype(F32))
        checkpoint(poll, r, 1)


def phase_attention_back(
    gbr_ref, w_out_ref, attc_ref, proj_ref, cos_ref, sin_ref, one_ref, mexp_ref,
    fq_ref, fk_ref, sq_ref, sk_ref, v_ref, state_ref, total_ref,
    dnum_ref, dstate_ref, dtotal_ref, gproj_ref, small_ref, h1_ref, g_qkv_ref, poll=None,
):
    length, width = gbr_ref.shape

    @pl.loop(0, GROUPS)
    def _(g):
        cols, feats = tile(g, WIDE), tile(g, SLIM)
        q_span = cols
        k_span = pl.ds(pl.multiple_of(width + g * WIDE, WIDE), WIDE)
        v_span = pl.ds(pl.multiple_of(2 * width + g * WIDE, WIDE), WIDE)
        plain, turned = projection_blocks(proj_ref, g)
        q_place, k_place, v_place = (tile(3 * g + kind, WIDE) for kind in range(3))
        dtotal_ref[...] = jnp.zeros_like(dtotal_ref)
        for span in (q_span, k_span, v_span):
            small_ref[BIAS_QKV : BIAS_QKV + 1, span] = jnp.zeros((1, WIDE), F32)

        def unrotate(grad, rows, span, place):
            high, low = split_two(grad)
            back = (nn(high, plain) + nn(low, plain)) * twice(cos_ref[rows, :])
            back = back + (nn(high, turned) + nn(low, turned)) * twice(sin_ref[rows, :])
            back = back.astype(BF16)
            gproj_ref[rows, place] = back
            small_ref[BIAS_QKV : BIAS_QKV + 1, span] += column_sum(back.astype(F32))

        @pl.loop(0, length // 256)
        def _(r):
            rows = tile(r, 256)
            grad_att = nt(gbr_ref[rows, :], w_out_ref[cols, :])
            fq = fq_ref[rows, feats]
            total_rows, wide, slim, _absent = denominators(fq, one_ref[:, rows], total_ref[:, feats])
            dnum = (grad_att / wide).astype(BF16)
            dnum_ref[rows, :] = dnum
            dots = nn(
                (dnum.astype(F32) * attc_ref[rows, cols].astype(F32)).astype(BF16),
                ones_where(head_blocks(WIDE, SLIM, HEAD_DIM, FEATS)),
            )
            dden = -dots
            dfq = masked_sum(nt(dnum, state_ref[tile(g, STATE), :]), mexp_ref[rows, :])
            dfq = dfq + dden * total_rows
            dtotal_ref[...] += nn(one_ref[:, rows], (dden * fq.astype(F32)).astype(BF16))
            unrotate(dfq * sq_ref[rows, feats], rows, q_span, q_place)
            checkpoint(poll, g, 10, 0, r, 4)

        segment_states(fq_ref, one_ref, dnum_ref[...], g, dstate_ref, 0)

        @pl.loop(0, length // 256)
        def _(r):
            rows = tile(r, 256)
            dv = nn(spread(fk_ref[rows, feats], mexp_ref[rows, :]), dstate_ref[...]).astype(BF16)
            gproj_ref[rows, v_place] = dv
            small_ref[BIAS_QKV : BIAS_QKV + 1, v_span] += column_sum(dv.astype(F32))
            high, low = split_two(dtotal_ref[...])
            one_rows = one_ref[:, rows]
            dfk = masked_sum(nt(v_ref[rows, cols], dstate_ref[...]), mexp_ref[rows, :])
            dfk = dfk + tn(one_rows, high) + tn(one_rows, low)
            unrotate(dfk * sk_ref[rows, feats], rows, k_span, k_place)
            checkpoint(poll, g, 10, 4, r, 4)

        @pl.loop(0, width // 384)
        def _(i):
            rows = tile(i, 384)
            g_qkv_ref[g, rows, :] = tn(h1_ref[:, rows], gproj_ref[:, tile(g, 3 * WIDE)]).astype(BF16)
            checkpoint(poll, g, 10, 8, i, 2)


def phase_norm_one_back(
    gproj_ref, w_qkv_ref, tok_ref, gmid_ref, vec_ref, tgrad_ref, small_ref, poll=None
):
    length, width = tok_ref.shape
    small_ref[GAIN1 : SHIFT1 + 1, :width] = jnp.zeros((2, width), F32)

    @pl.loop(0, length // 256)
    def _(r):
        rows = tile(r, 256)
        incoming = jnp.zeros((256, width), F32)
        for group in range(GROUPS):
            incoming += nt(gproj_ref[rows, tile(group, 3 * WIDE)], w_qkv_ref[group])
        normed, inv_std = normalize(tok_ref[rows, :].astype(F32))
        back = normalize_back(incoming, normed, inv_std, vec_ref[GAIN1 : GAIN1 + 1, :width])
        tgrad_ref[rows, :] = (gmid_ref[rows, :] + back).astype(BF16)
        small_ref[GAIN1 : GAIN1 + 1, :width] += column_sum(incoming * normed)
        small_ref[SHIFT1 : SHIFT1 + 1, :width] += column_sum(incoming)
        checkpoint(poll, r, 1)


MESH = pl.DeviceIdType.MESH
ORDER = [(d, xr) for xr in (1, 0) for d in (3, 2, 1, 0)]


class Place:
    def __init__(self, depth):
        f, self.y = lax.axis_index("fsdp"), lax.axis_index("dp")
        self.depth = depth
        self.z, self.x, self.c = f // 4, (f // 2) % 2, f % 2

    def index(self, d=0, xr=0, cr=0):
        c = 1 - self.c if cr else self.c
        x = 1 - self.x if xr else self.x
        return ((self.z + d) % self.depth) * 4 + x * 2 + c

    def device(self, d=0, xr=0, cr=0, yr=0):
        return (self.index(d, xr, cr), 1 - self.y if yr else self.y)

    def partners(self):
        far = [self.device(d=d) for d in range(1, self.depth)]
        return far + [self.device(xr=1), self.device(cr=1), self.device(yr=1)]

    def greet(self):
        barrier = pltpu.get_barrier_semaphore()
        partners = self.partners()
        for partner in partners:
            pl.semaphore_signal(barrier, inc=1, device_id=partner, device_id_type=MESH)
        pl.semaphore_wait(barrier, len(partners))


class Region:
    def __init__(self, place, ref, stride, base=0, rows=None, columns=None):
        self.ref, self.stride, self.base, self.rows = ref, stride, base, stride if rows is None else rows
        start, size = (0, ref.shape[1]) if columns is None else columns
        self.columns, self.width = slice(start, start + size), size
        self.third = third = self.rows // 3
        self.all = (0, self.rows)
        self.moved = (place.y * third, 2 * third)
        self.mine, self.other = (place.y * 2 * third, third), ((1 - place.y) * 2 * third, third)
        self.common = (third, third)

    def where(self, index, span):
        start, size = span
        return pl.ds(pl.multiple_of(index * self.stride + self.base + start, 16), size), self.columns

    def at(self, index, span):
        return self.ref.at[self.where(index, span)]

    def bulk(self, thirds):
        return self.ref.at[pl.ds(0, thirds * self.third), self.columns]


def remote(src, dst, send, recv, device):
    return pltpu.make_async_remote_copy(
        src_ref=src, dst_ref=dst, send_sem=send, recv_sem=recv, device_id=device, device_id_type=MESH
    )


class Gather:
    def __init__(self, place, full, sems, pieces):
        self.place, self.full, self.sems, self.pieces = place, full, sems, pieces
        depth = place.depth
        self.z, self.x, self.y = 0, depth, 2 * depth
        self.sibling, self.sent, self.own = 4 * depth, 4 * depth + 1, 4 * depth + 2

    @staticmethod
    def count(depth):
        return 4 * depth + 3

    def copy(self, index, span, slot, device):
        ref = self.full.at(index, span)
        return remote(ref, ref, self.sems.at[self.sent], self.sems.at[slot], device)

    def fetch(self):
        for src, dst in self.pieces:
            pltpu.make_async_copy(src, dst, self.sems.at[self.own]).start()

    def start(self):
        place, full = self.place, self.full
        mine = full.at(place.index(), full.all)
        pltpu.make_async_copy(mine, mine, self.sems.at[self.own]).wait()
        for d in (2, 1, 3):
            self.copy(place.index(), full.moved, self.z + d, place.device(d=d)).start()
        self.copy(place.index(), full.moved, self.x, place.device(xr=1)).start()
        self.copy(place.index(), full.all, self.sibling, place.device(cr=1)).start()

    def z_step(self, d):
        place, full = self.place, self.full
        index = place.index(d=place.depth - d)
        self.copy(index, full.moved, self.z + d, place.device()).wait_recv()
        self.copy(index, full.moved, self.x + d, place.device(xr=1)).start()
        self.copy(index, full.mine, self.y + 2 * d, place.device(yr=1)).start()
        self.copy(index, full.moved, self.sibling, place.device(cr=1)).start()

    def x_step(self, d):
        place, full = self.place, self.full
        index = place.index(d=place.depth - d, xr=1)
        self.copy(index, full.moved, self.x + d, place.device()).wait_recv()
        self.copy(index, full.mine, self.y + 2 * d + 1, place.device(yr=1)).start()
        self.copy(index, full.moved, self.sibling, place.device(cr=1)).start()

    def y_step(self, d, xr):
        place, full = self.place, self.full
        index = place.index(d=place.depth - d, xr=xr)
        self.copy(index, full.other, self.y + 2 * d + xr, place.device()).wait_recv()
        self.copy(index, full.other, self.sibling, place.device(cr=1)).start()

    def done(self):
        half = self.full.bulk(6 * self.place.depth)
        pltpu.make_async_copy(half, half, self.sems.at[self.sibling]).wait()

    def drain(self):
        depth = self.place.depth
        sent = self.full.bulk(2 * (depth - 1) + 2 + 3 + 5 * (depth - 1) + 3 * depth + 2 * depth - 1)
        pltpu.make_async_copy(sent, sent, self.sems.at[self.sent]).wait()

    def stages(self):
        depth = self.place.depth
        return (
            [functools.partial(self.z_step, d) for d in (1, 3, 2)],
            [functools.partial(self.x_step, d) for d in (0, 1, 3, 2)],
            [functools.partial(self.y_step, d, 0) for d in (1, 3, 2)]
            + [functools.partial(self.y_step, d, 1) for d in (0, 1, 3, 2)],
            [self.done],
        )


class Reduce:
    def __init__(self, place, full, bufs, sems, emit, source=None):
        self.place, self.full, self.sems, self.emit = place, full, sems, emit
        self.source = full if source is None else source
        depth = place.depth
        self.c_buf, self.y_buf, self.x_buf, self.z_buf, self.f_send, self.f_recv = bufs
        self.c, self.y, self.x, self.z = 0, 2 * depth, 4 * depth, 5 * depth
        self.f, self.sent = 6 * depth, 6 * depth + 1

    @staticmethod
    def count(depth):
        return 6 * depth + 2

    @staticmethod
    def buffers(depth, rows, columns):
        third = rows // 3
        return [
            pltpu.VMEM((2 * depth, rows, columns), BF16),
            pltpu.VMEM((2 * depth, third, columns), BF16),
            pltpu.VMEM((depth, 2 * third, columns), BF16),
            pltpu.VMEM((depth - 1, 2 * third, columns), BF16),
            pltpu.VMEM((rows, columns), BF16),
            pltpu.VMEM((rows, columns), BF16),
        ]

    def copy(self, src, dst, slot, device):
        return remote(src, dst, self.sems.at[self.sent], self.sems.at[slot], device)

    def c_copy(self, d, xr):
        slot = 2 * d + xr
        src = self.source.at(self.place.index(d, xr, 1), self.full.all)
        return self.copy(src, self.c_buf.at[slot], self.c + slot, self.place.device(cr=1))

    def y_copy(self, d, xr):
        slot = 2 * d + xr
        src = self.full.at(self.place.index(d, xr), self.full.other)
        return self.copy(src, self.y_buf.at[slot], self.y + slot, self.place.device(yr=1))

    def x_copy(self, d):
        src = self.full.at(self.place.index(d, 1), self.full.moved)
        return self.copy(src, self.x_buf.at[d], self.x + d, self.place.device(xr=1))

    def z_copy(self, d):
        src = self.full.at(self.place.index(d), self.full.moved)
        return self.copy(src, self.z_buf.at[d - 1], self.z + d, self.place.device(d=d))

    def f_rows(self, span):
        start, size = span
        return pl.ds(start if isinstance(start, int) else pl.multiple_of(start, 16), size)

    def f_copy(self):
        rows = self.f_rows(self.full.moved)
        return self.copy(self.f_send.at[rows], self.f_recv.at[rows], self.f, self.place.device(yr=1))

    def add(self, where, values):
        self.full.ref[where] = self.full.ref[where] + values

    def c_send(self, d, xr):
        self.c_copy(d, xr).start()

    def c_step(self, d, xr):
        self.c_copy(d, xr).wait_recv()
        self.add(self.full.where(self.place.index(d, xr), self.full.all), self.c_buf[2 * d + xr])
        self.y_copy(d, xr).start()

    def y_step(self, d, xr):
        self.y_copy(d, xr).wait_recv()
        self.add(self.full.where(self.place.index(d, xr), self.full.mine), self.y_buf[2 * d + xr])
        if xr:
            self.x_copy(d).start()

    def x_step(self, d):
        self.x_copy(d).wait_recv()
        self.add(self.full.where(self.place.index(d), self.full.moved), self.x_buf[d])
        if d:
            self.z_copy(d).start()

    def z_step(self):
        total = self.full.ref[self.full.where(self.place.index(), self.full.moved)].astype(F32)
        for d in range(1, self.place.depth):
            self.z_copy(d).wait_recv()
            total = total + self.z_buf[d - 1].astype(F32)
        self.f_send[self.f_rows(self.full.moved), :] = total.astype(BF16)
        self.f_copy().start()

    def f_step(self):
        self.f_copy().wait_recv()
        mine, other, common = (self.f_rows(x) for x in (self.full.mine, self.full.other, self.full.common))
        self.emit(self.full.mine, self.f_send[mine, :].astype(F32))
        self.emit(self.full.other, self.f_recv[other, :].astype(F32))
        self.emit(self.full.common, self.f_send[common, :].astype(F32) + self.f_recv[common, :].astype(F32))

    def drain(self):
        sent = self.full.bulk(12 * self.place.depth)
        pltpu.make_async_copy(sent, sent, self.sems.at[self.sent]).wait()

    def sends(self):
        return [functools.partial(self.c_send, d, xr) for d, xr in ORDER]

    def stages(self):
        depth = self.place.depth
        return (
            [functools.partial(self.c_step, d, xr) for d, xr in ORDER],
            [functools.partial(self.y_step, d, xr) for d, xr in ORDER],
            [functools.partial(self.x_step, d) for d in range(depth - 1, -1, -1)],
            [self.z_step],
            [self.f_step],
        )


def wave(units, slots=None):
    stages = [unit.stages() for unit in units]
    depth = len(stages[0])
    out = []
    for slot in range(len(units) + depth - 1):
        steps = []
        for number in range(depth - 1, -1, -1):
            if 0 <= slot - number < len(units):
                steps += stages[slot - number][number]
        out.append(steps)
    return out


def spread_steps(steps, checkpoints, start=0):
    plan = [[] for _ in range(checkpoints)]
    span = checkpoints - start
    for number, step in enumerate(steps):
        plan[start + number * span // len(steps)].append(step)
    return plan


def run(steps):
    for step in steps:
        step()


SMALL_ROWS, SMALL_COLUMNS = 48, 256
SMALL_LAYOUT = (
    (GAIN1, 1, 0, 0), (SHIFT1, 1, 0, 1), (BIAS_OUT, 1, 0, 2), (GAIN2, 1, 0, 3), (SHIFT2, 1, 0, 4),
    (BIAS_QKV, 3, 1, 0), (BIAS_FFO, 1, 1, 3), (BIAS_IN, 4, 2, 0),
)


GRAD_LAYOUT = tuple((name, 0, many, third, place) for name, many, third, place in SMALL_LAYOUT if name != BIAS_QKV)
GRAD_LAYOUT += ((QUERY_KEY, 0, 2, 1, 0), (VALUE, 2, 1, 1, 2))


def small_block(vectors):
    rows = []
    for third in range(3):
        parts = [vectors[name] for name, _m, row, _p in SMALL_LAYOUT if row == third]
        flat = jnp.concatenate(parts)
        rows.append(jnp.pad(flat, (0, SMALL_COLUMNS - flat.shape[0])))
    return jnp.pad(jnp.stack(rows)[:, None, :], ((0, 0), (0, 15), (0, 0))).reshape(SMALL_ROWS, SMALL_COLUMNS)


def selector(unit, many, offset, groups):
    size = unit * many
    lane = iota((SMALL_COLUMNS, size * groups), 1) % size
    return ones_where(iota((SMALL_COLUMNS, size * groups), 0) == lane + offset * unit)


def owner_mask(size, groups):
    return iota((groups, size * groups), 0) == iota((groups, size * groups), 1) // size


def unpack_small(gathered_ref, vec_ref, groups, unit):
    blocks = gathered_ref[...].astype(F32).reshape(groups, SMALL_ROWS, SMALL_COLUMNS)
    thirds = [jnp.sum(blocks[:, 16 * k : 16 * k + 16], axis=1).astype(BF16) for k in range(3)]
    for name, many, third, offset in SMALL_LAYOUT:
        size = unit * many
        laid = nn(thirds[third], selector(unit, many, offset, groups))
        vec_ref[name : name + 1, : size * groups] = column_sum(jnp.where(owner_mask(size, groups), laid, 0.0))


def pack_small(small_ref, out_ref, groups, unit):
    thirds = [jnp.zeros((groups, SMALL_COLUMNS), F32) for _ in range(3)]
    for name, start, many, third, offset in GRAD_LAYOUT:
        size, row = unit * many, name if name < QUERY_KEY else BIAS_QKV
        row = small_ref[row : row + 1, start * unit * groups : (start + many) * unit * groups]
        spaced = jnp.where(owner_mask(size, groups), row, 0.0).astype(BF16)
        thirds[third] = thirds[third] + nt(spaced, selector(unit, many, offset, groups))
    first = iota((groups, 16, SMALL_COLUMNS), 1) == 0
    laid = [jnp.where(first, part[:, None, :], 0.0) for part in thirds]
    out_ref[...] = jnp.concatenate(laid, axis=1).reshape(groups * SMALL_ROWS, SMALL_COLUMNS).astype(BF16)


class Names:
    def __getattr__(self, name):
        return name


N = Names()
GIVEN, LOAD, FAR, MADE, SPILL, SCRATCH = range(6)


class Arrays:
    def __init__(self, spec, refs, sems):
        self.hbm, self.spec, self.sems, self.open = {}, spec, sems, []
        self.slots = {name: n for n, name in enumerate(x for x in spec if spec[x][0] in (LOAD, SPILL))}
        for name, ref in refs.items():
            setattr(self, name, ref)

    def copy(self, name):
        hbm, vmem, sem = self.hbm[name], getattr(self, name), self.sems.at[self.slots[name]]
        if self.spec[name][0] == LOAD:
            return pltpu.make_async_copy(hbm, vmem, sem)
        return pltpu.make_async_copy(vmem, hbm, sem)

    def load(self, *names):
        for name in names:
            self.copy(name).start()

    def ready(self, *names):
        for name in names:
            self.copy(name).wait()

    def spill(self, *names):
        for name in names:
            self.copy(name).start()
            self.open.append(name)

    def close(self):
        self.ready(*self.open)


def call(name, body, spec, operands, collective_id=None, flops=0):
    ins = [n for n in spec if spec[n][0] in (GIVEN, LOAD, FAR)]
    outs = [n for n in spec if spec[n][0] in (MADE, SPILL)]
    moved = [n for n in spec if spec[n][0] in (LOAD, SPILL)]
    tmps = [n for n in spec if spec[n][0] == SCRATCH]
    scratch = [pltpu.VMEM(spec[n][1], spec[n][2]) for n in moved] + [spec[n][1] for n in tmps]
    scratch.append(pltpu.SemaphoreType.DMA((max(1, len(moved)),)))

    def kernel(*refs):
        given, made, inner = refs[: len(ins)], refs[len(ins) : len(ins) + len(outs)], refs[len(ins) + len(outs) :]
        arrays = Arrays(spec, dict(zip(moved + tmps, inner)), inner[-1])
        for names, group in ((ins, given), (outs, made)):
            for n, ref in zip(names, group):
                if n in moved:
                    arrays.hbm[n] = ref
                else:
                    setattr(arrays, n, ref)
        body(arrays)
        arrays.close()

    vmem, anywhere = pl.BlockSpec(memory_space=pltpu.VMEM), pl.BlockSpec(memory_space=pl.ANY)
    results = pl.pallas_call(
        kernel,
        out_shape=[jax.ShapeDtypeStruct(spec[n][1], spec[n][2]) for n in outs],
        in_specs=[vmem if spec[n][0] == GIVEN else anywhere for n in ins],
        out_specs=[vmem if spec[n][0] == MADE else anywhere for n in outs],
        scratch_shapes=scratch,
        compiler_params=pltpu.CompilerParams(
            vmem_limit_bytes=VMEM_LIMIT,
            collective_id=collective_id,
            has_side_effects=collective_id is not None,
        ),
        name=name,
    )(*[operands[n] for n in ins])
    return dict(zip(outs, results))


def flat(slots):
    return [step for steps in slots for step in steps]


def forward_body(k, groups, linked):
    depth, width = groups // 4, k.tok.shape[1]
    unit = width // groups
    if linked:
        place = Place(depth)
        index = place.index()

        def gather(number, full, *pieces):
            own = full.where(index, full.all)
            if len(pieces) == 1:
                targets = [full.ref.at[own]]
            else:
                targets = [full.ref.at[own[0], pl.ds(n * WIDE, WIDE)] for n in range(len(pieces))]
            return Gather(place, full, k.gather_sems.at[number], list(zip(pieces, targets)))

        small = gather(0, Region(place, k.small_all, SMALL_ROWS), k.small_block)
        units = [
            gather(
                1 + g,
                Region(place, k.w_qkv.at[g], unit),
                *(k.qkv_block.at[:, pl.ds(kind * width + g * WIDE, WIDE)] for kind in range(3)),
            )
            for g in range(GROUPS)
        ]
        units.append(gather(4, Region(place, k.w_out, unit), k.out_block))
        for n in range(4):
            full = Region(place, k.w_in, unit, columns=(n * width, width))
            units.append(gather(5 + n, full, k.in_block.at[:, pl.ds(n * width, width)]))
        for n in range(4):
            full = Region(place, k.w_ffo, 4 * unit, n * unit, unit)
            units.append(gather(9 + n, full, k.ffo_block.at[pl.ds(n * unit, unit), :]))
        for one in [small] + units:
            one.fetch()
        place.greet()
        slots = wave(units)
        for n in range(len(units) - 1):
            slots[n] = [units[n + 1].start] + slots[n]
        small.start()
        units[0].start()
        segment_masks(k.seg, k.one, k.mexp)
        phase_normalize(k.tok, k.mid)
        z, x, y, done = small.stages()
        run(z)
        run(slots[0])
        run(x)
        run(slots[1])
        run(y + done)
        unpack_small(k.small_all, k.vec, groups, unit)
        k.spill(N.vec)
        phase_norm_one(k.mid, k.vec, k.h1, k.hbar)
        run(slots[2])
        run(slots[3])
        poll = Poll(*spread_steps(flat(slots[4:5]), 5), *spread_steps(flat(slots[5:7]), 5), *spread_steps(flat(slots[7:9]), 5))
    else:
        k.load(N.w_qkv, N.w_out, N.w_in)
        poll = None
        segment_masks(k.seg, k.one, k.mexp)
        phase_normalize(k.tok, k.mid)
        phase_norm_one(k.mid, k.vec, k.h1, k.hbar)
        k.ready(N.w_qkv)
    k.spill(N.h1)
    phase_attention(
        k.h1, k.hbar, k.w_qkv, k.vec, k.proj, k.cos, k.sin, k.one, k.mexp,
        k.fq, k.fk, k.sq, k.sk, k.v, k.state, k.total, k.att, k.attc, poll,
    )
    k.spill(N.fq, N.fk, N.sq, N.sk, N.v, N.state, N.total, N.att, N.attc)
    if not linked:
        k.ready(N.w_out, N.w_in)
    phase_middle(k.tok, k.att, k.w_out, k.vec, k.mid, k.h2)
    k.spill(N.mid, N.h2)
    if not linked:
        phase_gelu(k.h2, k.w_in, k.vec, k.act, k.slope)
        k.spill(N.act, N.slope)
        return
    k.spill(N.w_qkv, N.w_out)
    for n in range(4):
        if n:
            run(slots[8 + n])
        phase_gelu(k.h2, k.w_in, k.vec, k.act, k.slope, 3 * n, 3 * n + 3)
    k.spill(N.w_in, N.act, N.slope)
    run(flat(slots[12:]))
    k.spill(N.w_ffo)
    for one in [small] + units:
        one.drain()


def feed_body(k, groups, linked):
    depth, width = groups // 4, k.mid.shape[1]
    unit = width // groups
    k.load(N.act, N.cot, N.mid, N.w_ffo, N.vec, N.slope, N.h2, N.w_in)
    polls = [None] * 5
    if linked:
        place = Place(depth)

        def into(base):
            def emit(span, values):
                start, size = span
                k.ffo_grad[pl.ds(pl.multiple_of(base + start, 16), size), :] = values

            return emit

        units = []
        for n in range(4):
            bufs = [getattr(k, name) for name in buffer_names((N.ffo, n))]
            full = Region(place, k.g_ffo, 4 * unit, n * unit, unit)
            units.append(Reduce(place, full, bufs, k.reduce_sems.at[n], into(n * unit)))
        place.greet()
        slots = wave(units)
        sends = [unit.sends() for unit in units]
    k.ready(N.act, N.cot)
    if linked:
        @pl.loop(0, k.g_ffo.shape[0] // 384)
        def _(i):
            rows = tile(i, 384)
            k.g_ffo[rows, :] = tn(k.act[:, rows], k.cot[...]).astype(BF16)

        for one in units:
            run(one.sends())
        polls = [
            None,
            Poll(*spread_steps(flat(slots[0:1]), 4)),
            Poll(*spread_steps(flat(slots[1:3]), 12)),
            Poll(*spread_steps(flat(slots[3:5]), 8)),
            Poll(*spread_steps(flat(slots[5:7]), 2)),
        ]
    else:
        phase_weight_grad(k.act, k.cot, k.g_ffo)
    k.ready(N.mid, N.w_ffo, N.vec)
    if not linked:
        k.spill(N.g_ffo)
    phase_output(k.mid, k.act, k.w_ffo, k.vec, k.output, polls[1])
    k.spill(N.output)
    k.ready(N.slope)
    phase_grad_pre(k.cot, k.w_ffo, k.slope, k.slope, k.small, polls[2])
    k.ready(N.h2)
    phase_weight_grad(k.h2, k.slope, k.g_in, polls[3])
    k.spill(N.g_in)
    k.ready(N.w_in)
    phase_norm_two_back(k.slope, k.w_in, k.mid, k.cot, k.vec, k.gmid, k.gbr, k.small, polls[4])
    k.spill(N.gmid, N.gbr)
    if linked:
        run(flat(slots[7:]))
        for one in units:
            one.drain()


def back_body(k, groups, linked):
    depth, width = groups // 4, k.tok.shape[1]
    unit = width // groups
    k.load(N.att, N.gbr, N.w_out, N.fq, N.fk, N.sq, N.sk, N.v, N.state, N.total, N.attc, N.h1)
    polls = [None] * 3
    if linked:
        place = Place(depth)

        def into(ref, column=0):
            def emit(span, values):
                start, size = span
                start = start if isinstance(start, int) else pl.multiple_of(start, 16)
                ref[pl.ds(start, size), column : column + values.shape[1]] = values

            return emit

        def into_group(group):
            def emit(span, values):
                for kind in range(3):
                    part = values[:, kind * WIDE : (kind + 1) * WIDE]
                    into(k.qkv_grad, kind * width + group * WIDE)(span, part)

            return emit

        def reducer(number, base, full, emit, source=None):
            bufs = [getattr(k, n) for n in buffer_names(base)]
            return Reduce(place, full, bufs, k.reduce_sems.at[number], emit, source)

        wide = [
            reducer(
                n,
                (N.wide, n),
                Region(place, k.g_in, unit, columns=(n * width, width)),
                into(k.in_grad, n * width),
                Region(place, k.hbm[N.g_in], unit, columns=(n * width, width)),
            )
            for n in range(4)
        ]
        out = reducer(4, N.out, Region(place, k.g_out, unit), into(k.out_grad))
        qkv = [
            reducer(5 + g, (N.qkv, g), Region(place, k.g_qkv.at[g], unit), into_group(g)) for g in range(GROUPS)
        ]
        small = reducer(5 + GROUPS, N.small, Region(place, k.small_all, SMALL_ROWS), into(k.small_grad))
        k.load(N.g_in)
        place.greet()
        units = wide + [out] + qkv + [small]
        slots = wave(units)
        for one in wide:
            run(one.sends())
        plan = spread_steps(flat(slots[0:6]), 10 * GROUPS)
        for g in range(GROUPS):
            plan[10 * g + 9] = plan[10 * g + 9] + qkv[g].sends()
        polls = [Poll([], out.sends()), Poll(*plan), Poll(*spread_steps(flat(slots[6:8]), 4))]
    segment_masks(k.seg, k.one, k.mexp)
    k.ready(N.att, N.gbr)
    if linked:
        k.ready(N.g_in)
    phase_weight_grad(k.att, k.gbr, k.g_out, polls[0])
    k.ready(N.w_out, N.fq, N.fk, N.sq, N.sk, N.v, N.state, N.total, N.attc, N.h1)
    k.load(N.w_qkv, N.tok, N.gmid)
    phase_attention_back(
        k.gbr, k.w_out, k.attc, k.proj, k.cos, k.sin, k.one, k.mexp, k.fq, k.fk, k.sq, k.sk, k.v,
        k.state, k.total, k.dnum, k.dstate, k.dtotal, k.gproj, k.small, k.h1, k.g_qkv, polls[1],
    )
    k.ready(N.w_qkv, N.tok, N.gmid)
    phase_norm_one_back(k.gproj, k.w_qkv, k.tok, k.gmid, k.vec, k.tgrad, k.small, polls[2])
    k.spill(N.tgrad)
    if linked:
        for row in (BIAS_OUT, GAIN2, SHIFT2, BIAS_FFO, BIAS_IN):
            k.small[row : row + 1, :] = k.small_two[row : row + 1, :]
        pack_small(k.small, k.small_all, groups, unit)
        run(small.sends())
        run(flat(slots[8:]))
        for one in units:
            one.drain()
    else:
        k.spill(N.g_out, N.g_qkv)


def buffer_names(base):
    base = base if isinstance(base, str) else base[0] + N.g * (1 + base[1])
    return [base + N.b * (1 + n) for n in range(6)]


def position_tables(length):
    half = HEAD_DIM // 2
    frequency = 10000.0 ** (-np.arange(half, dtype=np.float64) / half)
    angles = np.arange(length, dtype=np.float64)[:, None] * frequency[None, :]
    repeat = SLIM // half
    return (
        np.tile(np.cos(angles), (1, repeat)).astype(np.float32),
        np.tile(np.sin(angles), (1, repeat)).astype(np.float32),
    )


def gather(value):
    return lax.all_gather(value, "fsdp", axis=0, tiled=True)


def by_group(weight):
    width = weight.shape[0]
    return weight.reshape(width, 3, GROUPS, WIDE).transpose(2, 0, 1, 3).reshape(GROUPS, width, 3 * WIDE)


def reduce_full(grad):
    piece = lax.psum_scatter(grad.astype(F32), "fsdp", scatter_dimension=0, tiled=True)
    return lax.psum(piece.astype(BF16), "dp").astype(F32)


class Sizes:
    def __init__(self, length, width, hidden, groups, linked):
        self.length, self.width, self.hidden, self.groups, self.linked = length, width, hidden, groups, linked
        self.depth, self.unit = groups // 4, width // groups
        feats = HEADS * FEATS
        rows_wide, rows_feats = (length, width), (length, feats)
        self.weights = dict(
            w_qkv=(GROUPS, width, 3 * WIDE), w_out=(width, width), w_in=(width, hidden), w_ffo=(hidden, width)
        )
        self.common = dict(
            seg=(GIVEN, (1, length), jnp.int32),
            proj=(GIVEN, (feats, HEAD_DIM), F32),
            cos=(GIVEN, (length, SLIM), F32),
            sin=(GIVEN, (length, SLIM), F32),
        )
        self.masks = dict(
            one=(SCRATCH, pltpu.VMEM((SEGS, length), BF16)), mexp=(SCRATCH, pltpu.VMEM((length, STATE), BF16))
        )
        self.saved = dict(
            h1=(rows_wide, BF16), fq=(rows_feats, BF16), fk=(rows_feats, BF16), sq=(rows_feats, F32),
            sk=(rows_feats, F32), v=(rows_wide, BF16), state=((GROUPS * STATE, WIDE), BF16),
            total=((SEGS, feats), F32), att=(rows_wide, BF16), attc=(rows_wide, BF16),
        )
        self.hidden_rows = dict(
            mid=(rows_wide, F32), h2=(rows_wide, BF16), act=((length, hidden), BF16), slope=((length, hidden), BF16)
        )
        self.rows = rows_wide


def run_forward(z, values):
    spec = dict(tok=(GIVEN, z.rows, BF16), **z.common)
    if z.linked:
        spec.update(small_block=(FAR, (SMALL_ROWS, SMALL_COLUMNS), BF16))
        for n in (N.qkv_block, N.out_block, N.in_block, N.ffo_block):
            spec[n] = (FAR, values[n].shape, BF16)
        spec.update({n: (SPILL, dims, BF16) for n, dims in z.weights.items()})
        spec.update(
            vec=(SPILL, (8, z.hidden), F32),
            small_all=(SCRATCH, pltpu.VMEM((z.groups * SMALL_ROWS, SMALL_COLUMNS), BF16)),
            gather_sems=(SCRATCH, pltpu.SemaphoreType.DMA((13, Gather.count(z.depth)))),
        )
    else:
        spec.update({n: (LOAD, z.weights[n], BF16) for n in (N.w_qkv, N.w_out, N.w_in)})
        spec.update(vec=(GIVEN, (8, z.hidden), F32))
    spec.update({n: (SPILL,) + v for n, v in {**z.saved, **z.hidden_rows}.items()})
    spec.update(z.masks, hbar=(SCRATCH, pltpu.VMEM((8, z.width), F32)))
    return call(
        N.forward, lambda k: forward_body(k, z.groups, z.linked), spec, values, 1 if z.linked else None
    )


def run_feed(z, values):
    spec = {n: (LOAD,) + z.hidden_rows[n] for n in (N.act, N.mid, N.slope, N.h2)}
    spec.update(
        cot=(LOAD, z.rows, BF16), w_ffo=(LOAD, z.weights[N.w_ffo], BF16), w_in=(LOAD, z.weights[N.w_in], BF16),
        vec=(LOAD, (8, z.hidden), F32), output=(SPILL, z.rows, BF16), g_in=(SPILL, z.weights[N.w_in], BF16),
        gmid=(SPILL, z.rows, F32), gbr=(SPILL, z.rows, BF16), small=(MADE, (8, z.hidden), F32),
    )
    if z.linked:
        spec.update(
            ffo_grad=(MADE, (z.hidden // z.groups, z.width), F32),
            g_ffo=(SCRATCH, pltpu.VMEM((z.hidden, z.width), BF16)),
            reduce_sems=(SCRATCH, pltpu.SemaphoreType.DMA((4, Reduce.count(z.depth)))),
        )
        for number in range(4):
            buffers = Reduce.buffers(z.depth, z.unit, z.width)
            spec.update({n: (SCRATCH, buf) for n, buf in zip(buffer_names((N.ffo, number)), buffers)})
    else:
        spec.update(g_ffo=(SPILL, (z.hidden, z.width), BF16))
    return call(N.feed, lambda k: feed_body(k, z.groups, z.linked), spec, values, 2 if z.linked else None)


def run_back(z, values):
    width, weights = z.width, z.weights
    spec = dict(vec=(GIVEN, (8, z.hidden), F32), **z.common)
    spec.update({n: (LOAD,) + v for n, v in z.saved.items()})
    spec.update(
        tok=(LOAD, z.rows, BF16), gbr=(LOAD, z.rows, BF16), gmid=(LOAD, z.rows, F32),
        w_qkv=(LOAD, weights[N.w_qkv], BF16), w_out=(LOAD, weights[N.w_out], BF16),
        tgrad=(SPILL, z.rows, BF16),
        dnum=(SCRATCH, pltpu.VMEM((z.length, WIDE), BF16)), dstate=(SCRATCH, pltpu.VMEM((STATE, WIDE), BF16)),
        dtotal=(SCRATCH, pltpu.VMEM((SEGS, SLIM), F32)), gproj=(SCRATCH, pltpu.VMEM((z.length, 3 * width), BF16)),
        **z.masks,
    )
    if z.linked:
        spec.update(
            small=(SCRATCH, pltpu.VMEM((8, z.hidden), F32)), small_two=(GIVEN, (8, z.hidden), F32),
            g_in=(LOAD, weights[N.w_in], BF16), g_out=(SCRATCH, pltpu.VMEM(weights[N.w_out], BF16)),
            g_qkv=(SCRATCH, pltpu.VMEM((GROUPS, width, 3 * WIDE), BF16)),
            small_all=(SCRATCH, pltpu.VMEM((z.groups * SMALL_ROWS, SMALL_COLUMNS), BF16)),
            in_grad=(MADE, (z.unit, z.hidden), F32), out_grad=(MADE, (z.unit, width), F32),
            qkv_grad=(MADE, (z.unit, 3 * width), F32), small_grad=(MADE, (SMALL_ROWS, SMALL_COLUMNS), F32),
            reduce_sems=(SCRATCH, pltpu.SemaphoreType.DMA((6 + GROUPS, Reduce.count(z.depth)))),
        )
        sizes = [(N.out, (z.unit, width)), (N.small, (SMALL_ROWS, SMALL_COLUMNS))]
        sizes += [((N.wide, n), (z.unit, width)) for n in range(4)]
        sizes += [((N.qkv, g), (z.unit, 3 * WIDE)) for g in range(GROUPS)]
        for base, dims in sizes:
            spec.update({n: (SCRATCH, buf) for n, buf in zip(buffer_names(base), Reduce.buffers(z.depth, *dims))})
    else:
        spec.update(
            small=(MADE, (8, z.hidden), F32), g_out=(SPILL, weights[N.w_out], BF16),
            g_qkv=(SPILL, (GROUPS, width, 3 * WIDE), BF16),
        )
    return call(N.back, lambda k: back_body(k, z.groups, z.linked), spec, values, 3 if z.linked else None)


def body(
    linked,
    tokens, segment_ids, projection, norm1_gain, norm1_bias, qkv_weight, qkv_bias, out_weight, out_bias,
    norm2_gain, norm2_bias, in_weight, in_bias, ffn_out_weight, ffn_out_bias, cotangent,
):
    length, width = tokens.shape
    hidden = in_weight.shape[1]
    groups = lax.axis_size(N.fsdp)
    unit = width // groups
    z = Sizes(length, width, hidden, groups, linked)
    cos, sin = position_tables(length)
    vectors = {
        GAIN1: norm1_gain, SHIFT1: norm1_bias, BIAS_OUT: out_bias, GAIN2: norm2_gain, SHIFT2: norm2_bias,
        BIAS_FFO: ffn_out_bias, BIAS_QKV: qkv_bias, BIAS_IN: in_bias,
    }
    values = dict(
        tok=tokens, seg=segment_ids, proj=projection.reshape(HEADS * FEATS, HEAD_DIM), cos=cos, sin=sin,
        cot=cotangent, qkv_block=qkv_weight, out_block=out_weight, in_block=in_weight, ffo_block=ffn_out_weight,
    )
    if linked:
        values.update(small_block=small_block(vectors))
    else:
        values.update(
            w_qkv=by_group(gather(qkv_weight)), w_out=gather(out_weight), w_in=gather(in_weight), w_ffo=gather(ffn_out_weight),
            vec=jnp.stack(
                [
                    jnp.pad(gather(vectors[n]).astype(F32), (0, hidden - vectors[n].shape[0] * groups))
                    for n in range(len(vectors))
                ]
            ),
        )
    values.update(run_forward(z, values))
    made = run_feed(z, values)
    small_two = made.pop(N.small)
    values.update(made, small_two=small_two)
    values.update(run_back(z, values))
    if linked:
        smalls = {}
        for name, _start, many, third, offset in GRAD_LAYOUT:
            smalls[name] = values[N.small_grad][16 * third, offset * unit : (offset + many) * unit]
        grads = [values[n] for n in (N.qkv_grad, N.out_grad, N.in_grad, N.ffo_grad)]
    else:
        small_one = values[N.small]
        full = {
            n: (small_one if n in (GAIN1, SHIFT1, BIAS_QKV) else small_two)[n, : vectors[n].shape[0] * groups]
            for n in vectors
        }
        smalls = {n: reduce_full(v) for n, v in full.items() if n != BIAS_QKV}
        smalls[QUERY_KEY] = reduce_full(full[BIAS_QKV][: 2 * width])
        smalls[VALUE] = reduce_full(full[BIAS_QKV][2 * width :])
        g_qkv = values[N.g_qkv].reshape(GROUPS, width, 3, WIDE).transpose(1, 2, 0, 3).reshape(width, 3 * width)
        grads = [reduce_full(g) for g in (g_qkv, values[N.g_out], values[N.g_in], values[N.g_ffo])]
    return (
        values[N.output], values[N.tgrad], smalls[GAIN1], smalls[SHIFT1], grads[0], smalls[QUERY_KEY],
        smalls[VALUE], grads[1], smalls[BIAS_OUT], smalls[GAIN2], smalls[SHIFT2], grads[2], smalls[BIAS_IN],
        grads[3], smalls[BIAS_FFO],
    )


def solution(mesh):
    rows = P(("fsdp", "dp"), None)
    vector, matrix = P("fsdp"), P("fsdp", None)
    in_specs = (
        rows, rows, P(), vector, vector, matrix, vector, matrix, vector,
        vector, vector, matrix, vector, matrix, vector, rows,
    )
    out_specs = (
        rows, rows, vector, vector, matrix, vector, vector, matrix, vector,
        vector, vector, matrix, vector, matrix, vector,
    )
    linked = mesh.shape["fsdp"] == 16 and mesh.shape["dp"] == 2
    return jax.shard_map(
        functools.partial(body, linked), mesh=mesh, in_specs=in_specs, out_specs=out_specs, check_vma=False
    )
```

time: 676 us -> 248 us (0.37)
  waiting for transfers between devices: 357 us -> 0 us
  blocking collectives: 127 us -> 0 us
  Pallas kernels: 150 us -> 230 us
  between operations: 17.9 us -> 0.69 us
  other arithmetic: 10.5 us -> 0.76 us
    reduce_scatter x4 -> x0, waiting for transfers between devices: 283 us -> none  [reduce_full(): lax.psum_scatter(grad.astype(F32), 'fsdp', scatter_dimension=0, tiled=True)]
    unnamed x2 -> x0, blocking collectives: 122 us -> none
    pallas_call x3, Pallas kernels: 150 us -> 230 us  [call(): pl.pallas_call(kernel, out_shape=[jax.ShapeDtypeStruct(spec[n][1], spec[n...]
    all_gather x4 -> x0, waiting for transfers between devices: 70 us -> none  [gather(): return lax.all_gather(value, 'fsdp', axis=0, tiled=True)]
    convert_element_type x13 -> x0, other arithmetic: 9.8 us -> none  [reduce_full(): return lax.psum(piece.astype(BF16), 'dp').astype(F32)]
  transfers between devices with their start and end apart: 9 -> 0, of which waited for: 7 -> 0; matrix products, arithmetic and copies ran while one was open for 3% -> 0% of each run, Pallas kernels for 8% -> 0%
where the time goes in v2:
time: 248 us; the launch traced here: 247 us
  Pallas kernels  230 us (93%)
  local copies, waits for them, and re-layouts  15.7 us (6%)
    pallas_call x3, Pallas kernels, call(): pl.pallas_call(kernel, out_shape=[jax.ShapeDtypeStruct(spec[n][1], spec[n...  230 us
    unnamed x17, local copies, waits for them, and re-layouts  7.11 us

profile of v2, /device:TPU:0, one launch (start us, length us, event | category | flops | bytes accessed | tf_op | source)
XLA Modules:
  0.0 247.3 jit_solution(3377603172785242758)
XLA Ops:
  0.6 3.4 %concatenate.6 = bf16[240]{0:T(256)(128)(2,1)S(1)} concatenate(bf16[48]{0:T(256)(128)(2,1)} %param.21, bf16[48]{0:T(256)(128)(2,1)} %param.22, bf16[48]{0:T(256)(128)(2,1)} %param.26, bf16[48]{0:T(256)(128)(2,1)} %param.27, bf16[48]{0:T(256)(128)(2,1)} %param.28), dimensions={0} | concatenate | bytes 960 | tf_op jit(solution)/shard_map/concatenate | solution.py:700
  4.1 0.7 fusion.2
  4.8 0.7 pad.17
  5.5 0.6 pad.18.clone
  6.2 89.1 %forward.1 = (bf16[3,768,768]{2,1,0:T(8,128)(2,1)}, bf16[768,768]{1,0:T(8,128)(2,1)}, bf16[768,3072]{1,0:T(8,128)(2,1)}, bf16[3072,768]{1,0:T(8,128)(2,1)}, f32[...) custom-call(bf16[1024,768]{1,0:T(8,128)(2,1)} %refs_15_.1, ...), custom_call_target="tpu_custom_call" | custom-call | tf_op jit(solution)/shard_map/forward/pallas_call | solution.py:796
  95.3 55.9 %feed.1 = (bf16[1024,768]{1,0:T(8,128)(2,1)}, bf16[768,3072]{1,0:T(8,128)(2,1)}, f32[1024,768]{1,0:T(8,128)}, bf16[1024,768]{1,0:T(8,128)(2,1)}, f32[8,3072]{1,0:T(8,128)}, /*index=5*/f32[192,768]{1,0:T(8,128)}) custom-call(bf16[1024,3072]{1,0:T(8,128)(2,1)} %get-tuple-element.45.refs_0_, f32[1024,768]{1,0:T(8,128)} %get-tuple-element.46.refs_1_, ...), custom_call_target="tpu_custom_call" | custom-call | tf_op jit(solution)/shard_map/feed/pallas_call | solution.py:796
  151.1 85.2 %back.1 = (bf16[1024,768]{1,0:T(8,128)(2,1)}, f32[48,3072]{1,0:T(8,128)}, f32[48,768]{1,0:T(8,128)}, f32[48,2304]{1,0:T(8,128)}, f32[48,256]{1,0:T(8,128)}) custom-call(f32[8,3072]{1,0:T(8,128)} %get-tuple-element.51.refs_7_.refs_0_, s32[1,1024]{1,0:T(1,128)} %refs_1_.3, f32[384,64]{1,0:T(8,128)} %bitcast.22, f32[1024,128]{1,0:T(8,128)} %constant.7.clone.refs_3_, ...), custom_call_target="tpu_custom_call" | custom-call | tf_op jit(solution)/shard_map/back/pallas_call | solution.py:796
  236.4 1.2 slice_bitcast_fusion.5
  237.6 1.3 slice.34
  238.8 1.4 slice_bitcast_fusion
  240.2 0.0 copy-start
  240.2 2.8 %copy.41 = bf16[1024,768]{1,0:T(8,128)(2,1)} copy(bf16[1024,768]{1,0:T(8,128)(2,1)} %get-tuple-element.97) | data formatting | bytes 3145728
  243.0 0.0 copy-done
  243.0 0.0 copy-start.3
  243.0 0.0 copy-start.4
  243.0 0.0 copy-start.2
  243.0 1.1 copy.42
  244.2 0.1 copy-done.3
  244.3 0.0 copy-start.1
  244.3 0.8 copy.43
  245.0 0.0 copy-done.4
  245.0 0.7 copy.44
  245.7 0.0 copy-done.2
  245.7 0.8 copy.45
  246.5 0.0 copy-done.1
  246.5 0.8 copy.46
  (6 shorter events, 0.0 us)
Async XLA Ops:
  240.2 2.8 %copy-start = (bf16[1024,768]{1,0:T(8,128)(2,1)S(1)}, bf16[1024,768]{1,0:T(8,128)(2,1)}, u32[]{:S(2)}) copy-start(bf16[1024,768]{1,0:T(8,128)(2,1)} %get-tuple-element.98) | copy-start | bytes 4718596
  243.0 1.3 copy-start.3
  243.0 2.0 copy-start.4
  243.0 2.7 %copy-start.2 = (f32[48,3072]{1,0:T(8,128)S(1)}, f32[48,3072]{1,0:T(8,128)}, u32[]{:S(2)}) copy-start(f32[48,3072]{1,0:T(8,128)} %get-tuple-element.108) | copy-start | bytes 1769476
  244.3 2.2 copy-start.1

commit v3 on v2

--- a/solution.py
+++ b/solution.py
@@ -281,8 +281,10 @@
         checkpoint(poll, r, 1)
 
 
-def phase_grad_pre(cot_ref, w_ffo_ref, slope_ref, gpre_ref, small_ref, poll=None):
-    @pl.loop(0, w_ffo_ref.shape[0] // 256)
+def phase_grad_pre(cot_ref, w_ffo_ref, slope_ref, gpre_ref, small_ref, first=0, last=None, poll=None):
+    last = w_ffo_ref.shape[0] // 256 if last is None else last
+
+    @pl.loop(first, last)
     def _(j):
         cols = tile(j, 256)
         grad = nt(cot_ref[...], w_ffo_ref[cols, :]) * slope_ref[:, cols].astype(F32)
@@ -290,6 +292,13 @@
         gpre_ref[:, cols] = grad
         small_ref[BIAS_IN : BIAS_IN + 1, cols] = column_sum(grad.astype(F32))
         checkpoint(poll, j, 1)
+
+
+def phase_ffo_grad(act_ref, cot_ref, g_ffo_ref, first, last):
+    @pl.loop(first, last)
+    def _(i):
+        rows = tile(i, 384)
+        g_ffo_ref[rows, :] = tn(act_ref[:, rows], cot_ref[...]).astype(BF16)
 
 
 def phase_weight_grad(left_ref, right_ref, out_ref, poll=None):
@@ -334,7 +343,7 @@
 def phase_attention_back(
     gbr_ref, w_out_ref, attc_ref, proj_ref, cos_ref, sin_ref, one_ref, mexp_ref,
     fq_ref, fk_ref, sq_ref, sk_ref, v_ref, state_ref, total_ref,
-    dnum_ref, dstate_ref, dtotal_ref, gproj_ref, small_ref, h1_ref, g_qkv_ref, poll=None,
+    dnum_ref, dstate_ref, dtotal_ref, gproj_ref, small_ref, h1_ref, g_qkv_ref, arrive, poll=None,
 ):
     length, width = gbr_ref.shape
 
@@ -378,6 +387,7 @@
             checkpoint(poll, g, 10, 0, r, 4)
 
         segment_states(fq_ref, one_ref, dnum_ref[...], g, dstate_ref, 0)
+        pl.when(g == 0)(arrive)
 
         @pl.loop(0, length // 256)
         def _(r):
@@ -535,15 +545,15 @@
         sent = self.full.bulk(2 * (depth - 1) + 2 + 3 + 5 * (depth - 1) + 3 * depth + 2 * depth - 1)
         pltpu.make_async_copy(sent, sent, self.sems.at[self.sent]).wait()
 
-    def stages(self):
-        depth = self.place.depth
-        return (
-            [functools.partial(self.z_step, d) for d in (1, 3, 2)],
-            [functools.partial(self.x_step, d) for d in (0, 1, 3, 2)],
-            [functools.partial(self.y_step, d, 0) for d in (1, 3, 2)]
-            + [functools.partial(self.y_step, d, 1) for d in (0, 1, 3, 2)],
-            [self.done],
-        )
+    def step(self, code):
+        if code == 0:
+            self.start()
+        elif code < 5:
+            self.z_step(code - 1)
+        elif code < 9:
+            self.x_step(code - 5)
+        else:
+            self.y_step((code - 9) // 2, (code - 9) % 2)
 
 
 class Reduce:
@@ -645,36 +655,31 @@
     def sends(self):
         return [functools.partial(self.c_send, d, xr) for d, xr in ORDER]
 
-    def stages(self):
-        depth = self.place.depth
-        return (
-            [functools.partial(self.c_step, d, xr) for d, xr in ORDER],
-            [functools.partial(self.y_step, d, xr) for d, xr in ORDER],
-            [functools.partial(self.x_step, d) for d in range(depth - 1, -1, -1)],
-            [self.z_step],
-            [self.f_step],
-        )
-
-
-def wave(units, slots=None):
-    stages = [unit.stages() for unit in units]
-    depth = len(stages[0])
-    out = []
-    for slot in range(len(units) + depth - 1):
-        steps = []
-        for number in range(depth - 1, -1, -1):
-            if 0 <= slot - number < len(units):
-                steps += stages[slot - number][number]
-        out.append(steps)
-    return out
-
-
-def spread_steps(steps, checkpoints, start=0):
-    plan = [[] for _ in range(checkpoints)]
-    span = checkpoints - start
-    for number, step in enumerate(steps):
-        plan[start + number * span // len(steps)].append(step)
-    return plan
+    def step(self, code):
+        if code < 8:
+            self.c_step(code // 2, code % 2)
+        elif code < 16:
+            self.y_step((code - 8) // 2, code % 2)
+        elif code < 20:
+            self.x_step(code - 16)
+        elif code == 20:
+            self.z_step()
+        else:
+            self.f_step()
+
+
+class Plan:
+    def __init__(self, sections, units):
+        self.sections, self.units = iter(sections), units
+
+    def take(self):
+        return [functools.partial(self.units[number // 32].step, number % 32) for number in next(self.sections)]
+
+    def takes(self, count):
+        return [self.take() for _ in range(count)]
+
+    def run(self):
+        run(self.take())
 
 
 def run(steps):
@@ -694,12 +699,13 @@
 
 
 def small_block(vectors):
-    rows = []
-    for third in range(3):
-        parts = [vectors[name] for name, _m, row, _p in SMALL_LAYOUT if row == third]
-        flat = jnp.concatenate(parts)
-        rows.append(jnp.pad(flat, (0, SMALL_COLUMNS - flat.shape[0])))
-    return jnp.pad(jnp.stack(rows)[:, None, :], ((0, 0), (0, 15), (0, 0))).reshape(SMALL_ROWS, SMALL_COLUMNS)
+    unit = vectors[GAIN1].shape[0]
+    block = jnp.zeros((3, 16, SMALL_COLUMNS), BF16)
+    for name, many, third, place in SMALL_LAYOUT:
+        start, size = place * unit, many * unit
+        ends = ((third, 2 - third), (0, 15), (start, SMALL_COLUMNS - start - size))
+        block = block + jnp.pad(vectors[name].reshape(1, 1, size), ends)
+    return block.reshape(SMALL_ROWS, SMALL_COLUMNS)
 
 
 def selector(unit, many, offset, groups):
@@ -743,14 +749,23 @@
 
 
 class Arrays:
+    COPIES = 48
+
     def __init__(self, spec, refs, sems):
-        self.hbm, self.spec, self.sems, self.open = {}, spec, sems, []
-        self.slots = {name: n for n, name in enumerate(x for x in spec if spec[x][0] in (LOAD, SPILL))}
+        self.hbm, self.spec, self.sems, self.open, self.slots = {}, spec, sems, [], {}
         for name, ref in refs.items():
             setattr(self, name, ref)
 
-    def copy(self, name):
-        hbm, vmem, sem = self.hbm[name], getattr(self, name), self.sems.at[self.slots[name]]
+    def copy(self, what):
+        name, part, parts, axis = (what, 0, 1, 0) if isinstance(what, str) else what
+        hbm, vmem = self.hbm[name], getattr(self, name)
+        if parts > 1:
+            size = vmem.shape[axis] // parts
+            span = pl.ds(part * size, size)
+            where = (span,) if axis == 0 else (slice(None), span)
+            hbm, vmem = hbm.at[where], vmem.at[where]
+        sem = self.sems.at[self.slots.setdefault(what, len(self.slots))]
+        assert len(self.slots) <= self.COPIES
         if self.spec[name][0] == LOAD:
             return pltpu.make_async_copy(hbm, vmem, sem)
         return pltpu.make_async_copy(vmem, hbm, sem)
@@ -770,6 +785,10 @@
 
     def close(self):
         self.ready(*self.open)
+
+
+def parts_of(name, parts, axis):
+    return [(name, part, parts, axis) for part in range(parts)]
 
 
 def call(name, body, spec, operands, collective_id=None, flops=0):
@@ -778,7 +797,7 @@
     moved = [n for n in spec if spec[n][0] in (LOAD, SPILL)]
     tmps = [n for n in spec if spec[n][0] == SCRATCH]
     scratch = [pltpu.VMEM(spec[n][1], spec[n][2]) for n in moved] + [spec[n][1] for n in tmps]
-    scratch.append(pltpu.SemaphoreType.DMA((max(1, len(moved)),)))
+    scratch.append(pltpu.SemaphoreType.DMA((Arrays.COPIES,)))
 
     def kernel(*refs):
         given, made, inner = refs[: len(ins)], refs[len(ins) : len(ins) + len(outs)], refs[len(ins) + len(outs) :]
@@ -809,13 +828,128 @@
     return dict(zip(outs, results))
 
 
-def flat(slots):
-    return [step for steps in slots for step in steps]
+PLAN_FORWARD = (
+    (32, 64),
+    (389,),
+    (5, 388, 387, 37, 386, 69, 394, 10, 399, 392, 4, 397, 391, 390, 42, 395, 3, 74, 2, 96, 400, 15, 398, 396, 8, 36,
+     13, 7, 35, 11),
+    (6, 34, 101, 128),
+    (16, 14, 40, 47),
+    (68, 45, 39, 67, 12, 66, 160, 38, 43, 106, 48, 133),
+    (46, 72, 79, 77, 100, 99),
+    (44, 70, 71, 75, 98, 138, 192),
+    (165,),
+    (80, 104, 111, 132, 131),
+    (76, 78, 102, 103, 107, 109, 130, 224),
+    (),
+    (112, 143, 164, 170, 197),
+    (136, 135, 141, 162, 163, 256),
+    (108, 110, 134),
+    (139, 175, 196, 202, 229),
+    (144, 142, 166, 168, 171, 194, 195, 288),
+    (),
+    (140, 167, 173, 207, 228, 261),
+    (200, 227, 234),
+    (172, 176, 198, 226, 320),
+    (174, 199, 203, 205, 260),
+    (208, 232, 239, 237, 258, 259, 266, 293, 352),
+    (),
+    (204, 206, 230, 231, 235, 271, 292),
+    (),
+    (240, 264, 267, 290, 291, 325),
+    (236, 262, 263, 269, 298),
+    (),
+    (238, 272, 296, 303, 322, 324, 323, 357),
+    (294, 295, 299, 301, 330),
+    (),
+    (268, 270, 304, 356, 355),
+    (326, 328, 331, 335, 333, 354),
+    (),
+    (300, 302, 327, 367, 362),
+    (332, 360, 359, 365),
+    (),
+    (336,),
+    (363, 358, 334, 368),
+    (366, 364),
+)
+PLAN_FEED = (
+    (),
+    (),
+    (7, 5, 3, 1),
+    (6, 4, 2, 0, 39),
+    (37, 35, 33, 38, 36),
+    (34, 32, 71, 69, 67),
+    (65, 70, 68, 66, 64, 103),
+    (101, 99, 97, 102, 100),
+    (15, 13, 98, 96),
+    (11,),
+    (9,),
+    (14,),
+    (12, 10),
+    (8,),
+    (19, 47, 45),
+    (18, 43),
+    (17, 41, 46),
+    (44, 42),
+    (16, 40),
+    (51, 79, 77),
+    (50, 75),
+    (49, 48, 73, 78, 76, 74, 72),
+    (20, 83, 82, 81, 111, 109, 107, 105, 110),
+    (80, 108, 106, 104),
+    (),
+    (21, 52, 115),
+    (114,),
+    (113, 112, 53, 84, 85, 116, 117),
+)
+PLAN_BACK = (
+    (7,),
+    (5, 3, 1, 6, 4, 2, 0, 39, 37, 35),
+    (33, 38, 36, 34, 32, 71, 69, 67, 65, 70),
+    (15, 68, 66, 64, 103, 101, 99, 97, 102, 100, 98),
+    (13, 96),
+    (11, 9, 14, 135, 133, 131, 129, 134, 132, 130),
+    (12, 10, 128),
+    (8, 19, 18, 47, 45, 43, 41),
+    (17, 16, 46, 44),
+    (42, 40),
+    (79, 77, 75),
+    (51, 73),
+    (50, 78, 76),
+    (49, 74, 72),
+    (48, 111, 109, 107),
+    (20, 83, 82, 105, 110, 167, 165, 163, 161, 166, 164, 162),
+    (81, 108, 106, 104, 160),
+    (80, 115, 143, 141, 139, 137),
+    (52, 114, 142, 140, 138),
+    (113, 112, 136),
+    (21, 175),
+    (147, 173, 171),
+    (84, 146, 169, 174),
+    (145, 172, 170),
+    (144, 168),
+    (53, 116, 179, 178, 199, 197, 195, 193, 198, 196, 194),
+    (85, 177, 192),
+    (176,),
+    (117, 148, 207, 205),
+    (203, 201),
+    (206, 204),
+    (202, 200),
+    (149, 180, 211),
+    (210,),
+    (209, 208, 231),
+    (181, 229, 227, 225, 230, 228, 226, 224),
+    (),
+    (239,),
+    (237, 235, 233, 212, 238, 263, 261, 259, 236, 257, 262, 260, 258, 256, 234, 243, 232, 242, 213, 241, 271, 269,
+     267, 265, 270, 268, 240, 266, 264, 275, 274, 273, 272, 244, 276, 245, 277),
+)
 
 
 def forward_body(k, groups, linked):
     depth, width = groups // 4, k.tok.shape[1]
     unit = width // groups
+    k.load(N.cot)
     if linked:
         place = Place(depth)
         index = place.index()
@@ -847,25 +981,29 @@
         for one in [small] + units:
             one.fetch()
         place.greet()
-        slots = wave(units)
-        for n in range(len(units) - 1):
-            slots[n] = [units[n + 1].start] + slots[n]
+        units.append(small)
+        plan = Plan(PLAN_FORWARD, units)
         small.start()
         units[0].start()
         segment_masks(k.seg, k.one, k.mexp)
+        plan.run()
         phase_normalize(k.tok, k.mid)
-        z, x, y, done = small.stages()
-        run(z)
-        run(slots[0])
-        run(x)
-        run(slots[1])
-        run(y + done)
+        plan.run()
+        plan.run()
+        small.done()
         unpack_small(k.small_all, k.vec, groups, unit)
         k.spill(N.vec)
+        plan.run()
         phase_norm_one(k.mid, k.vec, k.h1, k.hbar)
-        run(slots[2])
-        run(slots[3])
-        poll = Poll(*spread_steps(flat(slots[4:5]), 5), *spread_steps(flat(slots[5:7]), 5), *spread_steps(flat(slots[7:9]), 5))
+        plan.run()
+        plan.run()
+        units[0].done()
+        sections = []
+        for g in range(GROUPS):
+            sections += plan.takes(5)
+            if g + 1 < GROUPS:
+                sections[-1] = sections[-1] + plan.take() + [units[g + 1].done]
+        poll = Poll(*sections)
     else:
         k.load(N.w_qkv, N.w_out, N.w_in)
         poll = None
@@ -879,31 +1017,48 @@
         k.fq, k.fk, k.sq, k.sk, k.v, k.state, k.total, k.att, k.attc, poll,
     )
     k.spill(N.fq, N.fk, N.sq, N.sk, N.v, N.state, N.total, N.att, N.attc)
-    if not linked:
+    if linked:
+        plan.run()
+        units[3].done()
+    else:
         k.ready(N.w_out, N.w_in)
     phase_middle(k.tok, k.att, k.w_out, k.vec, k.mid, k.h2)
     k.spill(N.mid, N.h2)
-    if not linked:
-        phase_gelu(k.h2, k.w_in, k.vec, k.act, k.slope)
-        k.spill(N.act, N.slope)
-        return
-    k.spill(N.w_qkv, N.w_out)
+    k.ready(N.cot)
+    if linked:
+        k.spill(N.w_qkv, N.w_out)
+        plan.run()
     for n in range(4):
-        if n:
-            run(slots[8 + n])
+        if linked:
+            plan.run()
+            units[4 + n].done()
         phase_gelu(k.h2, k.w_in, k.vec, k.act, k.slope, 3 * n, 3 * n + 3)
-    k.spill(N.w_in, N.act, N.slope)
-    run(flat(slots[12:]))
-    k.spill(N.w_ffo)
-    for one in [small] + units:
-        one.drain()
+        if linked:
+            plan.run()
+        phase_ffo_grad(k.act, k.cot, k.g_ffo, 2 * n, 2 * n + 2)
+        k.spill((N.act, n, 4, 1), (N.slope, n, 4, 1), (N.g_ffo, n, 4, 0))
+        if linked:
+            plan.run()
+    if linked:
+        k.spill(N.w_in)
+        for one in units[8:12]:
+            plan.run()
+            one.done()
+        k.spill(N.w_ffo)
+        for one in units:
+            one.drain()
 
 
 def feed_body(k, groups, linked):
     depth, width = groups // 4, k.mid.shape[1]
     unit = width // groups
-    k.load(N.act, N.cot, N.mid, N.w_ffo, N.vec, N.slope, N.h2, N.w_in)
-    polls = [None] * 5
+    k.load(N.cot)
+    for n in range(4):
+        k.load((N.w_ffo, n, 4, 0), (N.slope, n, 4, 1))
+        if linked and n == 0:
+            k.load(N.g_ffo)
+    k.load(N.h2, N.w_in, N.mid, N.vec, N.act)
+    polls = [[None] * 4, None, None, None]
     if linked:
         place = Place(depth)
 
@@ -918,43 +1073,38 @@
         for n in range(4):
             bufs = [getattr(k, name) for name in buffer_names((N.ffo, n))]
             full = Region(place, k.g_ffo, 4 * unit, n * unit, unit)
-            units.append(Reduce(place, full, bufs, k.reduce_sems.at[n], into(n * unit)))
+            source = Region(place, k.hbm[N.g_ffo], 4 * unit, n * unit, unit)
+            units.append(Reduce(place, full, bufs, k.reduce_sems.at[n], into(n * unit), source))
         place.greet()
-        slots = wave(units)
-        sends = [unit.sends() for unit in units]
-    k.ready(N.act, N.cot)
-    if linked:
-        @pl.loop(0, k.g_ffo.shape[0] // 384)
-        def _(i):
-            rows = tile(i, 384)
-            k.g_ffo[rows, :] = tn(k.act[:, rows], k.cot[...]).astype(BF16)
-
         for one in units:
             run(one.sends())
+        plan = Plan(PLAN_FEED, units)
+        first = plan.take()
+        sections = plan.takes(12)
         polls = [
-            None,
-            Poll(*spread_steps(flat(slots[0:1]), 4)),
-            Poll(*spread_steps(flat(slots[1:3]), 12)),
-            Poll(*spread_steps(flat(slots[3:5]), 8)),
-            Poll(*spread_steps(flat(slots[5:7]), 2)),
+            [Poll(*([[]] * (3 * n)), *sections[3 * n : 3 * n + 3]) for n in range(4)],
+            Poll(*plan.takes(8)),
+            Poll(*plan.takes(2)),
+            Poll(*plan.takes(4)),
         ]
-    else:
-        phase_weight_grad(k.act, k.cot, k.g_ffo)
-    k.ready(N.mid, N.w_ffo, N.vec)
-    if not linked:
-        k.spill(N.g_ffo)
-    phase_output(k.mid, k.act, k.w_ffo, k.vec, k.output, polls[1])
+    k.ready(N.cot)
+    for n in range(4):
+        k.ready((N.w_ffo, n, 4, 0), (N.slope, n, 4, 1))
+        if linked and n == 0:
+            k.ready(N.g_ffo)
+            run(first)
+        phase_grad_pre(k.cot, k.w_ffo, k.slope, k.slope, k.small, 3 * n, 3 * n + 3, polls[0][n])
+    k.ready(N.h2)
+    phase_weight_grad(k.h2, k.slope, k.g_in, polls[1])
+    k.spill(N.g_in)
+    k.ready(N.w_in, N.mid, N.vec)
+    phase_norm_two_back(k.slope, k.w_in, k.mid, k.cot, k.vec, k.gmid, k.gbr, k.small, polls[2])
+    k.spill(N.gmid, N.gbr)
+    k.ready(N.act)
+    phase_output(k.mid, k.act, k.w_ffo, k.vec, k.output, polls[3])
     k.spill(N.output)
-    k.ready(N.slope)
-    phase_grad_pre(k.cot, k.w_ffo, k.slope, k.slope, k.small, polls[2])
-    k.ready(N.h2)
-    phase_weight_grad(k.h2, k.slope, k.g_in, polls[3])
-    k.spill(N.g_in)
-    k.ready(N.w_in)
-    phase_norm_two_back(k.slope, k.w_in, k.mid, k.cot, k.vec, k.gmid, k.gbr, k.small, polls[4])
-    k.spill(N.gmid, N.gbr)
     if linked:
-        run(flat(slots[7:]))
+        plan.run()
         for one in units:
             one.drain()
 
@@ -962,7 +1112,14 @@
 def back_body(k, groups, linked):
     depth, width = groups // 4, k.tok.shape[1]
     unit = width // groups
-    k.load(N.att, N.gbr, N.w_out, N.fq, N.fk, N.sq, N.sk, N.v, N.state, N.total, N.attc, N.h1)
+    first = (N.w_out, N.fq, N.attc, N.total, N.state, N.sq)
+    later = (N.v, N.fk, N.sk, N.h1)
+    k.load(N.att, N.gbr)
+    if linked:
+        k.load(N.g_in)
+    k.load(*first)
+    if linked:
+        k.load(*later)
     polls = [None] * 3
     if linked:
         place = Place(depth)
@@ -1002,26 +1159,31 @@
             reducer(5 + g, (N.qkv, g), Region(place, k.g_qkv.at[g], unit), into_group(g)) for g in range(GROUPS)
         ]
         small = reducer(5 + GROUPS, N.small, Region(place, k.small_all, SMALL_ROWS), into(k.small_grad))
-        k.load(N.g_in)
         place.greet()
         units = wide + [out] + qkv + [small]
-        slots = wave(units)
+        plan = Plan(PLAN_BACK, units)
         for one in wide:
             run(one.sends())
-        plan = spread_steps(flat(slots[0:6]), 10 * GROUPS)
+        first_steps = plan.take()
+        sections = plan.takes(2)
+        polls = [Poll(sections[0], sections[1] + out.sends())]
+        sections = plan.takes(10 * GROUPS)
         for g in range(GROUPS):
-            plan[10 * g + 9] = plan[10 * g + 9] + qkv[g].sends()
-        polls = [Poll([], out.sends()), Poll(*plan), Poll(*spread_steps(flat(slots[6:8]), 4))]
+            sections[10 * g + 9] = sections[10 * g + 9] + qkv[g].sends()
+        polls += [Poll(*sections), Poll(*plan.takes(4))]
     segment_masks(k.seg, k.one, k.mexp)
     k.ready(N.att, N.gbr)
     if linked:
         k.ready(N.g_in)
+        run(first_steps)
     phase_weight_grad(k.att, k.gbr, k.g_out, polls[0])
-    k.ready(N.w_out, N.fq, N.fk, N.sq, N.sk, N.v, N.state, N.total, N.attc, N.h1)
+    k.ready(*first)
+    if not linked:
+        k.load(*later)
     k.load(N.w_qkv, N.tok, N.gmid)
     phase_attention_back(
         k.gbr, k.w_out, k.attc, k.proj, k.cos, k.sin, k.one, k.mexp, k.fq, k.fk, k.sq, k.sk, k.v,
-        k.state, k.total, k.dnum, k.dstate, k.dtotal, k.gproj, k.small, k.h1, k.g_qkv, polls[1],
+        k.state, k.total, k.dnum, k.dstate, k.dtotal, k.gproj, k.small, k.h1, k.g_qkv, lambda: k.ready(*later), polls[1],
     )
     k.ready(N.w_qkv, N.tok, N.gmid)
     phase_norm_one_back(k.gproj, k.w_qkv, k.tok, k.gmid, k.vec, k.tgrad, k.small, polls[2])
@@ -1030,8 +1192,9 @@
         for row in (BIAS_OUT, GAIN2, SHIFT2, BIAS_FFO, BIAS_IN):
             k.small[row : row + 1, :] = k.small_two[row : row + 1, :]
         pack_small(k.small, k.small_all, groups, unit)
+        plan.run()
         run(small.sends())
-        run(flat(slots[8:]))
+        plan.run()
         for one in units:
             one.drain()
     else:
@@ -1098,7 +1261,9 @@
 
 
 def run_forward(z, values):
-    spec = dict(tok=(GIVEN, z.rows, BF16), **z.common)
+    spec = dict(
+        tok=(GIVEN, z.rows, BF16), cot=(LOAD, z.rows, BF16), g_ffo=(SPILL, z.weights[N.w_ffo], BF16), **z.common
+    )
     if z.linked:
         spec.update(small_block=(FAR, (SMALL_ROWS, SMALL_COLUMNS), BF16))
         for n in (N.qkv_block, N.out_block, N.in_block, N.ffo_block):
@@ -1129,14 +1294,12 @@
     if z.linked:
         spec.update(
             ffo_grad=(MADE, (z.hidden // z.groups, z.width), F32),
-            g_ffo=(SCRATCH, pltpu.VMEM((z.hidden, z.width), BF16)),
+            g_ffo=(LOAD, z.weights[N.w_ffo], BF16),
             reduce_sems=(SCRATCH, pltpu.SemaphoreType.DMA((4, Reduce.count(z.depth)))),
         )
         for number in range(4):
             buffers = Reduce.buffers(z.depth, z.unit, z.width)
             spec.update({n: (SCRATCH, buf) for n, buf in zip(buffer_names((N.ffo, number)), buffers)})
-    else:
-        spec.update(g_ffo=(SPILL, (z.hidden, z.width), BF16))
     return call(N.feed, lambda k: feed_body(k, z.groups, z.linked), spec, values, 2 if z.linked else None)
 
 
@@ -1175,6 +1338,40 @@
     return call(N.back, lambda k: back_body(k, z.groups, z.linked), spec, values, 3 if z.linked else None)
 
 
+def run_finish(z, values):
+    names = (N.output, N.tgrad, N.in_grad, N.ffo_grad, N.qkv_grad, N.out_grad)
+    sizes = [z.unit * many for _name, _start, many, _third, _place in GRAD_LAYOUT]
+
+    def kernel(*refs):
+        ins, small, refs = refs[: len(names)], refs[len(names)], refs[len(names) + 1 :]
+        outs, smalls, refs = refs[: len(names)], refs[len(names) : len(names) + len(sizes)], refs[len(names) + len(sizes) :]
+        held, sems = refs[: len(names)], refs[len(names)]
+        for n in range(len(names)):
+            pltpu.make_async_copy(ins[n], held[n], sems.at[n]).start()
+        for (_name, _start, many, third, place), ref in zip(GRAD_LAYOUT, smalls):
+            ref[...] = small[16 * third : 16 * third + 1, place * z.unit : (place + many) * z.unit]
+        for n in range(len(names)):
+            pltpu.make_async_copy(ins[n], held[n], sems.at[n]).wait()
+            pltpu.make_async_copy(held[n], outs[n], sems.at[n]).start()
+        for n in range(len(names)):
+            pltpu.make_async_copy(held[n], outs[n], sems.at[n]).wait()
+
+    vmem, anywhere = pl.BlockSpec(memory_space=pltpu.VMEM), pl.BlockSpec(memory_space=pl.ANY)
+    arrays = [values[n] for n in names]
+    results = pl.pallas_call(
+        kernel,
+        out_shape=[jax.ShapeDtypeStruct(a.shape, a.dtype) for a in arrays]
+        + [jax.ShapeDtypeStruct((1, size), F32) for size in sizes],
+        in_specs=[anywhere] * len(names) + [vmem],
+        out_specs=[anywhere] * len(names) + [vmem] * len(sizes),
+        scratch_shapes=[pltpu.VMEM(a.shape, a.dtype) for a in arrays] + [pltpu.SemaphoreType.DMA((len(names),))],
+        compiler_params=pltpu.CompilerParams(vmem_limit_bytes=VMEM_LIMIT),
+        name=N.finish,
+    )(*arrays, values[N.small_grad])
+    smalls = {row[0]: v.reshape(-1) for row, v in zip(GRAD_LAYOUT, results[len(names) :])}
+    return dict(zip(names, results)), smalls
+
+
 def body(
     linked,
     tokens, segment_ids, projection, norm1_gain, norm1_bias, qkv_weight, qkv_bias, out_weight, out_bias,
@@ -1183,7 +1380,6 @@
     length, width = tokens.shape
     hidden = in_weight.shape[1]
     groups = lax.axis_size(N.fsdp)
-    unit = width // groups
     z = Sizes(length, width, hidden, groups, linked)
     cos, sin = position_tables(length)
     vectors = {
@@ -1212,9 +1408,8 @@
     values.update(made, small_two=small_two)
     values.update(run_back(z, values))
     if linked:
-        smalls = {}
-        for name, _start, many, third, offset in GRAD_LAYOUT:
-            smalls[name] = values[N.small_grad][16 * third, offset * unit : (offset + many) * unit]
+        made, smalls = run_finish(z, values)
+        values.update(made)
         grads = [values[n] for n in (N.qkv_grad, N.out_grad, N.in_grad, N.ffo_grad)]
     else:
         small_one = values[N.small]

time: 248 us -> 206 us (0.83)
  Pallas kernels: 230 us -> 202 us
  local copies, waits for them, and re-layouts: 15.7 us -> 1.32 us
    pallas_call x3, Pallas kernels: 230 us -> 197 us  [call(): pl.pallas_call(kernel, out_shape=[jax.ShapeDtypeStruct(spec[n][1], spec[n...]
    unnamed x17 -> x0, local copies, waits for them, and re-layouts: 7.11 us -> none
    pallas_call x0 -> x1, Pallas kernels: none -> 5.08 us  [run_finish(): pl.pallas_call(kernel, out_shape=[jax.ShapeDtypeStruct(a.shape, a.dtype)...]
    concatenate x1 -> x0, local copies, waits for them, and re-layouts: 3.43 us -> none  [small_block(): flat = jnp.concatenate(parts)]
    squeeze x2 -> x0, local copies, waits for them, and re-layouts: 2.6 us -> none  [body(): values[N.small_grad][16 * third, offset * unit:(offset + many) * unit]]
where the time goes in v3:
time: 206 us
  Pallas kernels  202 us (98%)
    pallas_call x3, Pallas kernels, call(): pl.pallas_call(kernel, out_shape=[jax.ShapeDtypeStruct(spec[n][1], spec[n...  197 us
    pallas_call x1, Pallas kernels, run_finish(): pl.pallas_call(kernel, out_shape=[jax.ShapeDtypeStruct(a.shape, a.dtype)...  5.08 us

profile of v3, /device:TPU:0, one launch (start us, length us, event | category | flops | bytes accessed | tf_op | source)
XLA Modules:
  0.0 205.7 jit_solution(9422984146890016300)
XLA Ops:
  0.6 0.7 reshape.93
  1.3 0.7 reshape.95
  2.0 1.4 pad_add_fusion
  3.4 82.0 %forward.1 = (bf16[3072,768]{1,0:T(8,128)(2,1)}, bf16[3,768,768]{2,1,0:T(8,128)(2,1)}, bf16[768,768]{1,0:T(8,128)(2,1)}, bf16[768,3072]{1,0:T(8,128)(2,1)}, bf16...) custom-call(bf16[1024,768]{1,0:T(8,128)(2,1)} %refs_15_.1, ...), custom_call_target="tpu_custom_call" | custom-call | tf_op jit(solution)/shard_map/forward/pallas_call | solution.py:815
  85.4 44.3 %feed.1 = (bf16[1024,768]{1,0:T(8,128)(2,1)}, bf16[768,3072]{1,0:T(8,128)(2,1)}, f32[1024,768]{1,0:T(8,128)}, bf16[1024,768]{1,0:T(8,128)(2,1)}, f32[8,3072]{1,0:T(8,128)}, /*index=5*/f32[192,768]{1,0:T(8,128)}) custom-call(bf16[1024,3072]{1,0:T(8,128)(2,1)} %get-tuple-element.61.refs_0_, f32[1024,768]{1,0:T(8,128)} %get-tuple-element.62.refs_1_, ...), custom_call_target="tpu_custom_call" | custom-call | tf_op jit(solution)/shard_map/feed/pallas_call | solution.py:815
  129.8 70.6 %back.1 = (bf16[1024,768]{1,0:T(8,128)(2,1)}, f32[48,3072]{1,0:T(8,128)}, f32[48,768]{1,0:T(8,128)}, f32[48,2304]{1,0:T(8,128)}, f32[48,256]{1,0:T(8,128)}) custom-call(f32[8,3072]{1,0:T(8,128)} %get-tuple-element.67.refs_7_.refs_0_, s32[1,1024]{1,0:T(1,128)} %refs_1_.3, f32[384,64]{1,0:T(8,128)} %bitcast.18, f32[1024,128]{1,0:T(8,128)} %constant.7.clone.refs_4_.refs_3_, ...), custom_call_target="tpu_custom_call" | custom-call | tf_op jit(solution)/shard_map/back/pallas_call | solution.py:815
  200.4 5.1 %finish.1 = (bf16[1024,768]{1,0:T(8,128)(2,1)}, bf16[1024,768]{1,0:T(8,128)(2,1)}, f32[48,3072]{1,0:T(8,128)}, f32[192,768]{1,0:T(8,128)}, f32[48,2304]{1,0:T(8,...) custom-call(bf16[1024,768]{1,0:T(8,128)(2,1)} %get-tuple-element.69., ...), custom_call_target="tpu_custom_call" | custom-call | tf_op jit(solution)/shard_map/finish/pallas_call | solution.py:1361

commit v4 on v3

--- a/solution.py
+++ b/solution.py
@@ -193,50 +193,41 @@
     def _(g):
         cols, feats = tile(g, WIDE), tile(g, SLIM)
         plain, turned = projection_blocks(proj_ref, g)
-        for kind, (feat_ref, slope_ref) in enumerate(((fq_ref, sq_ref), (fk_ref, sk_ref))):
-            span = pl.ds(pl.multiple_of(kind * width + g * WIDE, WIDE), WIDE)
-            weight = w_qkv_ref.at[g, :, pl.ds(kind * WIDE, WIDE)]
-
-            @pl.loop(0, length // 512)
-            def _(r):
-                rows = tile(r, 512)
-                x = nn(h1_ref[rows, :], weight[...]) + vec_ref[BIAS_QKV : BIAS_QKV + 1, span]
+        weight = w_qkv_ref.at[g]
+        shared = nn(hbar_ref[...].astype(BF16), w_qkv_ref[g, :, 2 * WIDE :])[0:1]
+        v_span = pl.ds(pl.multiple_of(2 * width + g * WIDE, WIDE), WIDE)
+
+        @pl.loop(0, length // 512)
+        def _(r):
+            rows = tile(r, 512)
+            projected = nn(h1_ref[rows, :], weight[...])
+            v_ref[rows, cols] = (projected[:, 2 * WIDE :] - shared).astype(BF16)
+            for kind, (feat_ref, slope_ref) in enumerate(((fq_ref, sq_ref), (fk_ref, sk_ref))):
+                span = pl.ds(pl.multiple_of(kind * width + g * WIDE, WIDE), WIDE)
+                x = projected[:, kind * WIDE : (kind + 1) * WIDE] + vec_ref[BIAS_QKV : BIAS_QKV + 1, span]
                 u = nt((x * twice(cos_ref[rows, :])).astype(BF16), plain) + nt(
                     (x * twice(sin_ref[rows, :])).astype(BF16), turned
                 )
                 small = jnp.exp(-jnp.abs(u))
                 feat_ref[rows, feats] = (jnp.maximum(u, 0.0) + jnp.log1p(small)).astype(BF16)
                 slope_ref[rows, feats] = jnp.where(u >= 0.0, 1.0, small) / (1.0 + small)
-
-            checkpoint(poll, g, 5, kind)
-
-        span = pl.ds(pl.multiple_of(2 * width + g * WIDE, WIDE), WIDE)
-        weight = w_qkv_ref.at[g, :, pl.ds(2 * WIDE, WIDE)]
-        shared = nn(hbar_ref[...].astype(BF16), weight[...])[0:1]
+            checkpoint(poll, g, 5, 0, r, 2)
+
+        shared = shared + vec_ref[BIAS_QKV : BIAS_QKV + 1, v_span]
+        segment_states(fk_ref, one_ref, v_ref[:, cols], g, state_ref, g * STATE)
+        total_ref[:, feats] = nn(one_ref[...], fk_ref[:, feats])
+        checkpoint(poll, g, 5, 2)
 
         @pl.loop(0, length // 512)
         def _(r):
             rows = tile(r, 512)
-            v_ref[rows, cols] = (nn(h1_ref[rows, :], weight[...]) - shared).astype(BF16)
-
-        checkpoint(poll, g, 5, 2)
-        shared = shared + vec_ref[BIAS_QKV : BIAS_QKV + 1, span]
-
-        segment_states(fk_ref, one_ref, v_ref[:, cols], g, state_ref, g * STATE)
-        total_ref[:, feats] = nn(one_ref[...], fk_ref[:, feats])
-        checkpoint(poll, g, 5, 3)
-
-        @pl.loop(0, length // 256)
-        def _(r):
-            rows = tile(r, 256)
             fq = fq_ref[rows, feats]
             numerator = nn(spread(fq, mexp_ref[rows, :]), state_ref[tile(g, STATE), :])
             _rows, wide, _slim, absent = denominators(fq, one_ref[:, rows], total_ref[:, feats])
             centred = numerator / wide
             attc_ref[rows, cols] = centred.astype(BF16)
             att_ref[rows, cols] = (centred + (1.0 - absent) * shared).astype(BF16)
-
-        checkpoint(poll, g, 5, 4)
+            checkpoint(poll, g, 5, 3, r, 2)
 
 
 def phase_middle(tok_ref, att_ref, w_out_ref, vec_ref, mid_ref, h2_ref):
@@ -367,9 +358,9 @@
             gproj_ref[rows, place] = back
             small_ref[BIAS_QKV : BIAS_QKV + 1, span] += column_sum(back.astype(F32))
 
-        @pl.loop(0, length // 256)
+        @pl.loop(0, length // 512)
         def _(r):
-            rows = tile(r, 256)
+            rows = tile(r, 512)
             grad_att = nt(gbr_ref[rows, :], w_out_ref[cols, :])
             fq = fq_ref[rows, feats]
             total_rows, wide, slim, _absent = denominators(fq, one_ref[:, rows], total_ref[:, feats])
@@ -384,14 +375,14 @@
             dfq = dfq + dden * total_rows
             dtotal_ref[...] += nn(one_ref[:, rows], (dden * fq.astype(F32)).astype(BF16))
             unrotate(dfq * sq_ref[rows, feats], rows, q_span, q_place)
-            checkpoint(poll, g, 10, 0, r, 4)
+            checkpoint(poll, g, 6, 0, r, 2)
 
         segment_states(fq_ref, one_ref, dnum_ref[...], g, dstate_ref, 0)
         pl.when(g == 0)(arrive)
 
-        @pl.loop(0, length // 256)
+        @pl.loop(0, length // 512)
         def _(r):
-            rows = tile(r, 256)
+            rows = tile(r, 512)
             dv = nn(spread(fk_ref[rows, feats], mexp_ref[rows, :]), dstate_ref[...]).astype(BF16)
             gproj_ref[rows, v_place] = dv
             small_ref[BIAS_QKV : BIAS_QKV + 1, v_span] += column_sum(dv.astype(F32))
@@ -400,13 +391,13 @@
             dfk = masked_sum(nt(v_ref[rows, cols], dstate_ref[...]), mexp_ref[rows, :])
             dfk = dfk + tn(one_rows, high) + tn(one_rows, low)
             unrotate(dfk * sk_ref[rows, feats], rows, k_span, k_place)
-            checkpoint(poll, g, 10, 4, r, 4)
+            checkpoint(poll, g, 6, 2, r, 2)
 
         @pl.loop(0, width // 384)
         def _(i):
             rows = tile(i, 384)
             g_qkv_ref[g, rows, :] = tn(h1_ref[:, rows], gproj_ref[:, tile(g, 3 * WIDE)]).astype(BF16)
-            checkpoint(poll, g, 10, 8, i, 2)
+            checkpoint(poll, g, 6, 4, i, 2)
 
 
 def phase_norm_one_back(
@@ -451,21 +442,28 @@
         far = [self.device(d=d) for d in range(1, self.depth)]
         return far + [self.device(xr=1), self.device(cr=1), self.device(yr=1)]
 
-    def greet(self):
+    def plane(self):
+        ways = [(d, xr, cr) for d in range(self.depth) for xr in range(2) for cr in range(2)][1:]
+        return [self.device(*way) for way in ways] + [self.device(yr=1)]
+
+    def greet(self, partners=None):
         barrier = pltpu.get_barrier_semaphore()
-        partners = self.partners()
+        partners = self.partners() if partners is None else partners
         for partner in partners:
             pl.semaphore_signal(barrier, inc=1, device_id=partner, device_id_type=MESH)
         pl.semaphore_wait(barrier, len(partners))
 
 
 class Region:
-    def __init__(self, place, ref, stride, base=0, rows=None, columns=None):
+    def __init__(self, place, ref, stride, base=0, rows=None, columns=None, shared=False):
         self.ref, self.stride, self.base, self.rows = ref, stride, base, stride if rows is None else rows
         start, size = (0, ref.shape[1]) if columns is None else columns
         self.columns, self.width = slice(start, start + size), size
         self.third = third = self.rows // 3
-        self.all = (0, self.rows)
+        self.shared, self.all = shared, (0, self.rows)
+        if shared:
+            self.moved = self.common = self.all
+            return
         self.moved = (place.y * third, 2 * third)
         self.mine, self.other = (place.y * 2 * third, third), ((1 - place.y) * 2 * third, third)
         self.common = (third, third)
@@ -570,8 +568,12 @@
         return 6 * depth + 2
 
     @staticmethod
-    def buffers(depth, rows, columns):
+    def buffers(depth, rows, columns, shared=False):
         third = rows // 3
+        if shared:
+            tall = (rows, columns)
+            shapes = [(2 * depth, *tall), (1, 16, columns), (depth, *tall), (depth - 1, *tall), tall, tall]
+            return [pltpu.VMEM(dims, BF16) for dims in shapes]
         return [
             pltpu.VMEM((2 * depth, rows, columns), BF16),
             pltpu.VMEM((2 * depth, third, columns), BF16),
@@ -619,7 +621,10 @@
     def c_step(self, d, xr):
         self.c_copy(d, xr).wait_recv()
         self.add(self.full.where(self.place.index(d, xr), self.full.all), self.c_buf[2 * d + xr])
-        self.y_copy(d, xr).start()
+        if not self.full.shared:
+            self.y_copy(d, xr).start()
+        elif xr:
+            self.x_copy(d).start()
 
     def y_step(self, d, xr):
         self.y_copy(d, xr).wait_recv()
@@ -643,13 +648,17 @@
 
     def f_step(self):
         self.f_copy().wait_recv()
-        mine, other, common = (self.f_rows(x) for x in (self.full.mine, self.full.other, self.full.common))
-        self.emit(self.full.mine, self.f_send[mine, :].astype(F32))
-        self.emit(self.full.other, self.f_recv[other, :].astype(F32))
+        common = self.f_rows(self.full.common)
+        if not self.full.shared:
+            mine, other = self.f_rows(self.full.mine), self.f_rows(self.full.other)
+            self.emit(self.full.mine, self.f_send[mine, :].astype(F32))
+            self.emit(self.full.other, self.f_recv[other, :].astype(F32))
         self.emit(self.full.common, self.f_send[common, :].astype(F32) + self.f_recv[common, :].astype(F32))
 
     def drain(self):
-        sent = self.full.bulk(12 * self.place.depth)
+        depth = self.place.depth
+        thirds = 9 * depth + 3 * (depth - 1) + 3 if self.full.shared else 12 * depth
+        sent = self.full.bulk(thirds)
         pltpu.make_async_copy(sent, sent, self.sems.at[self.sent]).wait()
 
     def sends(self):
@@ -668,6 +677,39 @@
             self.f_step()
 
 
+class Exchange:
+    def __init__(self, place, full, held, sent, got, sems):
+        self.place, self.full, self.held, self.sent, self.got, self.sems = place, full, held, sent, got, sems
+        self.ways = [(d, xr, cr) for d in range(place.depth) for xr in range(2) for cr in range(2)][1:]
+
+    def copy(self, d, xr, cr):
+        slot = ((self.place.depth - d) % self.place.depth) * 4 + xr * 2 + cr
+        src = self.full.at[tile(self.place.index(d, xr, cr), 16)]
+        sems = self.sems.at[1]
+        return remote(src, self.held.at[slot], self.sems.at[0, slot], sems.at[slot], self.place.device(d, xr, cr))
+
+    def start(self):
+        for way in self.ways:
+            self.copy(*way).start()
+
+    def last(self):
+        sems = self.sems
+        return remote(self.sent, self.got, sems.at[0, 0], sems.at[1, 0], self.place.device(yr=1))
+
+    def relay(self):
+        total = self.full[tile(self.place.index(), 16), :].astype(F32)
+        for way in self.ways:
+            self.copy(*way).wait()
+        for slot in range(1, self.held.shape[0]):
+            total = total + self.held[slot].astype(F32)
+        self.sent[...] = total.astype(BF16)
+        self.last().start()
+
+    def finish(self, emit):
+        self.last().wait()
+        emit(self.sent[...].astype(F32) + self.got[...].astype(F32))
+
+
 class Plan:
     def __init__(self, sections, units):
         self.sections, self.units = iter(sections), units
@@ -734,9 +776,11 @@
         row = small_ref[row : row + 1, start * unit * groups : (start + many) * unit * groups]
         spaced = jnp.where(owner_mask(size, groups), row, 0.0).astype(BF16)
         thirds[third] = thirds[third] + nt(spaced, selector(unit, many, offset, groups))
-    first = iota((groups, 16, SMALL_COLUMNS), 1) == 0
-    laid = [jnp.where(first, part[:, None, :], 0.0) for part in thirds]
-    out_ref[...] = jnp.concatenate(laid, axis=1).reshape(groups * SMALL_ROWS, SMALL_COLUMNS).astype(BF16)
+    place = iota((groups, 16, SMALL_COLUMNS), 1)
+    laid = jnp.zeros((groups, 16, SMALL_COLUMNS), F32)
+    for third, part in enumerate(thirds):
+        laid = jnp.where(place == third, part[:, None, :], laid)
+    out_ref[...] = laid.reshape(groups * 16, SMALL_COLUMNS).astype(BF16)
 
 
 class Names:
@@ -836,113 +880,100 @@
     (6, 34, 101, 128),
     (16, 14, 40, 47),
     (68, 45, 39, 67, 12, 66, 160, 38, 43, 106, 48, 133),
-    (46, 72, 79, 77, 100, 99),
-    (44, 70, 71, 75, 98, 138, 192),
-    (165,),
-    (80, 104, 111, 132, 131),
-    (76, 78, 102, 103, 107, 109, 130, 224),
+    (46, 72, 79, 77, 100),
+    (44, 71, 75, 98, 99, 192),
+    (70, 138, 165),
+    (80, 104, 111, 132),
+    (78, 131),
     (),
+    (76, 102, 103, 107, 109, 130, 224),
     (112, 143, 164, 170, 197),
-    (136, 135, 141, 162, 163, 256),
-    (108, 110, 134),
-    (139, 175, 196, 202, 229),
-    (144, 142, 166, 168, 171, 194, 195, 288),
+    (136, 141, 163),
+    (108, 110, 135, 162, 256),
+    (134, 139, 175, 229),
     (),
-    (140, 167, 173, 207, 228, 261),
-    (200, 227, 234),
-    (172, 176, 198, 226, 320),
-    (174, 199, 203, 205, 260),
-    (208, 232, 239, 237, 258, 259, 266, 293, 352),
+    (144, 168, 196, 195, 202),
+    (142, 167, 171, 173, 194, 288),
+    (140, 166, 228, 234, 261),
+    (176, 200, 207, 227),
+    (174, 199, 205, 226, 320),
     (),
-    (204, 206, 230, 231, 235, 271, 292),
+    (172, 198, 203, 239, 293),
     (),
-    (240, 264, 267, 290, 291, 325),
-    (236, 262, 263, 269, 298),
+    (208, 206, 232, 231, 235, 237, 258, 260, 259, 266, 352),
+    (204, 230, 298),
     (),
-    (238, 272, 296, 303, 322, 324, 323, 357),
-    (294, 295, 299, 301, 330),
+    (240, 238, 262, 292, 291, 325),
+    (264, 267, 271, 269, 290),
     (),
-    (268, 270, 304, 356, 355),
-    (326, 328, 331, 335, 333, 354),
+    (236, 263, 268, 303, 324, 323, 357),
+    (272, 296, 295, 301, 322, 330),
     (),
-    (300, 302, 327, 367, 362),
-    (332, 360, 359, 365),
-    (),
-    (336,),
-    (363, 358, 334, 368),
-    (366, 364),
+    (270, 294, 299, 328, 335, 356, 355),
+    (304, 327, 333, 354, 362),
+    (302, 326),
+    (331, 300, 336, 360, 367, 359, 365),
+    (334, 358, 363, 332, 368, 366),
+    (364,),
 )
 PLAN_FEED = (
-    (),
-    (),
-    (7, 5, 3, 1),
-    (6, 4, 2, 0, 39),
-    (37, 35, 33, 38, 36),
-    (34, 32, 71, 69, 67),
-    (65, 70, 68, 66, 64, 103),
-    (101, 99, 97, 102, 100),
-    (15, 13, 98, 96),
-    (11,),
-    (9,),
-    (14,),
-    (12, 10),
-    (8,),
-    (19, 47, 45),
-    (18, 43),
-    (17, 41, 46),
-    (44, 42),
-    (16, 40),
-    (51, 79, 77),
-    (50, 75),
-    (49, 48, 73, 78, 76, 74, 72),
-    (20, 83, 82, 81, 111, 109, 107, 105, 110),
-    (80, 108, 106, 104),
-    (),
-    (21, 52, 115),
-    (114,),
-    (113, 112, 53, 84, 85, 116, 117),
+    (7,),
+    (5, 3, 1, 6, 4),
+    (2, 0, 39, 37, 35, 33),
+    (38, 36, 34, 32, 71),
+    (69, 67, 65, 70, 68),
+    (66, 64, 103, 101, 99, 97),
+    (19, 102, 100, 98, 96),
+    (47,),
+    (45, 43),
+    (18, 41),
+    (46,),
+    (17, 44),
+    (42,),
+    (16, 40, 79),
+    (77, 75),
+    (51, 73),
+    (50, 78, 76),
+    (49, 74),
+    (48, 72, 111),
+    (109, 107),
+    (20, 83, 105),
+    (82, 81, 80, 110, 108, 106, 104),
+    (21, 52, 115, 114),
+    (113,),
+    (112,),
+    (53,),
+    (84,),
+    (116, 85, 117),
 )
 PLAN_BACK = (
-    (7,),
-    (5, 3, 1, 6, 4, 2, 0, 39, 37, 35),
-    (33, 38, 36, 34, 32, 71, 69, 67, 65, 70),
-    (15, 68, 66, 64, 103, 101, 99, 97, 102, 100, 98),
-    (13, 96),
-    (11, 9, 14, 135, 133, 131, 129, 134, 132, 130),
-    (12, 10, 128),
-    (8, 19, 18, 47, 45, 43, 41),
-    (17, 16, 46, 44),
-    (42, 40),
-    (79, 77, 75),
-    (51, 73),
-    (50, 78, 76),
-    (49, 74, 72),
-    (48, 111, 109, 107),
-    (20, 83, 82, 105, 110, 167, 165, 163, 161, 166, 164, 162),
-    (81, 108, 106, 104, 160),
-    (80, 115, 143, 141, 139, 137),
-    (52, 114, 142, 140, 138),
-    (113, 112, 136),
-    (21, 175),
-    (147, 173, 171),
-    (84, 146, 169, 174),
-    (145, 172, 170),
-    (144, 168),
-    (53, 116, 179, 178, 199, 197, 195, 193, 198, 196, 194),
-    (85, 177, 192),
-    (176,),
-    (117, 148, 207, 205),
-    (203, 201),
-    (206, 204),
-    (202, 200),
-    (149, 180, 211),
-    (210,),
-    (209, 208, 231),
-    (181, 229, 227, 225, 230, 228, 226, 224),
-    (),
+    (7, 5, 3, 1, 6, 4, 2, 0, 39),
+    (37, 35, 33, 38, 36, 34, 32, 71, 69, 67),
+    (65, 70, 68, 66, 64, 103, 101, 99, 97, 102),
+    (15, 13, 11, 100, 98, 96),
+    (9, 14, 12, 10, 135, 133, 131, 129, 134, 132, 130, 128),
+    (8, 19, 18, 47, 45, 43, 41, 46),
+    (17, 16, 44, 42, 40, 79),
+    (77,),
+    (75, 73, 147),
+    (78, 76, 74, 72, 146),
+    (111, 109, 107, 145, 167, 165, 163, 161, 166, 164, 162, 160),
+    (20, 51, 50, 105, 110, 108, 106, 104, 144, 175),
+    (49, 48, 173, 171, 169, 174),
+    (83, 172),
+    (82, 148, 170, 168),
+    (21, 81, 80),
+    (115, 199, 197, 195, 193, 198, 196, 194, 192),
+    (52, 114, 113, 112, 149, 207),
+    (84, 179, 178, 205, 203, 201, 206),
+    (177, 204, 202),
+    (176, 200),
+    (53, 211),
+    (85, 210, 209, 231, 229, 227, 225, 230),
+    (116, 208, 228, 226, 224),
     (239,),
-    (237, 235, 233, 212, 238, 263, 261, 259, 236, 257, 262, 260, 258, 256, 234, 243, 232, 242, 213, 241, 271, 269,
-     267, 265, 270, 268, 240, 266, 264, 275, 274, 273, 272, 244, 276, 245, 277),
+    (237, 235),
+    (233, 180, 238, 117, 243, 236, 234, 242, 232, 241, 181, 212, 240, 213, 244, 245),
 )
 
 
@@ -1072,7 +1103,7 @@
         units = []
         for n in range(4):
             bufs = [getattr(k, name) for name in buffer_names((N.ffo, n))]
-            full = Region(place, k.g_ffo, 4 * unit, n * unit, unit)
+            full = Region(place, k.g_ffo, 4 * unit, n * unit, unit, shared=n == 0)
             source = Region(place, k.hbm[N.g_ffo], 4 * unit, n * unit, unit)
             units.append(Reduce(place, full, bufs, k.reduce_sems.at[n], into(n * unit), source))
         place.greet()
@@ -1154,22 +1185,26 @@
             )
             for n in range(4)
         ]
-        out = reducer(4, N.out, Region(place, k.g_out, unit), into(k.out_grad))
+        out = reducer(4, N.out, Region(place, k.g_out, unit, shared=True), into(k.out_grad))
         qkv = [
             reducer(5 + g, (N.qkv, g), Region(place, k.g_qkv.at[g], unit), into_group(g)) for g in range(GROUPS)
         ]
-        small = reducer(5 + GROUPS, N.small, Region(place, k.small_all, SMALL_ROWS), into(k.small_grad))
-        place.greet()
-        units = wide + [out] + qkv + [small]
+        small = Exchange(place, k.small_all, k.small_held, k.small_sent, k.small_got, k.small_sems)
+
+        def emit_small(values):
+            k.small_grad[...] = values
+
+        place.greet(place.plane())
+        units = wide + [out] + qkv
         plan = Plan(PLAN_BACK, units)
         for one in wide:
             run(one.sends())
         first_steps = plan.take()
         sections = plan.takes(2)
         polls = [Poll(sections[0], sections[1] + out.sends())]
-        sections = plan.takes(10 * GROUPS)
+        sections = plan.takes(6 * GROUPS)
         for g in range(GROUPS):
-            sections[10 * g + 9] = sections[10 * g + 9] + qkv[g].sends()
+            sections[6 * g + 5] = sections[6 * g + 5] + qkv[g].sends()
         polls += [Poll(*sections), Poll(*plan.takes(4))]
     segment_masks(k.seg, k.one, k.mexp)
     k.ready(N.att, N.gbr)
@@ -1192,9 +1227,13 @@
         for row in (BIAS_OUT, GAIN2, SHIFT2, BIAS_FFO, BIAS_IN):
             k.small[row : row + 1, :] = k.small_two[row : row + 1, :]
         pack_small(k.small, k.small_all, groups, unit)
+        small.start()
         plan.run()
-        run(small.sends())
-        plan.run()
+        last = plan.take()
+        run(last[: len(last) // 2])
+        small.relay()
+        run(last[len(last) // 2 :])
+        small.finish(emit_small)
         for one in units:
             one.drain()
     else:
@@ -1298,7 +1337,7 @@
             reduce_sems=(SCRATCH, pltpu.SemaphoreType.DMA((4, Reduce.count(z.depth)))),
         )
         for number in range(4):
-            buffers = Reduce.buffers(z.depth, z.unit, z.width)
+            buffers = Reduce.buffers(z.depth, z.unit, z.width, number == 0)
             spec.update({n: (SCRATCH, buf) for n, buf in zip(buffer_names((N.ffo, number)), buffers)})
     return call(N.feed, lambda k: feed_body(k, z.groups, z.linked), spec, values, 2 if z.linked else None)
 
@@ -1320,16 +1359,19 @@
             small=(SCRATCH, pltpu.VMEM((8, z.hidden), F32)), small_two=(GIVEN, (8, z.hidden), F32),
             g_in=(LOAD, weights[N.w_in], BF16), g_out=(SCRATCH, pltpu.VMEM(weights[N.w_out], BF16)),
             g_qkv=(SCRATCH, pltpu.VMEM((GROUPS, width, 3 * WIDE), BF16)),
-            small_all=(SCRATCH, pltpu.VMEM((z.groups * SMALL_ROWS, SMALL_COLUMNS), BF16)),
+            small_all=(SCRATCH, pltpu.VMEM((z.groups * 16, SMALL_COLUMNS), BF16)),
+            small_held=(SCRATCH, pltpu.VMEM((z.groups, 16, SMALL_COLUMNS), BF16)),
+            small_sent=(SCRATCH, pltpu.VMEM((16, SMALL_COLUMNS), BF16)),
+            small_got=(SCRATCH, pltpu.VMEM((16, SMALL_COLUMNS), BF16)),
+            small_sems=(SCRATCH, pltpu.SemaphoreType.DMA((2, z.groups))),
             in_grad=(MADE, (z.unit, z.hidden), F32), out_grad=(MADE, (z.unit, width), F32),
-            qkv_grad=(MADE, (z.unit, 3 * width), F32), small_grad=(MADE, (SMALL_ROWS, SMALL_COLUMNS), F32),
-            reduce_sems=(SCRATCH, pltpu.SemaphoreType.DMA((6 + GROUPS, Reduce.count(z.depth)))),
+            qkv_grad=(MADE, (z.unit, 3 * width), F32), small_grad=(MADE, (16, SMALL_COLUMNS), F32),
+            reduce_sems=(SCRATCH, pltpu.SemaphoreType.DMA((5 + GROUPS, Reduce.count(z.depth)))),
         )
-        sizes = [(N.out, (z.unit, width)), (N.small, (SMALL_ROWS, SMALL_COLUMNS))]
-        sizes += [((N.wide, n), (z.unit, width)) for n in range(4)]
-        sizes += [((N.qkv, g), (z.unit, 3 * WIDE)) for g in range(GROUPS)]
-        for base, dims in sizes:
-            spec.update({n: (SCRATCH, buf) for n, buf in zip(buffer_names(base), Reduce.buffers(z.depth, *dims))})
+        names = [N.out] + [(N.wide, n) for n in range(4)] + [(N.qkv, g) for g in range(GROUPS)]
+        for base in names:
+            buffers = Reduce.buffers(z.depth, z.unit, width, base == N.out)
+            spec.update({n: (SCRATCH, buf) for n, buf in zip(buffer_names(base), buffers)})
     else:
         spec.update(
             small=(MADE, (8, z.hidden), F32), g_out=(SPILL, weights[N.w_out], BF16),
@@ -1349,7 +1391,7 @@
         for n in range(len(names)):
             pltpu.make_async_copy(ins[n], held[n], sems.at[n]).start()
         for (_name, _start, many, third, place), ref in zip(GRAD_LAYOUT, smalls):
-            ref[...] = small[16 * third : 16 * third + 1, place * z.unit : (place + many) * z.unit]
+            ref[...] = small[third : third + 1, place * z.unit : (place + many) * z.unit]
         for n in range(len(names)):
             pltpu.make_async_copy(ins[n], held[n], sems.at[n]).wait()
             pltpu.make_async_copy(held[n], outs[n], sems.at[n]).start()

time: 206 us -> 193 us (0.937)
  Pallas kernels: 202 us -> 189 us
    pallas_call x3, Pallas kernels: 197 us -> 184 us  [call(): pl.pallas_call(kernel, out_shape=[jax.ShapeDtypeStruct(spec[n][1], spec[n...]
where the time goes in v4:
time: 193 us; the launch traced here: 192 us
  Pallas kernels  189 us (98%)
    pallas_call x3, Pallas kernels, call(): pl.pallas_call(kernel, out_shape=[jax.ShapeDtypeStruct(spec[n][1], spec[n...  184 us
    pallas_call x1, Pallas kernels, run_finish(): pl.pallas_call(kernel, out_shape=[jax.ShapeDtypeStruct(a.shape, a.dtype)...  5 us

profile of v4, /device:TPU:0, one launch (start us, length us, event | category | flops | bytes accessed | tf_op | source)
XLA Modules:
  0.0 192.4 jit_solution(7971628527743706447)
XLA Ops:
  0.6 0.7 reshape.93
  1.3 0.7 reshape.95
  2.0 1.4 pad_add_fusion
  3.4 79.2 %forward.1 = (bf16[3072,768]{1,0:T(8,128)(2,1)}, bf16[3,768,768]{2,1,0:T(8,128)(2,1)}, bf16[768,768]{1,0:T(8,128)(2,1)}, bf16[768,3072]{1,0:T(8,128)(2,1)}, bf16...) custom-call(bf16[1024,768]{1,0:T(8,128)(2,1)} %refs_15_.1, ...), custom_call_target="tpu_custom_call" | custom-call | tf_op jit(solution)/shard_map/forward/pallas_call | solution.py:859
  82.6 40.2 %feed.1 = (bf16[1024,768]{1,0:T(8,128)(2,1)}, bf16[768,3072]{1,0:T(8,128)(2,1)}, f32[1024,768]{1,0:T(8,128)}, bf16[1024,768]{1,0:T(8,128)(2,1)}, f32[8,3072]{1,0:T(8,128)}, /*index=5*/f32[192,768]{1,0:T(8,128)}) custom-call(bf16[1024,3072]{1,0:T(8,128)(2,1)} %get-tuple-element.61.refs_0_, f32[1024,768]{1,0:T(8,128)} %get-tuple-element.62.refs_1_, ...), custom_call_target="tpu_custom_call" | custom-call | tf_op jit(solution)/shard_map/feed/pallas_call | solution.py:859
  122.8 64.5 %back.1 = (bf16[1024,768]{1,0:T(8,128)(2,1)}, f32[48,3072]{1,0:T(8,128)}, f32[48,768]{1,0:T(8,128)}, f32[48,2304]{1,0:T(8,128)}, f32[16,256]{1,0:T(8,128)}) custom-call(f32[8,3072]{1,0:T(8,128)} %get-tuple-element.67.refs_7_.refs_0_, s32[1,1024]{1,0:T(1,128)} %refs_1_.3, f32[384,64]{1,0:T(8,128)} %bitcast.18, f32[1024,128]{1,0:T(8,128)} %constant.7.clone.refs_4_.refs_3_, ...), custom_call_target="tpu_custom_call" | custom-call | tf_op jit(solution)/shard_map/back/pallas_call | solution.py:859
  187.2 5.0 %finish.1 = (bf16[1024,768]{1,0:T(8,128)(2,1)}, bf16[1024,768]{1,0:T(8,128)(2,1)}, f32[48,3072]{1,0:T(8,128)}, f32[192,768]{1,0:T(8,128)}, f32[48,2304]{1,0:T(8,...) custom-call(bf16[1024,768]{1,0:T(8,128)(2,1)} %get-tuple-element.69., ...), custom_call_target="tpu_custom_call" | custom-call | tf_op jit(solution)/shard_map/finish/pallas_call | solution.py:1403
